TPU v7x, 256 devices: a whole 4x4x8 slice. The times are simulated.
256 devices in a mesh: section: 4 (over y), ctx: 64 (over z, x, core).
Axes of the slice: x: 4, y: 4, z: 8, core: 2. Of those that a mesh axis runs over, the one named last changes fastest.
Arguments:
- incoming: bfloat16 [4, 8192, 4096], P('section', 'ctx'), may hold values from -6 to 6
- layer_input: bfloat16 [4, 8192, 4096], P('section', 'ctx'), may hold values from -6 to 6
- pre_gate: bfloat16 [4, 8192, 4096], P('section', 'ctx'), may hold values from -6 to 6
- mid_gate: bfloat16 [4, 8192, 4096], P('section', 'ctx'), may hold values from -6 to 6
- long_gate: bfloat16 [4, 8192, 4096], P('section', 'ctx'), may hold values from -6 to 6
- out_gate: bfloat16 [4, 8192, 4096], P('section', 'ctx'), may hold values from -6 to 6
- long_filter: bfloat16 [4, 4096, 8192], P('section', 'ctx'), may hold values from -0.0625 to 0.0625
- mid_filter: bfloat16 [4, 128, 4096], P('section'), may hold values from -0.5 to 0.5
Outputs:
- input_grad: bfloat16 [4, 8192, 4096], P('section', 'ctx')
- long_grad: bfloat16 [4, 4096, 8192], P('section', 'ctx')
- mid_grad: bfloat16 [4, 128, 4096], P('section', None, 'ctx')
All inputs are finite; a program needn't handle non-finite values.
Results may differ from a plain program's by a relative error of at most 0.008.
Values may be sent and summed in bfloat16 or wider, within the bound.
A program may use at most 192 MiB of HBM per device.

v0:
```python
import functools
import math

import jax
import jax.numpy as jnp
from jax import lax
from jax.experimental import pallas as pl
from jax.experimental.pallas import tpu as pltpu
from jax.sharding import PartitionSpec as P

MESH_IDS = pl.DeviceIdType.MESH


def tap_exchange_kernel(nz, nx, nc, scale, x_ref, o_ref, r1, s1, r2, s2, r3, sems):
    me = lax.axis_index("ctx")
    sec = lax.axis_index("section")
    core = me % nc
    xi = (me // nc) % nx
    zi = me // (nc * nx)

    def device(z, x, c):
        return (sec, (z * nx + x) * nc + c)

    peers = [device(zi, xi, 1 - core)]
    peers += [device(zi, (xi + k) % nx, core) for k in range(1, nx)]
    peers += [device((zi + k) % nz, xi, core) for k in range(1, nz)]
    barrier = pltpu.get_barrier_semaphore()
    for peer in peers:
        pl.semaphore_signal(barrier, inc=1, device_id=peer, device_id_type=MESH_IDS)
    pl.semaphore_wait(barrier, len(peers))

    def send(src, dst, peer, out_slot, in_slot):
        return pltpu.make_async_remote_copy(
            src_ref=src,
            dst_ref=dst,
            send_sem=sems.at[0, out_slot],
            recv_sem=sems.at[1, in_slot],
            device_id=peer,
            device_id_type=MESH_IDS,
        )

    first = send(x_ref.at[1 - core], r1, peers[0], 0, 0)
    first.start()
    first.wait()
    s1[...] = x_ref[core] + r1[...]

    second = []
    for k in range(1, nx):
        target = (xi + k) % nx
        copy = send(s1.at[target], r2.at[xi], device(zi, target, core), 1 + target, 1 + xi)
        copy.start()
        second.append(copy)
    for k in range(1, nx):
        source = (xi + nx - k) % nx
        send(s1.at[source], r2.at[source], device(zi, source, core), 1 + source, 1 + source).wait_recv()
    for copy in second:
        copy.wait_send()
    r2[xi] = s1[xi]
    s2[...] = jnp.sum(r2[...], axis=0)

    third = []
    for k in range(1, nz):
        target = (zi + k) % nz
        copy = send(s2.at[target], r3.at[zi], device(target, xi, core), 1 + nx + target, 1 + nx + zi)
        copy.start()
        third.append(copy)
    for k in range(1, nz):
        source = (zi + nz - k) % nz
        send(s2.at[source], r3.at[source], device(source, xi, core), 1 + nx + source, 1 + nx + source).wait_recv()
    for copy in third:
        copy.wait_send()
    r3[zi] = s2[zi]
    o_ref[...] = (jnp.sum(r3[...], axis=0) * scale).astype(o_ref.dtype)


def tap_exchange(parts, scale):
    nc, nx, nz, taps, width = parts.shape
    return pl.pallas_call(
        functools.partial(tap_exchange_kernel, nz, nx, nc, scale),
        out_shape=jax.ShapeDtypeStruct((taps, width), jnp.bfloat16),
        in_specs=[pl.BlockSpec(memory_space=pltpu.VMEM)],
        out_specs=pl.BlockSpec(memory_space=pltpu.VMEM),
        scratch_shapes=[
            pltpu.VMEM((nx, nz, taps, width), jnp.float32),
            pltpu.VMEM((nx, nz, taps, width), jnp.float32),
            pltpu.VMEM((nx, nz, taps, width), jnp.float32),
            pltpu.VMEM((nz, taps, width), jnp.float32),
            pltpu.VMEM((nz, taps, width), jnp.float32),
            pltpu.SemaphoreType.DMA((2, 1 + nx + nz)),
        ],
        compiler_params=pltpu.CompilerParams(collective_id=0, has_side_effects=True),
    )(parts)


def passed_along(value, axis, steps):
    count = lax.axis_size(axis)
    pairs = [(source, (source + steps) % count) for source in range(count)]
    return lax.ppermute(value, axis, pairs)


def shifted(array, axis, by):
    devices = lax.axis_size(axis)
    pairs = [(i, i + by) for i in range(devices) if 0 <= i + by < devices]
    return lax.ppermute(array, axis, pairs)


def unit_roots(rows, cols, period):
    row_ids = jnp.arange(rows, dtype=jnp.int32)[:, None]
    col_ids = jnp.arange(cols, dtype=jnp.int32)[None, :]
    angle = (row_ids * col_ids % period).astype(jnp.float32) * (-2.0 * math.pi / period)
    return (jnp.cos(angle), jnp.sin(angle))


def contract(form, left, right):
    return jnp.einsum(
        form, left, right, precision=lax.Precision.HIGH, preferred_element_type=jnp.float32
    )


def to_spectrum(parts, factor_a, factor_b):
    channels = parts.shape[0]
    inputs_count = parts.shape[1]
    half = factor_a // 2
    period = factor_a * factor_b
    fa_cos, fa_sin = unit_roots(factor_a, half, factor_a)
    first_table = jnp.stack([jnp.stack([fa_cos, -fa_sin]), jnp.stack([fa_sin, fa_cos])])[
        :, :inputs_count
    ]
    tw_cos, tw_sin = unit_roots(factor_a, factor_b, period)
    fb_cos, fb_sin = unit_roots(factor_b, factor_b, factor_b)
    second_table = jnp.stack([jnp.stack([fb_cos, fb_sin]), jnp.stack([-fb_sin, fb_cos])])
    shaped = parts.reshape(channels, inputs_count, half, factor_b)
    first = contract("qrca,nrab->nqcb", first_table, shaped)
    first_re = first[:, 0]
    first_im = first[:, 1]
    turned = jnp.stack(
        [first_re * tw_cos - first_im * tw_sin, first_re * tw_sin + first_im * tw_cos], 1
    )
    return contract("nqcb,qpbd->npcd", turned, second_table)


def from_spectrum(spectrum, factor_a, factor_b, scale):
    channels = spectrum.shape[0]
    half = factor_a // 2
    period = factor_a * factor_b
    fb_cos, fb_sin = unit_roots(factor_b, factor_b, factor_b)
    back_table = jnp.stack([jnp.stack([fb_cos, -fb_sin]), jnp.stack([fb_sin, fb_cos])])
    tw_cos, tw_sin = unit_roots(factor_a, factor_b, period)
    fa_cos, fa_sin = unit_roots(half, factor_a, factor_a)
    last_table = jnp.stack(
        [
            jnp.stack([fa_cos, fa_sin]) * (scale / period),
            jnp.stack([-fa_sin, fa_cos]) * (1.0 / period),
        ]
    )
    middle = contract("npcd,pqdb->nqcb", spectrum, back_table)
    middle_re = middle[:, 0]
    middle_im = middle[:, 1]
    turned = jnp.stack(
        [middle_re * tw_cos + middle_im * tw_sin, middle_im * tw_cos - middle_re * tw_sin], 1
    )
    result = contract("rqac,nqcb->nrab", last_table, turned)
    length = half * factor_b
    return (result[:, 0].reshape(channels, length), result[:, 1].reshape(channels, length))


def depthwise(extended, kernel):
    result = lax.conv_general_dilated(
        extended[None],
        kernel[:, None, :],
        (1,),
        "VALID",
        dimension_numbers=("NWC", "WIO", "NWC"),
        feature_group_count=extended.shape[1],
        preferred_element_type=jnp.float32,
    )
    return result[0]


def per_device(
    incoming, layer_input, pre_gate, mid_gate, long_gate, out_gate, long_filter, mid_filter
):
    sections = lax.axis_size("section")
    beta = (2.0 * sections) ** (-0.5)
    adjoint = passed_along(incoming[0], "section", -1).astype(jnp.float32)
    inputs = layer_input[0].astype(jnp.float32)
    tokens = inputs.shape[0]
    gate_pre = pre_gate[0].astype(jnp.float32)
    gate_mid = mid_gate[0].astype(jnp.float32)
    gate_long = long_gate[0].astype(jnp.float32)
    gate_out = out_gate[0].astype(jnp.float32)
    filter_taps = mid_filter[0]
    reach = filter_taps.shape[0] - 1
    seq_len = tokens * lax.axis_size("ctx")
    scale = float(seq_len) ** (-0.5)
    mixed_in = (inputs * gate_pre).astype(jnp.bfloat16)
    earlier = shifted(mixed_in[tokens - reach :], "ctx", 1)
    extended = jnp.concatenate([earlier, mixed_in], 0)
    branch = depthwise(extended, filter_taps[::-1])
    resid = inputs + beta * branch * gate_mid
    long_in = (resid * gate_long).astype(jnp.bfloat16)
    grad_z = (beta * adjoint * gate_out).astype(jnp.bfloat16)
    channel_z, channel_w = lax.all_to_all(
        jnp.stack([grad_z.T, long_in.T]), "ctx", split_axis=1, concat_axis=2, tiled=True
    )
    factor_b = math.gcd(seq_len, 128)
    factor_a = 2 * seq_len // factor_b
    zspec = to_spectrum(channel_z[:, None], factor_a, factor_b)
    zspec_re = zspec[:, 0]
    zspec_im = zspec[:, 1]
    pair = to_spectrum(jnp.stack([channel_w, -long_filter[0]], 1), factor_a, factor_b)
    pair_re = pair[:, 0]
    pair_im = pair[:, 1]
    joint_re = zspec_re * pair_re + zspec_im * pair_im
    joint_im = zspec_im * pair_re - zspec_re * pair_im
    lag_grad, input_part = from_spectrum(
        jnp.stack([joint_re, joint_im], 1), factor_a, factor_b, scale
    )
    long_grad = lag_grad.astype(jnp.bfloat16)[None]
    returned = lax.all_to_all(
        input_part.astype(jnp.bfloat16), "ctx", split_axis=1, concat_axis=0, tiled=True
    ).T
    grad_u = adjoint + returned.astype(jnp.float32) * gate_long
    grad_b = (beta * grad_u * gate_mid).astype(jnp.bfloat16)
    later = shifted(grad_b[:reach], "ctx", -1)
    grad_act = depthwise(jnp.concatenate([grad_b, later], 0), filter_taps)
    input_grad = (grad_u + grad_act * gate_pre).astype(jnp.bfloat16)[None]
    tap_part = depthwise(extended, grad_b)
    devices = lax.axis_size("ctx")
    columns = tap_part.shape[1] // devices
    chip_cores, chips_x = 2, 4
    chips_z = devices // (chip_cores * chips_x)
    parts = tap_part.reshape(tap_part.shape[0], chips_z, chips_x, chip_cores, columns)
    parts = parts.transpose(3, 2, 1, 0, 4).reshape(
        chip_cores, chips_x, chips_z, tap_part.shape[0] * columns // 128, 128
    )
    mid_grad = tap_exchange(parts, scale).reshape(tap_part.shape[0], columns)[::-1][None]
    return (input_grad, long_grad, mid_grad)


def solution(mesh):
    placed = (
        P("section", "ctx", None),
        P("section", "ctx", None),
        P("section", "ctx", None),
        P("section", "ctx", None),
        P("section", "ctx", None),
        P("section", "ctx", None),
        P("section", "ctx", None),
        P("section", None, None),
    )
    return jax.shard_map(
        per_device,
        mesh=mesh,
        in_specs=placed,
        out_specs=(P("section", "ctx", None), P("section", "ctx", None), P("section", None, "ctx")),
        check_vma=False,
    )
```

profile of v0, /device:TPU:1, one launch (start us, length us, event | category | flops | bytes accessed | tf_op | source)
XLA Modules:
  0.0 314.1 jit_solution(13143648330587821570)
XLA Ops:
  3.8 4.5 %collective-permute-start.1 = (bf16[127,4096]{1,0:T(8,128)(2,1)}, bf16[127,4096]{1,0:T(8,128)(2,1)}, u32[]{:S(2)}, u32[]{:S(2)}) collective-permute-start(bf16[127,4096]{1,0:T(8,128)(2,1)} %slice.64), channel_id=1, source_target_pairs={{0,1},{1,2},{2,3},{3,4},{4,5},{5,6},{6,7},{7,8},{8,9},{9,10},{10,1... | collective-permute-start | bytes 3121160 | tf_op jit(solution)/shard_map/ppermute | solution.py:104
  8.3 2.8 collective-permute-start
  11.1 10.2 %rev.6 = bf16[128,4096]{1,0:T(8,128)(2,1)} reverse(bf16[128,4096]{1,0:T(8,128)(2,1)S(1)} %bitcast.190), dimensions={0} | reverse | bytes 2097152 | tf_op jit(solution)/shard_map/rev | solution.py:199
  23.0 27.4 %convolution_multiply_fusion = f32[1,128,4096]{2,0,1:T(1,128)S(1)} fusion(bf16[1,255,4096]{2,1,0:T(8,128)(2,1)S(1)} %maximum_bitcast_fusion.13, bf16[128,1,4096]{2,0,1:T(8,128)(2,1)S(1)} %bitcast.192), kind=kOutput, calls=%fused_computation.15 | convolution fusion | flops 134742016 | bytes 5234688 | tf_op jit(solution)/shard_map/conv_general_dilated | solution.py:168
  53.1 3.8 %copy.56 = bf16[2,4096,128]{2,0,1:T(2,128)(2,1)} copy(bf16[2,4096,128]{1,2,0:T(8,128)(2,1)S(1)} %pad_maximum_fusion) | data formatting | bytes 4194304 | tf_op jit(solution)/shard_map/stack | solution.py:204
  56.9 13.2 %all-to-all-start = ((bf16[2,4096,128]{2,0,1:T(2,128)(2,1)}), bf16[2,4096,128]{2,0,1:T(2,128)(2,1)S(1)}, u32[]{:S(2)}, u32[]{:S(2)}) async-start(bf16[2,4096,128]{2,0,1:T(2,128)(2,1)} %copy.56), calls=%async_computation | async-start | bytes 4194304 | tf_op jit(solution)/shard_map/all_to_all | solution.py:203
  76.2 43.4 %all-to-all-done = bf16[2,4096,128]{2,0,1:T(2,128)(2,1)S(1)} async-done(((bf16[2,4096,128]{2,0,1:T(2,128)(2,1)}), bf16[2,4096,128]{2,0,1:T(2,128)(2,1)S(1)}, u32[]{:S(2)}, u32[]{:S(2)}) %all-to-all-start) | async-done | bytes 2097184 | tf_op jit(solution)/shard_map/all_to_all | solution.py:203
  121.1 2.4 convolution_bitcast_fusion
  125.9 5.9 %multiply_subtract_fusion.3 = (f32[64,1,128,128]{2,3,1,0:T(8,128)}, f32[64,1,128,128]{2,3,1,0:T(8,128)}, f32[64,1,128,128]{2,3,1,0:T(8,128)S(1)}, f32[64,1,128,128]{2,3,1,0:T(8,128)}) fusion(f32[64,2,128,128]{2,3,1,0:T(8,128)S(1)} %convolution_bitcast_fusion, f32[128,128]{0,1:T(8,128)S(1)} %get-tuple-element.33, f32[128,128]{0,1:T(8,128)S(1)} %get-tuple-element.34, ...), kind=kLoop, calls=%fused_computation.24 | loop fusion | flops 12582912 | bytes 33685504 | tf_op jit(solution)/shard_map/sub | solution.py:137
  131.8 6.9 %fusion.20 = f32[64,2,128,128]{2,3,0,1:T(8,128)S(1)} fusion(f32[64,1,128,128]{2,3,1,0:T(8,128)} %get-tuple-element.14, f32[64,1,128,128]{2,3,1,0:T(8,128)} %get-tuple-element.13, f32[1,2,128,128]{2,3,0,1:T(8,128)S(1)} %get-tuple-element.20, f32[1,2,128,128]{2,3,0,1:T(8,128)S(1)} %get-tuple-element.25), kind=kOutput, calls=%fused_computation.33 | convolution fusion | flops 3223388160 | bytes 17039360 | tf_op jit(solution)/shard_map/nqcb,qpbd->npcd/dot_general | solution.py:115
  138.7 4.9 %fusion.19 = f32[64,2,128,128]{2,3,0,1:T(8,128)S(1)} fusion(f32[64,1,128,128]{2,3,1,0:T(8,128)S(1)} %get-tuple-element.23, f32[64,1,128,128]{2,3,1,0:T(8,128)S(1)} %copy-done.2, f32[1,2,128,128]{2,3,0,1:T(8,128)S(1)} %get-tuple-element.20, f32[1,2,128,128]{2,3,0,1:T(8,128)S(1)} %get-tuple-element.25), kind=kOutput, calls=%fused_computation.32 | convolution fusion | flops 3223388160 | bytes 17039360 | tf_op jit(solution)/shard_map/nqcb,qpbd->npcd/dot_general | solution.py:115
  145.5 5.0 %fusion.16 = f32[64,2,128,128]{2,3,1,0:T(8,128)S(1)} fusion(f32[64,1,128,128]{2,3,0,1:T(8,128)S(1)} %get-tuple-element.10, f32[64,1,128,128]{2,3,0,1:T(8,128)S(1)} %get-tuple-element.9, f32[1,2,128,128]{2,3,1,0:T(8,128)S(1)} %copy-done.22, f32[1,2,128,128]{2,3,1,0:T(8,128)S(1)} %copy-done.21), kind=kOutput, calls=%fused_computation.30 | convolution fusion | flops 3223388160 | bytes 17039360 | tf_op jit(solution)/shard_map/npcd,pqdb->nqcb/dot_general | solution.py:115
  152.5 4.7 %fusion.32 = bf16[64,2,64,128]{3,2,1,0:T(8,128)(2,1)S(1)} fusion(f32[64,1,128,128]{2,3,1,0:T(8,128)S(1)} %get-tuple-element.12, f32[64,1,128,128]{2,3,1,0:T(8,128)S(1)} %get-tuple-element.11, f32[1,2,64,128]{3,2,1,0:T(8,128)S(1)} %copy-done.20, f32[1,2,64,128]{3,2,1,0:T(8,128)S(1)} %copy-done.19), kind=kOutput, calls=%fused_computation.60 | convolution fusion | flops 1613791232 | bytes 10616832 | tf_op jit(solution)/shard_map/rqac,nqcb->nrab/dot_general | solution.py:115
  158.9 7.0 %all-to-all-start.1 = ((bf16[64,64,128]{2,0,1:T(8,128)(2,1)}), bf16[64,64,128]{2,0,1:T(8,128)(2,1)S(1)}, u32[]{:S(2)}, u32[]{:S(2)}) async-start(bf16[64,64,128]{2,0,1:T(8,128)(2,1)} %copy.68), calls=%async_computation.1 | async-start | bytes 2097152 | tf_op jit(solution)/shard_map/all_to_all | solution.py:220
  167.3 26.7 %all-to-all-done.1 = bf16[64,64,128]{2,0,1:T(8,128)(2,1)S(1)} async-done(((bf16[64,64,128]{2,0,1:T(8,128)(2,1)}), bf16[64,64,128]{2,0,1:T(8,128)(2,1)S(1)}, u32[]{:S(2)}, u32[]{:S(2)}) %all-to-all-start.1) | async-done | bytes 1048608 | tf_op jit(solution)/shard_map/all_to_all | solution.py:220
  197.5 3.9 %fusion.23 = bf16[128,4096]{1,0:T(8,128)(2,1)} fusion(bf16[1,128,4096]{2,1,0:T(8,128)(2,1)} %param.11, bf16[1,128,4096]{2,1,0:T(8,128)(2,1)} %param.12, f32[4096,128]{0,1:T(8,128)S(1)} %copy.69, bf16[128,4096]{1,0:T(8,128)(2,1)S(1)} %collective-permute-done), kind=kLoop, calls=%fused_computation.46 | loop fusion | flops 4194304 | bytes 6291456 | tf_op jit(solution)/shard_map/convert_element_type | solution.py:224
  201.4 3.3 %collective-permute-start.2 = (bf16[127,4096]{1,0:T(8,128)(2,1)}, bf16[127,4096]{1,0:T(8,128)(2,1)S(1)}, u32[]{:S(2)}, u32[]{:S(2)}) collective-permute-start(bf16[127,4096]{1,0:T(8,128)(2,1)} %bitcast.183), channel_id=1, source_target_pairs={{1,0},{2,1},{3,2},{4,3},{5,4},{6,5},{7,6},{8,7},{9,8},{10,9},{11,1... | collective-permute-start | bytes 3121160 | tf_op jit(solution)/shard_map/ppermute | solution.py:104
  204.7 28.8 %fusion.13 = f32[1,128,4096]{2,0,1:T(1,128)} fusion(bf16[1,255,4096]{2,1,0:T(8,128)(2,1)S(1)} %copy-done.12, bf16[128,1,4096]{2,0,1:T(8,128)(2,1)} %bitcast.72), kind=kOutput, calls=%fused_computation.27 | convolution fusion | flops 134217728 | bytes 5234688 | tf_op jit(solution)/shard_map/conv_general_dilated | solution.py:168
  233.5 5.6 %copy.74 = f32[1,128,4096]{1,2,0:T(8,128)} copy(f32[1,128,4096]{2,0,1:T(1,128)} %fusion.13) | data formatting | bytes 4194304 | tf_op jit(solution)/shard_map/conv_general_dilated | solution.py:168
  239.2 3.8 %copy.75 = f32[2,4,8,128,64]{4,3,2,1,0:T(8,128)} copy(f32[2,4,8,128,64]{3,4,0,1,2:T(8,128)} %bitcast.184) | data formatting | bytes 4194304 | tf_op jit(solution)/shard_map/transpose | solution.py:234
  243.0 4.7 %reshape.390.x_ref = f32[2,4,8,64,128]{4,3,2,1,0:T(8,128)} reshape(f32[2,4,8,128,64]{4,3,2,1,0:T(8,128)} %copy.75) | data formatting | bytes 4194304 | tf_op jit(solution)/shard_map/reshape | solution.py:234
  247.6 30.2 %shard_map.103 = bf16[64,128]{1,0:T(8,128)(2,1)} custom-call(f32[2,4,8,64,128]{4,3,2,1,0:T(8,128)} %reshape.390.x_ref), custom_call_target="tpu_custom_call" | custom-call | tf_op jit(solution)/shard_map/pallas_call | solution.py:78
  280.9 30.1 %fusion.11 = f32[1,128,4096]{2,0,1:T(1,128)S(1)} fusion(bf16[1,255,4096]{2,1,0:T(8,128)(2,1)S(1)} %maximum_bitcast_fusion.15, bf16[128,1,4096]{2,0,1:T(8,128)(2,1)S(1)} %bitcast.191), kind=kOutput, calls=%fused_computation.25 | convolution fusion | flops 134217728 | bytes 5234688 | tf_op jit(solution)/shard_map/conv_general_dilated | solution.py:168
  311.1 2.8 fusion.34
  (81 shorter events, 30.5 us)
Async XLA Ops:
  0.6 10.4 %copy-start.14 = (bf16[1,128,4096]{2,1,0:T(8,128)(2,1)S(1)}, bf16[1,128,4096]{2,1,0:T(8,128)(2,1)}, u32[]{:S(2)}) copy-start(bf16[1,128,4096]{2,1,0:T(8,128)(2,1)} %param.15) | copy-start | bytes 3145732
  3.8 17.6 %collective-permute-start.1 = (bf16[127,4096]{1,0:T(8,128)(2,1)}, bf16[127,4096]{1,0:T(8,128)(2,1)}, u32[]{:S(2)}, u32[]{:S(2)}) collective-permute-start(bf16[127,4096]{1,0:T(8,128)(2,1)} %slice.64), channel_id=1, source_target_pairs={{0,1},{1,2},{2,3},{3,4},{4,5},{5,6},{6,7},{7,8},{8,9},{9,10},{10,1... | collective-permute-start | bytes 3121160 | tf_op jit(solution)/shard_map/ppermute | solution.py:104
  8.3 44.3 %collective-permute-start = (bf16[128,4096]{1,0:T(8,128)(2,1)}, bf16[128,4096]{1,0:T(8,128)(2,1)S(1)}, u32[]{:S(2)}, u32[]{:S(2)}) collective-permute-start(bf16[128,4096]{1,0:T(8,128)(2,1)} %bitcast), channel_id=1, source_target_pairs={{0,192},{64,0},{128,64},{192,128},{1,193},{65,1},{129,65},{193,129... | collective-permute-start | bytes 3145736 | tf_op jit(solution)/shard_map/ppermute | solution.py:98
  22.9 27.5 %copy-start.11 = (bf16[1,255,4096]{2,1,0:T(8,128)(2,1)}, bf16[1,255,4096]{2,1,0:T(8,128)(2,1)S(1)}, u32[]{:S(2)}) copy-start(bf16[1,255,4096]{2,1,0:T(8,128)(2,1)S(1)} %maximum_bitcast_fusion.13) | copy-start | bytes 6266884
  23.0 27.5 %copy-start.5 = (bf16[1,128,4096]{2,1,0:T(8,128)(2,1)S(1)}, bf16[1,128,4096]{2,1,0:T(8,128)(2,1)}, u32[]{:S(2)}) copy-start(bf16[1,128,4096]{2,1,0:T(8,128)(2,1)} %param.12) | copy-start | bytes 3145732
  23.0 27.5 %copy-start.7 = (bf16[1,128,4096]{2,1,0:T(8,128)(2,1)S(1)}, bf16[1,128,4096]{2,1,0:T(8,128)(2,1)}, u32[]{:S(2)}) copy-start(bf16[1,128,4096]{2,1,0:T(8,128)(2,1)} %param.9) | copy-start | bytes 3145732
  23.0 27.5 %copy-start.8 = (bf16[1,128,4096]{2,1,0:T(8,128)(2,1)S(1)}, bf16[1,128,4096]{2,1,0:T(8,128)(2,1)}, u32[]{:S(2)}) copy-start(bf16[1,128,4096]{2,1,0:T(8,128)(2,1)} %param.11) | copy-start | bytes 3145732
  50.5 2.1 copy-start.13
  52.6 144.9 %copy-start.3 = (bf16[128,4096]{1,0:T(8,128)(2,1)}, bf16[128,4096]{1,0:T(8,128)(2,1)S(1)}, u32[]{:S(2)}) copy-start(bf16[128,4096]{1,0:T(8,128)(2,1)S(1)} %collective-permute-done) | copy-start | bytes 3145732
  56.9 62.7 %all-to-all-start = ((bf16[2,4096,128]{2,0,1:T(2,128)(2,1)}), bf16[2,4096,128]{2,0,1:T(2,128)(2,1)S(1)}, u32[]{:S(2)}, u32[]{:S(2)}) async-start(bf16[2,4096,128]{2,0,1:T(2,128)(2,1)} %copy.56), calls=%async_computation | async-start | bytes 4194304 | tf_op jit(solution)/shard_map/all_to_all | solution.py:203
  121.1 2.4 copy-start.10
  131.8 7.0 %copy-start.2 = (f32[64,1,128,128]{2,3,1,0:T(8,128)S(1)}, f32[64,1,128,128]{2,3,1,0:T(8,128)}, u32[]{:S(2)}) copy-start(f32[64,1,128,128]{2,3,1,0:T(8,128)} %get-tuple-element.24) | copy-start | bytes 12582916
  143.7 1.8 copy-start.21
  150.5 1.9 copy-start.19
  150.5 1.9 copy-start.20
  158.9 35.0 %all-to-all-start.1 = ((bf16[64,64,128]{2,0,1:T(8,128)(2,1)}), bf16[64,64,128]{2,0,1:T(8,128)(2,1)S(1)}, u32[]{:S(2)}, u32[]{:S(2)}) async-start(bf16[64,64,128]{2,0,1:T(8,128)(2,1)} %copy.68), calls=%async_computation.1 | async-start | bytes 2097152 | tf_op jit(solution)/shard_map/all_to_all | solution.py:220
  197.5 36.0 %copy-start = (f32[4096,128]{0,1:T(8,128)}, f32[4096,128]{0,1:T(8,128)S(1)}, u32[]{:S(2)}) copy-start(f32[4096,128]{0,1:T(8,128)S(1)} %copy.69) | copy-start | bytes 6291460
  197.5 7.2 %copy-start.12 = (bf16[1,255,4096]{2,1,0:T(8,128)(2,1)S(1)}, bf16[1,255,4096]{2,1,0:T(8,128)(2,1)}, u32[]{:S(2)}) copy-start(bf16[1,255,4096]{2,1,0:T(8,128)(2,1)} %copy-done.11) | copy-start | bytes 6266884
  201.4 78.0 %collective-permute-start.2 = (bf16[127,4096]{1,0:T(8,128)(2,1)}, bf16[127,4096]{1,0:T(8,128)(2,1)S(1)}, u32[]{:S(2)}, u32[]{:S(2)}) collective-permute-start(bf16[127,4096]{1,0:T(8,128)(2,1)} %bitcast.183), channel_id=1, source_target_pairs={{1,0},{2,1},{3,2},{4,3},{5,4},{6,5},{7,6},{8,7},{9,8},{10,9},{11,1... | collective-permute-start | bytes 3121160 | tf_op jit(solution)/shard_map/ppermute | solution.py:104
  247.6 33.2 %copy-start.15 = (bf16[1,128,4096]{2,1,0:T(8,128)(2,1)S(1)}, bf16[1,128,4096]{2,1,0:T(8,128)(2,1)}, u32[]{:S(2)}) copy-start(bf16[1,128,4096]{2,1,0:T(8,128)(2,1)} %param.15) | copy-start | bytes 3145732
  280.9 30.2 %copy-start.1 = (f32[4096,128]{0,1:T(8,128)S(1)}, f32[4096,128]{0,1:T(8,128)}, u32[]{:S(2)}) copy-start(f32[4096,128]{0,1:T(8,128)} %copy-done) | copy-start | bytes 6291460
  280.9 30.2 %copy-start.4 = (bf16[128,4096]{1,0:T(8,128)(2,1)S(1)}, bf16[128,4096]{1,0:T(8,128)(2,1)}, u32[]{:S(2)}) copy-start(bf16[128,4096]{1,0:T(8,128)(2,1)} %copy-done.3) | copy-start | bytes 3145732
  280.9 30.2 %copy-start.6 = (bf16[1,128,4096]{2,1,0:T(8,128)(2,1)S(1)}, bf16[1,128,4096]{2,1,0:T(8,128)(2,1)}, u32[]{:S(2)}) copy-start(bf16[1,128,4096]{2,1,0:T(8,128)(2,1)} %param.12) | copy-start | bytes 3145732
  280.9 30.2 %copy-start.9 = (bf16[1,128,4096]{2,1,0:T(8,128)(2,1)S(1)}, bf16[1,128,4096]{2,1,0:T(8,128)(2,1)}, u32[]{:S(2)}) copy-start(bf16[1,128,4096]{2,1,0:T(8,128)(2,1)} %param.10) | copy-start | bytes 3145732
  (4 other events, 6.4 us)
where the time goes:
time: 320 us; the launch traced here: 314 us
  matrix products  113 us (35%)
  waiting for transfers between devices  70.2 us (22%)
  local copies, waits for them, and re-layouts  38.7 us (12%)
  starting transfers between devices  30.8 us (10%)
  Pallas kernels  30.2 us (9%)
  other arithmetic  30.1 us (9%)
    conv_general_dilated x3, matrix products, depthwise(): lax.conv_general_dilated(extended[None], kernel[:, None, :], (1,), 'VALID...  86.4 us
    all_to_all x1, waiting for transfers between devices, per_device(): lax.all_to_all(jnp.stack([grad_z.T, long_in.T]), 'ctx', split_axis=1, con...  43.4 us
    pallas_call x1, Pallas kernels, tap_exchange(): pl.pallas_call(functools.partial(tap_exchange_kernel, nz, nx, nc, scale),...  30.2 us
    all_to_all x1, waiting for transfers between devices, per_device(): lax.all_to_all(input_part.astype(jnp.bfloat16), 'ctx', split_axis=1, conc...  26.7 us
    dot_general x6, matrix products, contract(): jnp.einsum(form, left, right, precision=lax.Precision.HIGH, preferred_ele...  26.3 us
    all_to_all x1, starting transfers between devices, per_device(): lax.all_to_all(jnp.stack([grad_z.T, long_in.T]), 'ctx', split_axis=1, con...  13.2 us
    rev x1, local copies, waits for them, and re-layouts, per_device(): branch = depthwise(extended, filter_taps[::-1])  10.2 us
    ppermute x2, starting transfers between devices, shifted(): return lax.ppermute(array, axis, pairs)  7.75 us
  transfers between devices with their start and end apart: 5, of which 2 were waited for; matrix products, arithmetic and copies ran while one was open for 30% of the time, Pallas kernels for 10%

commit v1 on v0

--- a/solution.py
+++ b/solution.py
@@ -39,23 +39,23 @@
             device_id_type=MESH_IDS,
         )
 
-    first = send(x_ref.at[1 - core], r1, peers[0], 0, 0)
+    first = send(x_ref.at[:, :, 1 - core], r1, peers[0], 0, 0)
     first.start()
     first.wait()
-    s1[...] = x_ref[core] + r1[...]
+    s1[...] = x_ref[:, :, core] + r1[...]
 
     second = []
     for k in range(1, nx):
         target = (xi + k) % nx
-        copy = send(s1.at[target], r2.at[xi], device(zi, target, core), 1 + target, 1 + xi)
+        copy = send(s1.at[:, target], r2.at[xi], device(zi, target, core), 1 + target, 1 + xi)
         copy.start()
         second.append(copy)
     for k in range(1, nx):
         source = (xi + nx - k) % nx
-        send(s1.at[source], r2.at[source], device(zi, source, core), 1 + source, 1 + source).wait_recv()
+        send(s1.at[:, source], r2.at[source], device(zi, source, core), 1 + source, 1 + source).wait_recv()
     for copy in second:
         copy.wait_send()
-    r2[xi] = s1[xi]
+    r2[xi] = s1[:, xi]
     s2[...] = jnp.sum(r2[...], axis=0)
 
     third = []
@@ -74,15 +74,15 @@
 
 
 def tap_exchange(parts, scale):
-    nc, nx, nz, taps, width = parts.shape
+    nz, nx, nc, taps, width = parts.shape
     return pl.pallas_call(
         functools.partial(tap_exchange_kernel, nz, nx, nc, scale),
         out_shape=jax.ShapeDtypeStruct((taps, width), jnp.bfloat16),
         in_specs=[pl.BlockSpec(memory_space=pltpu.VMEM)],
         out_specs=pl.BlockSpec(memory_space=pltpu.VMEM),
         scratch_shapes=[
-            pltpu.VMEM((nx, nz, taps, width), jnp.float32),
-            pltpu.VMEM((nx, nz, taps, width), jnp.float32),
+            pltpu.VMEM((nz, nx, taps, width), jnp.float32),
+            pltpu.VMEM((nz, nx, taps, width), jnp.float32),
             pltpu.VMEM((nx, nz, taps, width), jnp.float32),
             pltpu.VMEM((nz, taps, width), jnp.float32),
             pltpu.VMEM((nz, taps, width), jnp.float32),
@@ -196,7 +196,9 @@
     mixed_in = (inputs * gate_pre).astype(jnp.bfloat16)
     earlier = shifted(mixed_in[tokens - reach :], "ctx", 1)
     extended = jnp.concatenate([earlier, mixed_in], 0)
-    branch = depthwise(extended, filter_taps[::-1])
+    flip = jnp.eye(filter_taps.shape[0], dtype=filter_taps.dtype)[::-1]
+    flipped_taps = jnp.dot(flip, filter_taps, preferred_element_type=jnp.float32)
+    branch = depthwise(extended, flipped_taps.astype(filter_taps.dtype))
     resid = inputs + beta * branch * gate_mid
     long_in = (resid * gate_long).astype(jnp.bfloat16)
     grad_z = (beta * adjoint * gate_out).astype(jnp.bfloat16)
@@ -225,16 +227,21 @@
     later = shifted(grad_b[:reach], "ctx", -1)
     grad_act = depthwise(jnp.concatenate([grad_b, later], 0), filter_taps)
     input_grad = (grad_u + grad_act * gate_pre).astype(jnp.bfloat16)[None]
-    tap_part = depthwise(extended, grad_b)
+    tap_part = lax.conv_general_dilated(
+        extended[None],
+        grad_b[:, None, :],
+        (1,),
+        "VALID",
+        dimension_numbers=("NWC", "WIO", "NCW"),
+        feature_group_count=extended.shape[1],
+        preferred_element_type=jnp.float32,
+    )[0]
     devices = lax.axis_size("ctx")
-    columns = tap_part.shape[1] // devices
+    columns = tap_part.shape[0] // devices
     chip_cores, chips_x = 2, 4
     chips_z = devices // (chip_cores * chips_x)
-    parts = tap_part.reshape(tap_part.shape[0], chips_z, chips_x, chip_cores, columns)
-    parts = parts.transpose(3, 2, 1, 0, 4).reshape(
-        chip_cores, chips_x, chips_z, tap_part.shape[0] * columns // 128, 128
-    )
-    mid_grad = tap_exchange(parts, scale).reshape(tap_part.shape[0], columns)[::-1][None]
+    parts = tap_part.reshape(chips_z, chips_x, chip_cores, columns, tap_part.shape[1])
+    mid_grad = tap_exchange(parts, scale).T[::-1][None]
     return (input_grad, long_grad, mid_grad)
 
 

time: 320 us -> 317 us (level)
  local copies, waits for them, and re-layouts: 38.7 us -> 22.3 us
  waiting for transfers between devices: 70.2 us -> 78.9 us
    conv_general_dilated x0 -> x1, matrix products: none -> 29.1 us  [per_device(): lax.conv_general_dilated(extended[None], grad_b[:, None, :], (1,), 'VALID...]
    conv_general_dilated x3 -> x2, matrix products: 86.4 us -> 57.5 us  [depthwise(): lax.conv_general_dilated(extended[None], kernel[:, None, :], (1,), 'VALID...]
    rev x2, local copies, waits for them, and re-layouts: 10.3 us -> 1.43 us  [the longest x1 1.4 us: per_device(): mid_grad = tap_exchange(parts, scale).T[::-1][None]]
    ppermute x2, waiting for transfers between devices: 0.01 us -> 8.74 us  [shifted(): return lax.ppermute(array, axis, pairs)]
    reshape x2 -> x0, local copies, waits for them, and re-layouts: 5.47 us -> none  [the longest x1 4.67 us: per_device(): parts.transpose(3, 2, 1, 0, 4)]
    transpose x1 -> x0, local copies, waits for them, and re-layouts: 3.82 us -> none  [per_device(): parts.transpose(3, 2, 1, 0, 4)]
  transfers between devices with their start and end apart: 5 -> 5, of which waited for: 2 -> 3; matrix products, arithmetic and copies ran while one was open for 30% -> 24% of each run, Pallas kernels for 10% -> 10%
where the time goes in v1:
time: 317 us; the launch traced here: 311 us
  matrix products  113 us (36%)
  waiting for transfers between devices  78.9 us (25%)
  other arithmetic  33.2 us (10%)
  starting transfers between devices  32 us (10%)
  Pallas kernels  30.1 us (9%)
  local copies, waits for them, and re-layouts  22.3 us (7%)
    conv_general_dilated x2, matrix products, depthwise(): lax.conv_general_dilated(extended[None], kernel[:, None, :], (1,), 'VALID...  57.5 us
    all_to_all x1, waiting for transfers between devices, per_device(): lax.all_to_all(jnp.stack([grad_z.T, long_in.T]), 'ctx', split_axis=1, con...  43.4 us
    pallas_call x1, Pallas kernels, tap_exchange(): pl.pallas_call(functools.partial(tap_exchange_kernel, nz, nx, nc, scale),...  30.1 us
    conv_general_dilated x1, matrix products, per_device(): lax.conv_general_dilated(extended[None], grad_b[:, None, :], (1,), 'VALID...  29.1 us
    all_to_all x1, waiting for transfers between devices, per_device(): lax.all_to_all(input_part.astype(jnp.bfloat16), 'ctx', split_axis=1, conc...  26.7 us
    dot_general x6, matrix products, contract(): jnp.einsum(form, left, right, precision=lax.Precision.HIGH, preferred_ele...  26.1 us
    all_to_all x1, starting transfers between devices, per_device(): lax.all_to_all(jnp.stack([grad_z.T, long_in.T]), 'ctx', split_axis=1, con...  14.4 us
    ppermute x2, waiting for transfers between devices, shifted(): return lax.ppermute(array, axis, pairs)  8.74 us
  transfers between devices with their start and end apart: 5, of which 3 were waited for; matrix products, arithmetic and copies ran while one was open for 24% of the time, Pallas kernels for 10%

profile of v1, /device:TPU:1, one launch (start us, length us, event | category | flops | bytes accessed | tf_op | source)
XLA Modules:
  0.0 311.1 jit_solution(17874671303719258003)
XLA Ops:
  3.8 4.5 %collective-permute-start.1 = (bf16[127,4096]{1,0:T(8,128)(2,1)}, bf16[127,4096]{1,0:T(8,128)(2,1)}, u32[]{:S(2)}, u32[]{:S(2)}) collective-permute-start(bf16[127,4096]{1,0:T(8,128)(2,1)} %slice.64), channel_id=1, source_target_pairs={{0,1},{1,2},{2,3},{3,4},{4,5},{5,6},{6,7},{7,8},{8,9},{9,10},{10,1... | collective-permute-start | bytes 3121160 | tf_op jit(solution)/shard_map/ppermute | solution.py:104
  8.3 2.8 collective-permute-start
  11.6 8.7 %collective-permute-done.1 = bf16[127,4096]{1,0:T(8,128)(2,1)} collective-permute-done((bf16[127,4096]{1,0:T(8,128)(2,1)}, bf16[127,4096]{1,0:T(8,128)(2,1)}, u32[]{:S(2)}, u32[]{:S(2)}) %collective-permute-start.1) | collective-permute-done | bytes 1040416 | tf_op jit(solution)/shard_map/ppermute | solution.py:104
  21.9 27.4 %convolution_multiply_fusion = f32[1,128,4096]{2,0,1:T(1,128)S(1)} fusion(bf16[1,255,4096]{2,1,0:T(8,128)(2,1)S(1)} %maximum_bitcast_fusion.13, bf16[128,1,4096]{2,0,1:T(8,128)(2,1)S(1)} %fusion.11), kind=kOutput, calls=%fused_computation.17 | convolution fusion | flops 134742016 | bytes 5234688 | tf_op jit(solution)/shard_map/conv_general_dilated | solution.py:168
  53.3 6.2 %copy.53 = bf16[2,4096,128]{2,0,1:T(2,128)(2,1)} copy(bf16[2,4096,128]{1,2,0:T(8,128)(2,1)} %pad_maximum_fusion) | data formatting | bytes 4194304 | tf_op jit(solution)/shard_map/stack | solution.py:206
  59.5 14.4 %all-to-all-start = ((bf16[2,4096,128]{2,0,1:T(2,128)(2,1)}), bf16[2,4096,128]{2,0,1:T(2,128)(2,1)S(1)}, u32[]{:S(2)}, u32[]{:S(2)}) async-start(bf16[2,4096,128]{2,0,1:T(2,128)(2,1)} %copy.53), calls=%async_computation | async-start | bytes 4194304 | tf_op jit(solution)/shard_map/all_to_all | solution.py:205
  79.9 43.4 %all-to-all-done = bf16[2,4096,128]{2,0,1:T(2,128)(2,1)S(1)} async-done(((bf16[2,4096,128]{2,0,1:T(2,128)(2,1)}), bf16[2,4096,128]{2,0,1:T(2,128)(2,1)S(1)}, u32[]{:S(2)}, u32[]{:S(2)}) %all-to-all-start) | async-done | bytes 2097184 | tf_op jit(solution)/shard_map/all_to_all | solution.py:205
  124.8 2.4 convolution_bitcast_fusion
  127.2 2.4 convolution_bitcast_fusion.1
  129.6 6.0 %multiply_subtract_fusion.3 = (f32[64,1,128,128]{2,3,1,0:T(8,128)S(1)}, f32[64,1,128,128]{2,3,1,0:T(8,128)}, f32[64,1,128,128]{2,3,1,0:T(8,128)}, f32[64,1,128,128]{2,3,1,0:T(8,128)}) fusion(f32[64,2,128,128]{2,3,1,0:T(8,128)S(1)} %convolution_bitcast_fusion, f32[128,128]{0,1:T(8,128)S(1)} %get-tuple-element.27, f32[128,128]{0,1:T(8,128)S(1)} %get-tuple-element.28, ...), kind=kLoop, calls=%fused_computation.26 | loop fusion | flops 12582912 | bytes 33685504 | tf_op jit(solution)/shard_map/sub | solution.py:137
  135.6 7.1 %fusion.21 = f32[64,2,128,128]{2,3,0,1:T(8,128)S(1)} fusion(f32[64,1,128,128]{2,3,1,0:T(8,128)} %get-tuple-element.8, f32[64,1,128,128]{2,3,1,0:T(8,128)S(1)} %get-tuple-element.7, f32[1,2,128,128]{2,3,0,1:T(8,128)S(1)} %get-tuple-element.14, f32[1,2,128,128]{2,3,0,1:T(8,128)S(1)} %get-tuple-element.19), kind=kOutput, calls=%fused_computation.35 | convolution fusion | flops 3223388160 | bytes 17039360 | tf_op jit(solution)/shard_map/nqcb,qpbd->npcd/dot_general | solution.py:115
  142.7 4.9 %fusion.20 = f32[64,2,128,128]{2,3,0,1:T(8,128)S(1)} fusion(f32[64,1,128,128]{2,3,1,0:T(8,128)S(1)} %copy-done.3, f32[64,1,128,128]{2,3,1,0:T(8,128)S(1)} %copy-done.4, f32[1,2,128,128]{2,3,0,1:T(8,128)S(1)} %get-tuple-element.14, f32[1,2,128,128]{2,3,0,1:T(8,128)S(1)} %get-tuple-element.19), kind=kOutput, calls=%fused_computation.34 | convolution fusion | flops 3223388160 | bytes 17039360 | tf_op jit(solution)/shard_map/nqcb,qpbd->npcd/dot_general | solution.py:115
  147.7 2.8 multiply_add_fusion.1
  150.5 5.0 %fusion.17 = f32[64,2,128,128]{2,3,1,0:T(8,128)S(1)} fusion(f32[64,1,128,128]{2,3,0,1:T(8,128)S(1)} %get-tuple-element.4, f32[64,1,128,128]{2,3,0,1:T(8,128)S(1)} %get-tuple-element.3, f32[1,2,128,128]{2,3,1,0:T(8,128)S(1)} %copy-done.21, f32[1,2,128,128]{2,3,1,0:T(8,128)S(1)} %copy-done.20), kind=kOutput, calls=%fused_computation.32 | convolution fusion | flops 3223388160 | bytes 17039360 | tf_op jit(solution)/shard_map/npcd,pqdb->nqcb/dot_general | solution.py:115
  157.4 4.4 %fusion.33 = bf16[64,2,64,128]{3,2,1,0:T(8,128)(2,1)S(1)} fusion(f32[64,1,128,128]{2,3,1,0:T(8,128)S(1)} %get-tuple-element.6, f32[64,1,128,128]{2,3,1,0:T(8,128)S(1)} %get-tuple-element.5, f32[1,2,64,128]{3,2,1,0:T(8,128)S(1)} %copy-done.19, f32[1,2,64,128]{3,2,1,0:T(8,128)S(1)} %copy-done.18), kind=kOutput, calls=%fused_computation.62 | convolution fusion | flops 1613791232 | bytes 10616832 | tf_op jit(solution)/shard_map/rqac,nqcb->nrab/dot_general | solution.py:115
  163.7 7.1 %all-to-all-start.1 = ((bf16[64,64,128]{2,0,1:T(8,128)(2,1)}), bf16[64,64,128]{2,0,1:T(8,128)(2,1)S(1)}, u32[]{:S(2)}, u32[]{:S(2)}) async-start(bf16[64,64,128]{2,0,1:T(8,128)(2,1)} %copy.65), calls=%async_computation.1 | async-start | bytes 2097152 | tf_op jit(solution)/shard_map/all_to_all | solution.py:222
  172.0 26.7 %all-to-all-done.1 = bf16[64,64,128]{2,0,1:T(8,128)(2,1)S(1)} async-done(((bf16[64,64,128]{2,0,1:T(8,128)(2,1)}), bf16[64,64,128]{2,0,1:T(8,128)(2,1)S(1)}, u32[]{:S(2)}, u32[]{:S(2)}) %all-to-all-start.1) | async-done | bytes 1048608 | tf_op jit(solution)/shard_map/all_to_all | solution.py:222
  202.3 4.2 %fusion.24 = bf16[128,4096]{1,0:T(8,128)(2,1)} fusion(bf16[1,128,4096]{2,1,0:T(8,128)(2,1)} %param.11, bf16[1,128,4096]{2,1,0:T(8,128)(2,1)} %param.12, f32[4096,128]{0,1:T(8,128)S(1)} %copy.66, bf16[128,4096]{1,0:T(8,128)(2,1)} %copy-done.5), kind=kLoop, calls=%fused_computation.48 | loop fusion | flops 4194304 | bytes 6291456 | tf_op jit(solution)/shard_map/convert_element_type | solution.py:226
  206.5 3.3 %collective-permute-start.2 = (bf16[127,4096]{1,0:T(8,128)(2,1)}, bf16[127,4096]{1,0:T(8,128)(2,1)}, u32[]{:S(2)}, u32[]{:S(2)}) collective-permute-start(bf16[127,4096]{1,0:T(8,128)(2,1)} %bitcast.184), channel_id=1, source_target_pairs={{1,0},{2,1},{3,2},{4,3},{5,4},{6,5},{7,6},{8,7},{9,8},{10,9},{11,1... | collective-permute-start | bytes 3121160 | tf_op jit(solution)/shard_map/ppermute | solution.py:104
  209.8 29.1 %fusion.14 = f32[1,4096,128]{1,0,2:T(1,128)} fusion(bf16[1,255,4096]{2,1,0:T(8,128)(2,1)S(1)} %copy-done.14, bf16[128,1,4096]{2,0,1:T(8,128)(2,1)} %bitcast.72), kind=kOutput, calls=%fused_computation.29 | convolution fusion | flops 134217728 | bytes 5234688 | tf_op jit(solution)/shard_map/conv_general_dilated | solution.py:230
  238.9 5.6 %copy.71 = f32[1,4096,128]{2,1,0:T(8,128)} copy(f32[1,4096,128]{1,0,2:T(1,128)} %fusion.14) | data formatting | bytes 4194304 | tf_op jit(solution)/shard_map/conv_general_dilated | solution.py:230
  244.5 30.1 %shard_map.103 = bf16[64,128]{1,0:T(8,128)(2,1)} custom-call(f32[8,4,2,64,128]{4,3,2,1,0:T(8,128)} %bitcast.190), custom_call_target="tpu_custom_call" | custom-call | tf_op jit(solution)/shard_map/pallas_call | solution.py:78
  277.8 30.1 %fusion.12 = f32[1,128,4096]{2,0,1:T(1,128)S(1)} fusion(bf16[1,255,4096]{2,1,0:T(8,128)(2,1)S(1)} %maximum_bitcast_fusion.15, bf16[128,1,4096]{2,0,1:T(8,128)(2,1)S(1)} %bitcast.185), kind=kOutput, calls=%fused_computation.27 | convolution fusion | flops 134217728 | bytes 5234688 | tf_op jit(solution)/shard_map/conv_general_dilated | solution.py:168
  308.0 2.8 fusion.35
  (77 shorter events, 28.3 us)
Async XLA Ops:
  0.6 10.5 %copy-start = (bf16[1,128,4096]{2,1,0:T(8,128)(2,1)S(1)}, bf16[1,128,4096]{2,1,0:T(8,128)(2,1)}, u32[]{:S(2)}) copy-start(bf16[1,128,4096]{2,1,0:T(8,128)(2,1)} %param.15) | copy-start | bytes 3145732
  3.8 16.5 %collective-permute-start.1 = (bf16[127,4096]{1,0:T(8,128)(2,1)}, bf16[127,4096]{1,0:T(8,128)(2,1)}, u32[]{:S(2)}, u32[]{:S(2)}) collective-permute-start(bf16[127,4096]{1,0:T(8,128)(2,1)} %slice.64), channel_id=1, source_target_pairs={{0,1},{1,2},{2,3},{3,4},{4,5},{5,6},{6,7},{7,8},{8,9},{9,10},{10,1... | collective-permute-start | bytes 3121160 | tf_op jit(solution)/shard_map/ppermute | solution.py:104
  8.3 43.2 %collective-permute-start = (bf16[128,4096]{1,0:T(8,128)(2,1)}, bf16[128,4096]{1,0:T(8,128)(2,1)S(1)}, u32[]{:S(2)}, u32[]{:S(2)}) collective-permute-start(bf16[128,4096]{1,0:T(8,128)(2,1)} %bitcast), channel_id=1, source_target_pairs={{0,192},{64,0},{128,64},{192,128},{1,193},{65,1},{129,65},{193,129... | collective-permute-start | bytes 3145736 | tf_op jit(solution)/shard_map/ppermute | solution.py:98
  21.8 27.5 %copy-start.13 = (bf16[1,255,4096]{2,1,0:T(8,128)(2,1)}, bf16[1,255,4096]{2,1,0:T(8,128)(2,1)S(1)}, u32[]{:S(2)}) copy-start(bf16[1,255,4096]{2,1,0:T(8,128)(2,1)S(1)} %maximum_bitcast_fusion.13) | copy-start | bytes 6266884
  21.9 27.5 %copy-start.7 = (bf16[1,128,4096]{2,1,0:T(8,128)(2,1)S(1)}, bf16[1,128,4096]{2,1,0:T(8,128)(2,1)}, u32[]{:S(2)}) copy-start(bf16[1,128,4096]{2,1,0:T(8,128)(2,1)} %param.12) | copy-start | bytes 3145732
  21.9 27.5 %copy-start.9 = (bf16[1,128,4096]{2,1,0:T(8,128)(2,1)S(1)}, bf16[1,128,4096]{2,1,0:T(8,128)(2,1)}, u32[]{:S(2)}) copy-start(bf16[1,128,4096]{2,1,0:T(8,128)(2,1)} %param.9) | copy-start | bytes 3145732
  21.9 27.5 %copy-start.10 = (bf16[1,128,4096]{2,1,0:T(8,128)(2,1)S(1)}, bf16[1,128,4096]{2,1,0:T(8,128)(2,1)}, u32[]{:S(2)}) copy-start(bf16[1,128,4096]{2,1,0:T(8,128)(2,1)} %param.11) | copy-start | bytes 3145732
  49.3 2.1 copy-start.15
  51.5 8.0 %copy-start.5 = (bf16[128,4096]{1,0:T(8,128)(2,1)}, bf16[128,4096]{1,0:T(8,128)(2,1)S(1)}, u32[]{:S(2)}) copy-start(bf16[128,4096]{1,0:T(8,128)(2,1)S(1)} %collective-permute-done) | copy-start | bytes 3145732
  59.5 63.9 %all-to-all-start = ((bf16[2,4096,128]{2,0,1:T(2,128)(2,1)}), bf16[2,4096,128]{2,0,1:T(2,128)(2,1)S(1)}, u32[]{:S(2)}, u32[]{:S(2)}) async-start(bf16[2,4096,128]{2,0,1:T(2,128)(2,1)} %copy.53), calls=%async_computation | async-start | bytes 4194304 | tf_op jit(solution)/shard_map/all_to_all | solution.py:205
  124.8 2.4 copy-start.12
  135.6 7.1 %copy-start.3 = (f32[64,1,128,128]{2,3,1,0:T(8,128)S(1)}, f32[64,1,128,128]{2,3,1,0:T(8,128)}, u32[]{:S(2)}) copy-start(f32[64,1,128,128]{2,3,1,0:T(8,128)} %get-tuple-element.17) | copy-start | bytes 12582916
  135.6 7.1 %copy-start.4 = (f32[64,1,128,128]{2,3,1,0:T(8,128)S(1)}, f32[64,1,128,128]{2,3,1,0:T(8,128)}, u32[]{:S(2)}) copy-start(f32[64,1,128,128]{2,3,1,0:T(8,128)} %get-tuple-element.18) | copy-start | bytes 12582916
  147.6 2.8 copy-start.20
  147.7 2.8 copy-start.21
  155.5 1.9 copy-start.18
  163.7 35.1 %all-to-all-start.1 = ((bf16[64,64,128]{2,0,1:T(8,128)(2,1)}), bf16[64,64,128]{2,0,1:T(8,128)(2,1)S(1)}, u32[]{:S(2)}, u32[]{:S(2)}) async-start(bf16[64,64,128]{2,0,1:T(8,128)(2,1)} %copy.65), calls=%async_computation.1 | async-start | bytes 2097152 | tf_op jit(solution)/shard_map/all_to_all | solution.py:222
  202.3 36.6 %copy-start.1 = (f32[4096,128]{0,1:T(8,128)}, f32[4096,128]{0,1:T(8,128)S(1)}, u32[]{:S(2)}) copy-start(f32[4096,128]{0,1:T(8,128)S(1)} %copy.66) | copy-start | bytes 6291460
  202.3 7.5 %copy-start.14 = (bf16[1,255,4096]{2,1,0:T(8,128)(2,1)S(1)}, bf16[1,255,4096]{2,1,0:T(8,128)(2,1)}, u32[]{:S(2)}) copy-start(bf16[1,255,4096]{2,1,0:T(8,128)(2,1)} %copy-done.13) | copy-start | bytes 6266884
  206.5 69.5 %collective-permute-start.2 = (bf16[127,4096]{1,0:T(8,128)(2,1)}, bf16[127,4096]{1,0:T(8,128)(2,1)}, u32[]{:S(2)}, u32[]{:S(2)}) collective-permute-start(bf16[127,4096]{1,0:T(8,128)(2,1)} %bitcast.184), channel_id=1, source_target_pairs={{1,0},{2,1},{3,2},{4,3},{5,4},{6,5},{7,6},{8,7},{9,8},{10,9},{11,1... | collective-permute-start | bytes 3121160 | tf_op jit(solution)/shard_map/ppermute | solution.py:104
  277.8 30.2 %copy-start.2 = (f32[4096,128]{0,1:T(8,128)S(1)}, f32[4096,128]{0,1:T(8,128)}, u32[]{:S(2)}) copy-start(f32[4096,128]{0,1:T(8,128)} %copy-done.1) | copy-start | bytes 6291460
  277.8 30.2 %copy-start.6 = (bf16[128,4096]{1,0:T(8,128)(2,1)S(1)}, bf16[128,4096]{1,0:T(8,128)(2,1)}, u32[]{:S(2)}) copy-start(bf16[128,4096]{1,0:T(8,128)(2,1)} %copy-done.5) | copy-start | bytes 3145732
  277.8 30.2 %copy-start.8 = (bf16[1,128,4096]{2,1,0:T(8,128)(2,1)S(1)}, bf16[1,128,4096]{2,1,0:T(8,128)(2,1)}, u32[]{:S(2)}) copy-start(bf16[1,128,4096]{2,1,0:T(8,128)(2,1)} %param.12) | copy-start | bytes 3145732
  277.8 30.2 %copy-start.11 = (bf16[1,128,4096]{2,1,0:T(8,128)(2,1)S(1)}, bf16[1,128,4096]{2,1,0:T(8,128)(2,1)}, u32[]{:S(2)}) copy-start(bf16[1,128,4096]{2,1,0:T(8,128)(2,1)} %param.10) | copy-start | bytes 3145732
  (3 other events, 4.8 us)

commit v2 on v1

--- a/solution.py
+++ b/solution.py
@@ -90,6 +90,90 @@
         ],
         compiler_params=pltpu.CompilerParams(collective_id=0, has_side_effects=True),
     )(parts)
+
+
+def exchange_kernel(n, send_part, recv_part, x_ref, o_ref, local_sem, send_sems, recv_sems):
+    me = lax.axis_index("ctx")
+    sec = lax.axis_index("section")
+    barrier = pltpu.get_barrier_semaphore()
+
+    def greet(k, carry):
+        peer = lax.rem(me + k, n)
+        pl.semaphore_signal(barrier, inc=1, device_id=(sec, peer), device_id_type=MESH_IDS)
+        return carry
+
+    lax.fori_loop(1, n, greet, 0)
+    pl.semaphore_wait(barrier, n - 1)
+
+    def copy(peer, source):
+        return pltpu.make_async_remote_copy(
+            src_ref=send_part(x_ref, peer),
+            dst_ref=recv_part(o_ref, source),
+            send_sem=send_sems.at[peer],
+            recv_sem=recv_sems.at[source],
+            device_id=(sec, peer),
+            device_id_type=MESH_IDS,
+        )
+
+    def start(k, carry):
+        copy(lax.rem(me + k, n), me).start()
+        return carry
+
+    lax.fori_loop(1, n, start, 0)
+    own = pltpu.make_async_copy(send_part(x_ref, me), recv_part(o_ref, me), local_sem)
+    own.start()
+
+    def finish(k, carry):
+        copy(lax.rem(me + n - k, n), lax.rem(me + n - k, n)).wait_recv()
+        copy(lax.rem(me + k, n), me).wait_send()
+        return carry
+
+    lax.fori_loop(1, n, finish, 0)
+    own.wait()
+
+
+def exchange(x, out_shape, send_part, recv_part, collective):
+    n = lax.axis_size("ctx")
+    return pl.pallas_call(
+        functools.partial(exchange_kernel, n, send_part, recv_part),
+        out_shape=jax.ShapeDtypeStruct(out_shape, x.dtype),
+        in_specs=[pl.BlockSpec(memory_space=pltpu.VMEM)],
+        out_specs=pl.BlockSpec(memory_space=pltpu.VMEM),
+        scratch_shapes=[
+            pltpu.SemaphoreType.DMA(()),
+            pltpu.SemaphoreType.DMA((n,)),
+            pltpu.SemaphoreType.DMA((n,)),
+        ],
+        compiler_params=pltpu.CompilerParams(collective_id=collective, has_side_effects=True),
+    )(x)
+
+
+def to_channels(x):
+    n = lax.axis_size("ctx")
+    count, channels, tokens = x.shape
+    rows = channels // n
+
+    def send_part(ref, peer):
+        return ref.at[:, pl.ds(pl.multiple_of(peer * rows, rows), rows), :]
+
+    def recv_part(ref, source):
+        return ref.at[:, :, pl.ds(pl.multiple_of(source * tokens, tokens), tokens)]
+
+    return exchange(x, (count, rows, tokens * n), send_part, recv_part, 1)
+
+
+def to_positions(x):
+    n = lax.axis_size("ctx")
+    rows, length = x.shape
+    tokens = length // n
+
+    def send_part(ref, peer):
+        return ref.at[:, pl.ds(pl.multiple_of(peer * tokens, tokens), tokens)]
+
+    def recv_part(ref, source):
+        return ref.at[pl.ds(pl.multiple_of(source * rows, rows), rows), :]
+
+    return exchange(x, (rows * n, tokens), send_part, recv_part, 2)
 
 
 def passed_along(value, axis, steps):
@@ -202,9 +286,7 @@
     resid = inputs + beta * branch * gate_mid
     long_in = (resid * gate_long).astype(jnp.bfloat16)
     grad_z = (beta * adjoint * gate_out).astype(jnp.bfloat16)
-    channel_z, channel_w = lax.all_to_all(
-        jnp.stack([grad_z.T, long_in.T]), "ctx", split_axis=1, concat_axis=2, tiled=True
-    )
+    channel_z, channel_w = to_channels(jnp.stack([grad_z.T, long_in.T]))
     factor_b = math.gcd(seq_len, 128)
     factor_a = 2 * seq_len // factor_b
     zspec = to_spectrum(channel_z[:, None], factor_a, factor_b)
@@ -219,9 +301,7 @@
         jnp.stack([joint_re, joint_im], 1), factor_a, factor_b, scale
     )
     long_grad = lag_grad.astype(jnp.bfloat16)[None]
-    returned = lax.all_to_all(
-        input_part.astype(jnp.bfloat16), "ctx", split_axis=1, concat_axis=0, tiled=True
-    ).T
+    returned = to_positions(input_part.astype(jnp.bfloat16)).T
     grad_u = adjoint + returned.astype(jnp.float32) * gate_long
     grad_b = (beta * grad_u * gate_mid).astype(jnp.bfloat16)
     later = shifted(grad_b[:reach], "ctx", -1)

time: 317 us -> 377 us (1.19)
  Pallas kernels: 30.1 us -> 130 us
  waiting for transfers between devices: 78.9 us -> 0.01 us
  local copies, waits for them, and re-layouts: 22.3 us -> 69.2 us
  starting transfers between devices: 32 us -> 9.16 us
  matrix products: 113 us -> 128 us
    pallas_call x0 -> x2, Pallas kernels: none -> 96.5 us  [exchange(): pl.pallas_call(functools.partial(exchange_kernel, n, send_part, recv_part...]
    all_to_all x2 -> x0, waiting for transfers between devices: 70.2 us -> none  [the longest x1 43.4 us: per_device(): lax.all_to_all(jnp.stack([grad_z.T, long_in.T]), 'ctx', split_axis=1, con...]
    broadcast_in_dim x0 -> x3, local copies, waits for them, and re-layouts: none -> 24.8 us  [the longest x2 20 us: depthwise(): extended[None]]
    all_to_all x2 -> x0, starting transfers between devices: 21.4 us -> none  [the longest x1 14.4 us: per_device(): lax.all_to_all(jnp.stack([grad_z.T, long_in.T]), 'ctx', split_axis=1, con...]
    unnamed x45 -> x56, local copies, waits for them, and re-layouts: 1.37 us -> 21.4 us
    conv_general_dilated x0 -> x2, local copies, waits for them, and re-layouts: none -> 11.4 us  [depthwise(): lax.conv_general_dilated(extended[None], kernel[:, None, :], (1,), 'VALID...]
    conv_general_dilated x2, matrix products: 57.5 us -> 68.6 us  [depthwise(): lax.conv_general_dilated(extended[None], kernel[:, None, :], (1,), 'VALID...]
    ppermute x2, waiting for transfers between devices: 8.74 us -> 0.01 us  [shifted(): return lax.ppermute(array, axis, pairs)]
  transfers between devices with their start and end apart: 5 -> 3, of which waited for: 3 -> 0; matrix products, arithmetic and copies ran while one was open for 24% -> 31% of each run, Pallas kernels for 10% -> 9%
where the time goes in v2:
time: 377 us; the launch traced here: 372 us
  Pallas kernels  130 us (34%)
  matrix products  128 us (34%)
  local copies, waits for them, and re-layouts  69.2 us (18%)
  other arithmetic  35.5 us (9%)
  starting transfers between devices  9.16 us (2%)
    pallas_call x2, Pallas kernels, exchange(): pl.pallas_call(functools.partial(exchange_kernel, n, send_part, recv_part...  96.5 us
    conv_general_dilated x2, matrix products, depthwise(): lax.conv_general_dilated(extended[None], kernel[:, None, :], (1,), 'VALID...  68.6 us
    pallas_call x1, Pallas kernels, tap_exchange(): pl.pallas_call(functools.partial(tap_exchange_kernel, nz, nx, nc, scale),...  33.2 us
    conv_general_dilated x1, matrix products, per_device(): lax.conv_general_dilated(extended[None], grad_b[:, None, :], (1,), 'VALID...  31.8 us
    dot_general x6, matrix products, contract(): jnp.einsum(form, left, right, precision=lax.Precision.HIGH, preferred_ele...  25.9 us
    unnamed x56, local copies, waits for them, and re-layouts  21.4 us
    broadcast_in_dim x2, local copies, waits for them, and re-layouts, depthwise(): extended[None]  20 us
    conv_general_dilated x2, local copies, waits for them, and re-layouts, depthwise(): lax.conv_general_dilated(extended[None], kernel[:, None, :], (1,), 'VALID...  11.4 us
  transfers between devices with their start and end apart: 3, of which 0 were waited for; matrix products, arithmetic and copies ran while one was open for 31% of the time, Pallas kernels for 9%

profile of v2, /device:TPU:1, one launch (start us, length us, event | category | flops | bytes accessed | tf_op | source)
XLA Modules:
  0.0 372.5 jit_solution(10671951576819328711)
XLA Ops:
  7.0 4.5 %collective-permute-start.1 = (bf16[127,4096]{0,1:T(8,128)(2,1)}, bf16[127,4096]{0,1:T(8,128)(2,1)}, u32[]{:S(2)}, u32[]{:S(2)}) collective-permute-start(bf16[127,4096]{0,1:T(8,128)(2,1)} %slice.62), channel_id=1, source_target_pairs={{0,1},{1,2},{2,3},{3,4},{4,5},{5,6},{6,7},{7,8},{8,9},{9,10},{10,1... | collective-permute-start | bytes 3121160 | tf_op jit(solution)/shard_map/ppermute | solution.py:188
  31.7 3.4 maximum_bitcast_fusion.13
  35.2 10.0 %copy.16 = bf16[1,255,4096]{2,0,1:T(2,128)(2,1)} copy(bf16[1,255,4096]{1,2,0:T(8,128)(2,1)} %maximum_bitcast_fusion.13) | data formatting | bytes 4177920 | tf_op jit(solution)/shard_map/broadcast_in_dim | solution.py:253
  45.2 34.3 %fusion.28 = f32[1,128,4096]{2,0,1:T(1,128)} fusion(bf16[1,255,4096]{2,0,1:T(2,128)(2,1)} %copy.16, bf16[128,1,4096]{2,0,1:T(8,128)(2,1)} %fusion.11), kind=kOutput, calls=%fused_computation.55 | convolution fusion | flops 134217728 | bytes 5234688 | tf_op jit(solution)/shard_map/conv_general_dilated | solution.py:252
  79.5 5.6 %copy.18 = f32[1,128,4096]{1,2,0:T(8,128)} copy(f32[1,128,4096]{2,0,1:T(1,128)} %fusion.28) | data formatting | bytes 4194304 | tf_op jit(solution)/shard_map/conv_general_dilated | solution.py:252
  85.2 2.8 fusion.31
  89.9 58.8 %shard_map.103 = bf16[2,64,8192]{2,1,0:T(8,128)(2,1)} custom-call(bf16[2,4096,128]{2,1,0:T(8,128)(2,1)} %pad_maximum_fusion.x_ref), custom_call_target="tpu_custom_call" | custom-call | tf_op jit(solution)/shard_map/pallas_call | solution.py:137
  155.8 7.6 %multiply_subtract_fusion.3 = (f32[64,1,128,128]{2,3,1,0:T(8,128)}, f32[64,1,128,128]{2,3,1,0:T(8,128)}, f32[64,1,128,128]{2,3,1,0:T(8,128)}, f32[64,1,128,128]{2,3,1,0:T(8,128)}) fusion(f32[64,2,128,128]{2,3,1,0:T(8,128)S(1)} %convolution_bitcast_fusion, f32[128,128]{0,1:T(8,128)S(1)} %get-tuple-element.32, f32[128,128]{0,1:T(8,128)S(1)} %get-tuple-element.33, ...), kind=kLoop, calls=%fused_computation.25 | loop fusion | flops 12582912 | bytes 33685504 | tf_op jit(solution)/shard_map/sub | solution.py:221
  163.4 6.8 %fusion.16 = f32[64,2,128,128]{2,3,0,1:T(8,128)S(1)} fusion(f32[64,1,128,128]{2,3,1,0:T(8,128)} %get-tuple-element.11, f32[64,1,128,128]{2,3,1,0:T(8,128)} %get-tuple-element.10, f32[1,2,128,128]{2,3,0,1:T(8,128)S(1)} %get-tuple-element.19, f32[1,2,128,128]{2,3,0,1:T(8,128)S(1)} %get-tuple-element.24), kind=kOutput, calls=%fused_computation.29 | convolution fusion | flops 3223388160 | bytes 17039360 | tf_op jit(solution)/shard_map/nqcb,qpbd->npcd/dot_general | solution.py:199
  170.2 4.9 %fusion.15 = f32[64,2,128,128]{2,3,0,1:T(8,128)S(1)} fusion(f32[64,1,128,128]{2,3,1,0:T(8,128)S(1)} %copy-done.3, f32[64,1,128,128]{2,3,1,0:T(8,128)S(1)} %copy-done.4, f32[1,2,128,128]{2,3,0,1:T(8,128)S(1)} %get-tuple-element.19, f32[1,2,128,128]{2,3,0,1:T(8,128)S(1)} %get-tuple-element.24), kind=kOutput, calls=%fused_computation.28 | convolution fusion | flops 3223388160 | bytes 17039360 | tf_op jit(solution)/shard_map/nqcb,qpbd->npcd/dot_general | solution.py:199
  175.2 2.7 multiply_add_fusion.1
  177.9 5.0 %fusion.12 = f32[64,2,128,128]{2,3,1,0:T(8,128)S(1)} fusion(f32[64,1,128,128]{2,3,0,1:T(8,128)S(1)} %get-tuple-element.7, f32[64,1,128,128]{2,3,0,1:T(8,128)S(1)} %get-tuple-element.6, f32[1,2,128,128]{2,3,1,0:T(8,128)S(1)} %copy-done.21, f32[1,2,128,128]{2,3,1,0:T(8,128)S(1)} %copy-done.20), kind=kOutput, calls=%fused_computation.26 | convolution fusion | flops 3223388160 | bytes 17039360 | tf_op jit(solution)/shard_map/npcd,pqdb->nqcb/dot_general | solution.py:199
  184.9 4.4 %fusion.30 = bf16[64,2,64,128]{3,2,1,0:T(8,128)(2,1)S(1)} fusion(f32[64,1,128,128]{2,3,1,0:T(8,128)S(1)} %get-tuple-element.9, f32[64,1,128,128]{2,3,1,0:T(8,128)S(1)} %get-tuple-element.8, f32[1,2,64,128]{3,2,1,0:T(8,128)S(1)} %copy-done.18, f32[1,2,64,128]{3,2,1,0:T(8,128)S(1)} %copy-done.17), kind=kOutput, calls=%fused_computation.57 | convolution fusion | flops 1613791232 | bytes 10616832 | tf_op jit(solution)/shard_map/rqac,nqcb->nrab/dot_general | solution.py:199
  192.2 37.7 %shard_map.104 = bf16[4096,128]{1,0:T(8,128)(2,1)} custom-call(bf16[64,8192]{1,0:T(8,128)(2,1)} %bitcast.198), custom_call_target="tpu_custom_call" | custom-call | tf_op jit(solution)/shard_map/pallas_call | solution.py:137
  229.9 3.1 fusion.19
  233.0 4.7 %copy.34 = bf16[128,1,4096]{2,1,0:T(2,128)(2,1)S(1)} copy(bf16[128,1,4096]{0,2,1:T(8,128)(2,1)} %bitcast.194) | data formatting | bytes 2097152 | tf_op jit(solution)/shard_map/broadcast_in_dim | solution.py:312
  239.7 31.8 %fusion.90 = f32[1,4096,128]{1,0,2:T(1,128)} fusion(bf16[1,255,4096]{2,0,1:T(2,128)(2,1)} %copy.16, bf16[128,1,4096]{2,1,0:T(2,128)(2,1)S(1)} %copy.34), kind=kOutput, calls=%fused_computation.149 | convolution fusion | flops 134217728 | bytes 5234688 | tf_op jit(solution)/shard_map/conv_general_dilated | solution.py:310
  271.5 5.8 %copy.35 = f32[1,4096,128]{2,1,0:T(8,128)} copy(f32[1,4096,128]{1,0,2:T(1,128)} %fusion.90) | data formatting | bytes 4194304 | tf_op jit(solution)/shard_map/conv_general_dilated | solution.py:310
  277.3 33.2 %shard_map.105 = bf16[64,128]{1,0:T(8,128)(2,1)} custom-call(f32[8,4,2,64,128]{4,3,2,1,0:T(8,128)} %bitcast.196), custom_call_target="tpu_custom_call" | custom-call | tf_op jit(solution)/shard_map/pallas_call | solution.py:78
  313.1 3.0 maximum_bitcast_fusion.16
  316.1 10.0 %copy.30 = bf16[1,255,4096]{2,0,1:T(2,128)(2,1)} copy(bf16[1,255,4096]{1,2,0:T(8,128)(2,1)} %maximum_bitcast_fusion.16) | data formatting | bytes 4177920 | tf_op jit(solution)/shard_map/broadcast_in_dim | solution.py:253
  326.1 34.3 %fusion.26 = f32[1,128,4096]{2,0,1:T(1,128)} fusion(bf16[1,255,4096]{2,0,1:T(2,128)(2,1)} %copy.30, bf16[128,1,4096]{2,0,1:T(8,128)(2,1)S(1)} %bitcast.193), kind=kOutput, calls=%fused_computation.53 | convolution fusion | flops 134217728 | bytes 5234688 | tf_op jit(solution)/shard_map/conv_general_dilated | solution.py:252
  360.4 5.8 %copy.32 = f32[1,128,4096]{1,2,0:T(8,128)} copy(f32[1,128,4096]{2,0,1:T(1,128)} %fusion.26) | data formatting | bytes 4194304 | tf_op jit(solution)/shard_map/conv_general_dilated | solution.py:252
  366.2 3.7 %fusion.32 = bf16[1,128,4096]{1,2,0:T(8,128)(2,1)} fusion(f32[1,128,4096]{1,2,0:T(8,128)} %copy.32, bf16[4096,128]{1,0:T(8,128)(2,1)} %shard_map.104, bf16[128,4096]{0,1:T(8,128)(2,1)S(1)} %copy-done.6, bf16[1,128,4096]{1,2,0:T(8,128)(2,1)S(1)} %copy-done.2, bf16[1,128,4096]{1,2,0:T(8,128)(2,1)} %copy-done.7), kind=kLoop, calls=%fused_computation.59 | loop fusion | flops 4718592 | bytes 7340032 | tf_op jit(solution)/shard_map/broadcast_in_dim | solution.py:309
  (85 shorter events, 47.0 us)
Async XLA Ops:
  0.6 29.7 %copy-start = (bf16[1,128,4096]{2,1,0:T(8,128)(2,1)S(1)}, bf16[1,128,4096]{2,1,0:T(8,128)(2,1)}, u32[]{:S(2)}) copy-start(bf16[1,128,4096]{2,1,0:T(8,128)(2,1)} %param.15) | copy-start | bytes 3145732
  2.4 11.4 %copy-start.9 = (bf16[1,128,4096]{1,2,0:T(8,128)(2,1)}, bf16[1,128,4096]{1,2,0:T(8,128)(2,1)S(1)}, u32[]{:S(2)}) copy-start(bf16[1,128,4096]{1,2,0:T(8,128)(2,1)S(1)} %copy.14) | copy-start | bytes 3145732
  4.4 9.4 %copy-start.7 = (bf16[1,128,4096]{1,2,0:T(8,128)(2,1)}, bf16[1,128,4096]{1,2,0:T(8,128)(2,1)S(1)}, u32[]{:S(2)}) copy-start(bf16[1,128,4096]{1,2,0:T(8,128)(2,1)S(1)} %copy.15) | copy-start | bytes 3145732
  7.0 24.7 %collective-permute-start.1 = (bf16[127,4096]{0,1:T(8,128)(2,1)}, bf16[127,4096]{0,1:T(8,128)(2,1)}, u32[]{:S(2)}, u32[]{:S(2)}) collective-permute-start(bf16[127,4096]{0,1:T(8,128)(2,1)} %slice.62), channel_id=1, source_target_pairs={{0,1},{1,2},{2,3},{3,4},{4,5},{5,6},{6,7},{7,8},{8,9},{9,10},{10,1... | collective-permute-start | bytes 3121160 | tf_op jit(solution)/shard_map/ppermute | solution.py:188
  13.8 74.2 %collective-permute-start = (bf16[128,4096]{0,1:T(8,128)(2,1)}, bf16[128,4096]{0,1:T(8,128)(2,1)S(1)}, u32[]{:S(2)}, u32[]{:S(2)}) collective-permute-start(bf16[128,4096]{0,1:T(8,128)(2,1)} %bitcast.202), channel_id=1, source_target_pairs={{0,192},{64,0},{128,64},{192,128},{1,193},{65,1},{129,65},{193,129... | collective-permute-start | bytes 3145736 | tf_op jit(solution)/shard_map/ppermute | solution.py:182
  19.3 210.6 %copy-start.1 = (bf16[1,128,4096]{1,2,0:T(8,128)(2,1)}, bf16[1,128,4096]{1,2,0:T(8,128)(2,1)S(1)}, u32[]{:S(2)}) copy-start(bf16[1,128,4096]{1,2,0:T(8,128)(2,1)S(1)} %copy.20) | copy-start | bytes 3145732
  24.3 6.0 %copy-start.19 = (bf16[128,128]{1,0:T(8,128)(2,1)S(1)}, bf16[128,128]{1,0:T(8,128)(2,1)}, u32[]{:S(2)}) copy-start(bf16[128,128]{1,0:T(8,128)(2,1)} %rev.6) | copy-start | bytes 98308
  24.3 7.4 %copy-start.11 = (bf16[128,4096]{0,1:T(8,128)(2,1)S(1)}, bf16[128,4096]{0,1:T(8,128)(2,1)}, u32[]{:S(2)}) copy-start(bf16[128,4096]{0,1:T(8,128)(2,1)} %copy-done.10) | copy-start | bytes 3145732
  85.2 2.8 copy-start.12
  88.0 141.9 %copy-start.5 = (bf16[128,4096]{0,1:T(8,128)(2,1)}, bf16[128,4096]{0,1:T(8,128)(2,1)S(1)}, u32[]{:S(2)}) copy-start(bf16[128,4096]{0,1:T(8,128)(2,1)S(1)} %collective-permute-done) | copy-start | bytes 3145732
  148.7 2.3 copy-start.15
  148.7 2.3 copy-start.16
  151.0 2.4 copy-start.14
  163.4 6.8 %copy-start.3 = (f32[64,1,128,128]{2,3,1,0:T(8,128)S(1)}, f32[64,1,128,128]{2,3,1,0:T(8,128)}, u32[]{:S(2)}) copy-start(f32[64,1,128,128]{2,3,1,0:T(8,128)} %get-tuple-element.22) | copy-start | bytes 12582916
  163.4 6.8 %copy-start.4 = (f32[64,1,128,128]{2,3,1,0:T(8,128)S(1)}, f32[64,1,128,128]{2,3,1,0:T(8,128)}, u32[]{:S(2)}) copy-start(f32[64,1,128,128]{2,3,1,0:T(8,128)} %get-tuple-element.23) | copy-start | bytes 12582916
  175.1 2.8 copy-start.20
  175.2 2.8 copy-start.21
  182.9 1.9 copy-start.17
  182.9 1.9 copy-start.18
  237.8 75.3 %collective-permute-start.2 = (bf16[127,4096]{0,1:T(8,128)(2,1)}, bf16[127,4096]{0,1:T(8,128)(2,1)}, u32[]{:S(2)}, u32[]{:S(2)}) collective-permute-start(bf16[127,4096]{0,1:T(8,128)(2,1)} %bitcast.195), channel_id=1, source_target_pairs={{1,0},{2,1},{3,2},{4,3},{5,4},{6,5},{7,6},{8,7},{9,8},{10,9},{11,1... | collective-permute-start | bytes 3121160 | tf_op jit(solution)/shard_map/ppermute | solution.py:188
  271.5 40.4 %copy-start.13 = (bf16[64,1,64,128]{3,2,1,0:T(8,128)(2,1)S(1)}, bf16[64,1,64,128]{3,2,1,0:T(8,128)(2,1)}, u32[]{:S(2)}) copy-start(bf16[64,1,64,128]{3,2,1,0:T(8,128)(2,1)} %get-tuple-element.14) | copy-start | bytes 3145732
  271.5 41.6 %copy-start.8 = (bf16[128,4096]{0,1:T(8,128)(2,1)S(1)}, bf16[128,4096]{0,1:T(8,128)(2,1)}, u32[]{:S(2)}) copy-start(bf16[128,4096]{0,1:T(8,128)(2,1)} %fusion.19) | copy-start | bytes 3145732
  360.4 5.8 %copy-start.2 = (bf16[1,128,4096]{1,2,0:T(8,128)(2,1)S(1)}, bf16[1,128,4096]{1,2,0:T(8,128)(2,1)}, u32[]{:S(2)}) copy-start(bf16[1,128,4096]{1,2,0:T(8,128)(2,1)} %copy-done.1) | copy-start | bytes 3145732
  360.4 5.8 %copy-start.6 = (bf16[128,4096]{0,1:T(8,128)(2,1)S(1)}, bf16[128,4096]{0,1:T(8,128)(2,1)}, u32[]{:S(2)}) copy-start(bf16[128,4096]{0,1:T(8,128)(2,1)} %copy-done.5) | copy-start | bytes 3145732
  (1 other events, 1.0 us)

commit v3 on v2

--- a/solution.py
+++ b/solution.py
@@ -92,7 +92,12 @@
     )(parts)
 
 
-def exchange_kernel(n, send_part, recv_part, x_ref, o_ref, local_sem, send_sems, recv_sems):
+def exchange_kernel(n, send_part, recv_part, x_ref, o_ref, local_sem, send_sems, recv_sems, *staged):
+    if staged:
+        (stage,) = staged
+        for index in range(x_ref.shape[0]):
+            stage[index] = x_ref[index].astype(jnp.float32).T.astype(stage.dtype)
+        x_ref = stage
     me = lax.axis_index("ctx")
     sec = lax.axis_index("section")
     barrier = pltpu.get_barrier_semaphore()
@@ -132,7 +137,7 @@
     own.wait()
 
 
-def exchange(x, out_shape, send_part, recv_part, collective):
+def exchange(x, out_shape, send_part, recv_part, collective, staged=()):
     n = lax.axis_size("ctx")
     return pl.pallas_call(
         functools.partial(exchange_kernel, n, send_part, recv_part),
@@ -143,6 +148,7 @@
             pltpu.SemaphoreType.DMA(()),
             pltpu.SemaphoreType.DMA((n,)),
             pltpu.SemaphoreType.DMA((n,)),
+            *staged,
         ],
         compiler_params=pltpu.CompilerParams(collective_id=collective, has_side_effects=True),
     )(x)
@@ -150,7 +156,7 @@
 
 def to_channels(x):
     n = lax.axis_size("ctx")
-    count, channels, tokens = x.shape
+    count, tokens, channels = x.shape
     rows = channels // n
 
     def send_part(ref, peer):
@@ -159,7 +165,8 @@
     def recv_part(ref, source):
         return ref.at[:, :, pl.ds(pl.multiple_of(source * tokens, tokens), tokens)]
 
-    return exchange(x, (count, rows, tokens * n), send_part, recv_part, 1)
+    stage = pltpu.VMEM((count, channels, tokens), x.dtype)
+    return exchange(x, (count, rows, tokens * n), send_part, recv_part, 1, (stage,))
 
 
 def to_positions(x):
@@ -286,7 +293,7 @@
     resid = inputs + beta * branch * gate_mid
     long_in = (resid * gate_long).astype(jnp.bfloat16)
     grad_z = (beta * adjoint * gate_out).astype(jnp.bfloat16)
-    channel_z, channel_w = to_channels(jnp.stack([grad_z.T, long_in.T]))
+    channel_z, channel_w = to_channels(jnp.stack([grad_z, long_in]))
     factor_b = math.gcd(seq_len, 128)
     factor_a = 2 * seq_len // factor_b
     zspec = to_spectrum(channel_z[:, None], factor_a, factor_b)
@@ -301,7 +308,9 @@
         jnp.stack([joint_re, joint_im], 1), factor_a, factor_b, scale
     )
     long_grad = lag_grad.astype(jnp.bfloat16)[None]
-    returned = to_positions(input_part.astype(jnp.bfloat16)).T
+    returned = lax.all_to_all(
+        input_part.astype(jnp.bfloat16), "ctx", split_axis=1, concat_axis=0, tiled=True
+    ).T
     grad_u = adjoint + returned.astype(jnp.float32) * gate_long
     grad_b = (beta * grad_u * gate_mid).astype(jnp.bfloat16)
     later = shifted(grad_b[:reach], "ctx", -1)

time: 377 us -> 317 us (0.84)
  local copies, waits for them, and re-layouts: 69.2 us -> 17.5 us
  Pallas kernels: 130 us -> 92.7 us
  waiting for transfers between devices: 0.01 us -> 28.8 us
  starting transfers between devices: 9.16 us -> 22.7 us
  matrix products: 128 us -> 116 us
    pallas_call x2 -> x1, Pallas kernels: 96.5 us -> 62.6 us  [exchange(): pl.pallas_call(functools.partial(exchange_kernel, n, send_part, recv_part...]
    all_to_all x0 -> x1, waiting for transfers between devices: none -> 26.7 us  [per_device(): lax.all_to_all(input_part.astype(jnp.bfloat16), 'ctx', split_axis=1, conc...]
    broadcast_in_dim x3 -> x0, local copies, waits for them, and re-layouts: 24.8 us -> none  [the longest x2 20 us: depthwise(): extended[None]]
    unnamed x56 -> x50, local copies, waits for them, and re-layouts: 21.4 us -> 3.63 us
    all_to_all x0 -> x1, starting transfers between devices: none -> 12.1 us  [per_device(): lax.all_to_all(input_part.astype(jnp.bfloat16), 'ctx', split_axis=1, conc...]
    conv_general_dilated x2 -> x0, local copies, waits for them, and re-layouts: 11.4 us -> none  [depthwise(): lax.conv_general_dilated(extended[None], kernel[:, None, :], (1,), 'VALID...]
    conv_general_dilated x2, matrix products: 68.6 us -> 60.5 us  [depthwise(): lax.conv_general_dilated(extended[None], kernel[:, None, :], (1,), 'VALID...]
  transfers between devices with their start and end apart: 3 -> 4, of which waited for: 0 -> 2; matrix products, arithmetic and copies ran while one was open for 31% -> 25% of each run, Pallas kernels for 9% -> 10%
where the time goes in v3:
time: 317 us; the launch traced here: 313 us
  matrix products  116 us (37%)
  Pallas kernels  92.7 us (29%)
  other arithmetic  33.6 us (11%)
  waiting for transfers between devices  28.8 us (9%)
  starting transfers between devices  22.7 us (7%)
  local copies, waits for them, and re-layouts  17.5 us (6%)
    pallas_call x1, Pallas kernels, exchange(): pl.pallas_call(functools.partial(exchange_kernel, n, send_part, recv_part...  62.6 us
    conv_general_dilated x2, matrix products, depthwise(): lax.conv_general_dilated(extended[None], kernel[:, None, :], (1,), 'VALID...  60.5 us
    pallas_call x1, Pallas kernels, tap_exchange(): pl.pallas_call(functools.partial(tap_exchange_kernel, nz, nx, nc, scale),...  30.1 us
    conv_general_dilated x1, matrix products, per_device(): lax.conv_general_dilated(extended[None], grad_b[:, None, :], (1,), 'VALID...  29.1 us
    all_to_all x1, waiting for transfers between devices, per_device(): lax.all_to_all(input_part.astype(jnp.bfloat16), 'ctx', split_axis=1, conc...  26.7 us
    dot_general x6, matrix products, contract(): jnp.einsum(form, left, right, precision=lax.Precision.HIGH, preferred_ele...  26.2 us
    all_to_all x1, starting transfers between devices, per_device(): lax.all_to_all(input_part.astype(jnp.bfloat16), 'ctx', split_axis=1, conc...  12.1 us
    ppermute x2, starting transfers between devices, shifted(): return lax.ppermute(array, axis, pairs)  7.75 us
  transfers between devices with their start and end apart: 4, of which 2 were waited for; matrix products, arithmetic and copies ran while one was open for 25% of the time, Pallas kernels for 10%

profile of v3, /device:TPU:1, one launch (start us, length us, event | category | flops | bytes accessed | tf_op | source)
XLA Modules:
  0.0 312.9 jit_solution(277915437278602303)
XLA Ops:
  3.8 4.5 %collective-permute-start.1 = (bf16[127,4096]{1,0:T(8,128)(2,1)}, bf16[127,4096]{1,0:T(8,128)(2,1)}, u32[]{:S(2)}, u32[]{:S(2)}) collective-permute-start(bf16[127,4096]{1,0:T(8,128)(2,1)} %slice_bitcast_fusion.1), channel_id=1, source_target_pairs={{0,1},{1,2},{2,3},{3,4},{4,5},{5,6},{6,7},{7,8},{8,9},{9,10},{10,1... | collective-permute-start | bytes 3121160 | tf_op jit(solution)/shard_map/ppermute | solution.py:195
  8.3 2.8 collective-permute-start
  18.2 2.1 collective-permute-done.1
  21.9 30.4 %fusion.16 = f32[1,128,4096]{2,0,1:T(1,128)S(1)} fusion(bf16[1,255,4096]{2,1,0:T(8,128)(2,1)S(1)} %maximum_bitcast_fusion.13, bf16[128,1,4096]{2,0,1:T(8,128)(2,1)S(1)} %fusion.11), kind=kOutput, calls=%fused_computation.30 | convolution fusion | flops 134217728 | bytes 5234688 | tf_op jit(solution)/shard_map/conv_general_dilated | solution.py:259
  52.4 2.1 fusion.31
  56.4 62.6 %shard_map.103 = bf16[2,64,8192]{2,1,0:T(8,128)(2,1)} custom-call(bf16[2,128,4096]{2,1,0:T(8,128)(2,1)} %pad_maximum_fusion.x_ref), custom_call_target="tpu_custom_call" | custom-call | tf_op jit(solution)/shard_map/pallas_call | solution.py:142
  121.3 2.4 convolution_bitcast_fusion
  123.8 2.4 convolution_bitcast_fusion.1
  126.1 6.3 %multiply_subtract_fusion.3 = (f32[64,1,128,128]{2,3,1,0:T(8,128)S(1)}, f32[64,1,128,128]{2,3,1,0:T(8,128)}, f32[64,1,128,128]{2,3,1,0:T(8,128)}, f32[64,1,128,128]{2,3,1,0:T(8,128)}) fusion(f32[64,2,128,128]{2,3,1,0:T(8,128)S(1)} %convolution_bitcast_fusion, f32[128,128]{0,1:T(8,128)S(1)} %get-tuple-element.29, f32[128,128]{0,1:T(8,128)S(1)} %get-tuple-element.30, ...), kind=kLoop, calls=%fused_computation.25 | loop fusion | flops 12582912 | bytes 33685504 | tf_op jit(solution)/shard_map/sub | solution.py:228
  132.5 7.1 %fusion.22 = f32[64,2,128,128]{2,3,0,1:T(8,128)S(1)} fusion(f32[64,1,128,128]{2,3,1,0:T(8,128)} %get-tuple-element.8, f32[64,1,128,128]{2,3,1,0:T(8,128)S(1)} %get-tuple-element.7, f32[1,2,128,128]{2,3,0,1:T(8,128)S(1)} %get-tuple-element.16, f32[1,2,128,128]{2,3,0,1:T(8,128)S(1)} %get-tuple-element.21), kind=kOutput, calls=%fused_computation.35 | convolution fusion | flops 3223388160 | bytes 17039360 | tf_op jit(solution)/shard_map/nqcb,qpbd->npcd/dot_general | solution.py:206
  139.6 4.9 %fusion.21 = f32[64,2,128,128]{2,3,0,1:T(8,128)S(1)} fusion(f32[64,1,128,128]{2,3,1,0:T(8,128)S(1)} %copy-done.3, f32[64,1,128,128]{2,3,1,0:T(8,128)S(1)} %copy-done.4, f32[1,2,128,128]{2,3,0,1:T(8,128)S(1)} %get-tuple-element.16, f32[1,2,128,128]{2,3,0,1:T(8,128)S(1)} %get-tuple-element.21), kind=kOutput, calls=%fused_computation.34 | convolution fusion | flops 3223388160 | bytes 17039360 | tf_op jit(solution)/shard_map/nqcb,qpbd->npcd/dot_general | solution.py:206
  144.5 2.7 multiply_add_fusion.1
  147.3 5.0 %fusion.18 = f32[64,2,128,128]{2,3,1,0:T(8,128)S(1)} fusion(f32[64,1,128,128]{2,3,0,1:T(8,128)S(1)} %get-tuple-element.4, f32[64,1,128,128]{2,3,0,1:T(8,128)S(1)} %get-tuple-element.3, f32[1,2,128,128]{2,3,1,0:T(8,128)S(1)} %copy-done.22, f32[1,2,128,128]{2,3,1,0:T(8,128)S(1)} %copy-done.21), kind=kOutput, calls=%fused_computation.32 | convolution fusion | flops 3223388160 | bytes 17039360 | tf_op jit(solution)/shard_map/npcd,pqdb->nqcb/dot_general | solution.py:206
  154.2 4.4 %fusion.38 = bf16[64,2,64,128]{3,2,1,0:T(8,128)(2,1)S(1)} fusion(f32[64,1,128,128]{2,3,1,0:T(8,128)S(1)} %get-tuple-element.6, f32[64,1,128,128]{2,3,1,0:T(8,128)S(1)} %get-tuple-element.5, f32[1,2,64,128]{3,2,1,0:T(8,128)S(1)} %copy-done.19, f32[1,2,64,128]{3,2,1,0:T(8,128)S(1)} %copy-done.18), kind=kOutput, calls=%fused_computation.66 | convolution fusion | flops 1613791232 | bytes 10616832 | tf_op jit(solution)/shard_map/rqac,nqcb->nrab/dot_general | solution.py:206
  160.5 12.1 %all-to-all-start = ((bf16[64,64,128]{2,0,1:T(8,128)(2,1)}), bf16[64,64,128]{2,0,1:T(8,128)(2,1)S(1)}, u32[]{:S(2)}, u32[]{:S(2)}) async-start(bf16[64,64,128]{2,0,1:T(8,128)(2,1)} %copy.65), calls=%async_computation | async-start | bytes 2097152 | tf_op jit(solution)/shard_map/all_to_all | solution.py:311
  173.9 26.7 %all-to-all-done = bf16[64,64,128]{2,0,1:T(8,128)(2,1)S(1)} async-done(((bf16[64,64,128]{2,0,1:T(8,128)(2,1)}), bf16[64,64,128]{2,0,1:T(8,128)(2,1)S(1)}, u32[]{:S(2)}, u32[]{:S(2)}) %all-to-all-start) | async-done | bytes 1048608 | tf_op jit(solution)/shard_map/all_to_all | solution.py:311
  202.3 1.9 copy.66
  204.2 4.2 %fusion.30 = bf16[128,4096]{1,0:T(8,128)(2,1)} fusion(bf16[1,128,4096]{2,1,0:T(8,128)(2,1)} %param.11, bf16[1,128,4096]{2,1,0:T(8,128)(2,1)} %param.12, f32[4096,128]{0,1:T(8,128)S(1)} %copy.66, bf16[128,4096]{1,0:T(8,128)(2,1)} %copy-done.5), kind=kLoop, calls=%fused_computation.53 | loop fusion | flops 4194304 | bytes 6291456 | tf_op jit(solution)/shard_map/convert_element_type | solution.py:315
  208.4 3.3 %collective-permute-start.2 = (bf16[127,4096]{1,0:T(8,128)(2,1)}, bf16[127,4096]{1,0:T(8,128)(2,1)}, u32[]{:S(2)}, u32[]{:S(2)}) collective-permute-start(bf16[127,4096]{1,0:T(8,128)(2,1)} %bitcast.182), channel_id=1, source_target_pairs={{1,0},{2,1},{3,2},{4,3},{5,4},{6,5},{7,6},{8,7},{9,8},{10,9},{11,1... | collective-permute-start | bytes 3121160 | tf_op jit(solution)/shard_map/ppermute | solution.py:195
  211.7 29.1 %fusion.14 = f32[1,4096,128]{1,0,2:T(1,128)} fusion(bf16[1,255,4096]{2,1,0:T(8,128)(2,1)S(1)} %copy-done.14, bf16[128,1,4096]{2,0,1:T(8,128)(2,1)} %bitcast.64), kind=kOutput, calls=%fused_computation.28 | convolution fusion | flops 134217728 | bytes 5234688 | tf_op jit(solution)/shard_map/conv_general_dilated | solution.py:319
  240.7 5.6 %copy.72 = f32[1,4096,128]{2,1,0:T(8,128)} copy(f32[1,4096,128]{1,0,2:T(1,128)} %fusion.14) | data formatting | bytes 4194304 | tf_op jit(solution)/shard_map/conv_general_dilated | solution.py:319
  246.4 30.1 %shard_map.104 = bf16[64,128]{1,0:T(8,128)(2,1)} custom-call(f32[8,4,2,64,128]{4,3,2,1,0:T(8,128)} %bitcast.186), custom_call_target="tpu_custom_call" | custom-call | tf_op jit(solution)/shard_map/pallas_call | solution.py:78
  279.7 30.1 %fusion.12 = f32[1,128,4096]{2,0,1:T(1,128)S(1)} fusion(bf16[1,255,4096]{2,1,0:T(8,128)(2,1)S(1)} %maximum_bitcast_fusion.16, bf16[128,1,4096]{2,0,1:T(8,128)(2,1)S(1)} %bitcast.183), kind=kOutput, calls=%fused_computation.26 | convolution fusion | flops 134217728 | bytes 5234688 | tf_op jit(solution)/shard_map/conv_general_dilated | solution.py:259
  309.9 2.8 fusion.39
  (78 shorter events, 25.8 us)
Async XLA Ops:
  0.6 17.2 %copy-start = (bf16[1,128,4096]{2,1,0:T(8,128)(2,1)S(1)}, bf16[1,128,4096]{2,1,0:T(8,128)(2,1)}, u32[]{:S(2)}) copy-start(bf16[1,128,4096]{2,1,0:T(8,128)(2,1)} %param.15) | copy-start | bytes 3145732
  3.8 16.5 %collective-permute-start.1 = (bf16[127,4096]{1,0:T(8,128)(2,1)}, bf16[127,4096]{1,0:T(8,128)(2,1)}, u32[]{:S(2)}, u32[]{:S(2)}) collective-permute-start(bf16[127,4096]{1,0:T(8,128)(2,1)} %slice_bitcast_fusion.1), channel_id=1, source_target_pairs={{0,1},{1,2},{2,3},{3,4},{4,5},{5,6},{6,7},{7,8},{8,9},{9,10},{10,1... | collective-permute-start | bytes 3121160 | tf_op jit(solution)/shard_map/ppermute | solution.py:195
  8.3 46.2 %collective-permute-start = (bf16[128,4096]{1,0:T(8,128)(2,1)}, bf16[128,4096]{1,0:T(8,128)(2,1)S(1)}, u32[]{:S(2)}, u32[]{:S(2)}) collective-permute-start(bf16[128,4096]{1,0:T(8,128)(2,1)} %bitcast), channel_id=1, source_target_pairs={{0,192},{64,0},{128,64},{192,128},{1,193},{65,1},{129,65},{193,129... | collective-permute-start | bytes 3145736 | tf_op jit(solution)/shard_map/ppermute | solution.py:189
  12.0 5.8 %copy-start.20 = (bf16[128,128]{1,0:T(8,128)(2,1)S(1)}, bf16[128,128]{1,0:T(8,128)(2,1)}, u32[]{:S(2)}) copy-start(bf16[128,128]{1,0:T(8,128)(2,1)} %rev.6) | copy-start | bytes 98308
  21.8 30.5 %copy-start.13 = (bf16[1,255,4096]{2,1,0:T(8,128)(2,1)}, bf16[1,255,4096]{2,1,0:T(8,128)(2,1)S(1)}, u32[]{:S(2)}) copy-start(bf16[1,255,4096]{2,1,0:T(8,128)(2,1)S(1)} %maximum_bitcast_fusion.13) | copy-start | bytes 6266884
  21.9 30.5 %copy-start.7 = (bf16[1,128,4096]{2,1,0:T(8,128)(2,1)S(1)}, bf16[1,128,4096]{2,1,0:T(8,128)(2,1)}, u32[]{:S(2)}) copy-start(bf16[1,128,4096]{2,1,0:T(8,128)(2,1)} %param.12) | copy-start | bytes 3145732
  21.9 30.5 %copy-start.9 = (bf16[1,128,4096]{2,1,0:T(8,128)(2,1)S(1)}, bf16[1,128,4096]{2,1,0:T(8,128)(2,1)}, u32[]{:S(2)}) copy-start(bf16[1,128,4096]{2,1,0:T(8,128)(2,1)} %param.9) | copy-start | bytes 3145732
  21.9 30.5 %copy-start.10 = (bf16[1,128,4096]{2,1,0:T(8,128)(2,1)S(1)}, bf16[1,128,4096]{2,1,0:T(8,128)(2,1)}, u32[]{:S(2)}) copy-start(bf16[1,128,4096]{2,1,0:T(8,128)(2,1)} %param.11) | copy-start | bytes 3145732
  54.5 64.5 %copy-start.5 = (bf16[128,4096]{1,0:T(8,128)(2,1)}, bf16[128,4096]{1,0:T(8,128)(2,1)S(1)}, u32[]{:S(2)}) copy-start(bf16[128,4096]{1,0:T(8,128)(2,1)S(1)} %collective-permute-done) | copy-start | bytes 3145732
  119.0 2.3 copy-start.16
  119.0 2.3 copy-start.17
  121.3 2.4 copy-start.12
  132.5 7.1 %copy-start.3 = (f32[64,1,128,128]{2,3,1,0:T(8,128)S(1)}, f32[64,1,128,128]{2,3,1,0:T(8,128)}, u32[]{:S(2)}) copy-start(f32[64,1,128,128]{2,3,1,0:T(8,128)} %get-tuple-element.19) | copy-start | bytes 12582916
  132.5 7.1 %copy-start.4 = (f32[64,1,128,128]{2,3,1,0:T(8,128)S(1)}, f32[64,1,128,128]{2,3,1,0:T(8,128)}, u32[]{:S(2)}) copy-start(f32[64,1,128,128]{2,3,1,0:T(8,128)} %get-tuple-element.20) | copy-start | bytes 12582916
  144.5 2.8 copy-start.21
  144.5 2.8 copy-start.22
  160.5 40.1 %all-to-all-start = ((bf16[64,64,128]{2,0,1:T(8,128)(2,1)}), bf16[64,64,128]{2,0,1:T(8,128)(2,1)S(1)}, u32[]{:S(2)}, u32[]{:S(2)}) async-start(bf16[64,64,128]{2,0,1:T(8,128)(2,1)} %copy.65), calls=%async_computation | async-start | bytes 2097152 | tf_op jit(solution)/shard_map/all_to_all | solution.py:311
  204.2 36.5 %copy-start.1 = (f32[4096,128]{0,1:T(8,128)}, f32[4096,128]{0,1:T(8,128)S(1)}, u32[]{:S(2)}) copy-start(f32[4096,128]{0,1:T(8,128)S(1)} %copy.66) | copy-start | bytes 6291460
  204.2 7.5 %copy-start.14 = (bf16[1,255,4096]{2,1,0:T(8,128)(2,1)S(1)}, bf16[1,255,4096]{2,1,0:T(8,128)(2,1)}, u32[]{:S(2)}) copy-start(bf16[1,255,4096]{2,1,0:T(8,128)(2,1)} %copy-done.13) | copy-start | bytes 6266884
  208.4 69.5 %collective-permute-start.2 = (bf16[127,4096]{1,0:T(8,128)(2,1)}, bf16[127,4096]{1,0:T(8,128)(2,1)}, u32[]{:S(2)}, u32[]{:S(2)}) collective-permute-start(bf16[127,4096]{1,0:T(8,128)(2,1)} %bitcast.182), channel_id=1, source_target_pairs={{1,0},{2,1},{3,2},{4,3},{5,4},{6,5},{7,6},{8,7},{9,8},{10,9},{11,1... | collective-permute-start | bytes 3121160 | tf_op jit(solution)/shard_map/ppermute | solution.py:195
  279.7 30.2 %copy-start.2 = (f32[4096,128]{0,1:T(8,128)S(1)}, f32[4096,128]{0,1:T(8,128)}, u32[]{:S(2)}) copy-start(f32[4096,128]{0,1:T(8,128)} %copy-done.1) | copy-start | bytes 6291460
  279.7 30.2 %copy-start.6 = (bf16[128,4096]{1,0:T(8,128)(2,1)S(1)}, bf16[128,4096]{1,0:T(8,128)(2,1)}, u32[]{:S(2)}) copy-start(bf16[128,4096]{1,0:T(8,128)(2,1)} %copy-done.5) | copy-start | bytes 3145732
  279.7 30.2 %copy-start.8 = (bf16[1,128,4096]{2,1,0:T(8,128)(2,1)S(1)}, bf16[1,128,4096]{2,1,0:T(8,128)(2,1)}, u32[]{:S(2)}) copy-start(bf16[1,128,4096]{2,1,0:T(8,128)(2,1)} %param.12) | copy-start | bytes 3145732
  279.7 30.2 %copy-start.11 = (bf16[1,128,4096]{2,1,0:T(8,128)(2,1)S(1)}, bf16[1,128,4096]{2,1,0:T(8,128)(2,1)}, u32[]{:S(2)}) copy-start(bf16[1,128,4096]{2,1,0:T(8,128)(2,1)} %param.10) | copy-start | bytes 3145732
  (3 other events, 6.0 us)

commit v4 on v1

--- a/solution.py
+++ b/solution.py
@@ -90,6 +90,78 @@
         ],
         compiler_params=pltpu.CompilerParams(collective_id=0, has_side_effects=True),
     )(parts)
+
+
+def channel_kernel(n, x_ref, o_ref, stage, local_sems, send_sems, recv_sems):
+    count, channels, tokens = stage.shape
+    rows = channels // n
+    me = lax.axis_index("ctx")
+    sec = lax.axis_index("section")
+    barrier = pltpu.get_barrier_semaphore()
+
+    def greet(k, carry):
+        peer = lax.rem(me + k, n)
+        pl.semaphore_signal(barrier, inc=1, device_id=(sec, peer), device_id_type=MESH_IDS)
+        return carry
+
+    lax.fori_loop(1, n, greet, 0)
+    pl.semaphore_wait(barrier, n - 1)
+
+    def copy(index, peer, source):
+        return pltpu.make_async_remote_copy(
+            src_ref=stage.at[index, pl.ds(pl.multiple_of(peer * rows, rows), rows), :],
+            dst_ref=o_ref.at[index, :, pl.ds(pl.multiple_of(source * tokens, tokens), tokens)],
+            send_sem=send_sems.at[index, peer],
+            recv_sem=recv_sems.at[index, source],
+            device_id=(sec, peer),
+            device_id_type=MESH_IDS,
+        )
+
+    owns = []
+    for index in range(count):
+        stage[index] = x_ref[index].astype(jnp.float32).T.astype(stage.dtype)
+
+        def start(k, carry, index=index):
+            copy(index, lax.rem(me + k, n), me).start()
+            return carry
+
+        lax.fori_loop(1, n, start, 0)
+        own = pltpu.make_async_copy(
+            stage.at[index, pl.ds(pl.multiple_of(me * rows, rows), rows), :],
+            o_ref.at[index, :, pl.ds(pl.multiple_of(me * tokens, tokens), tokens)],
+            local_sems.at[index],
+        )
+        own.start()
+        owns.append(own)
+
+    for index in range(count):
+
+        def finish(k, carry, index=index):
+            source = lax.rem(me + n - k, n)
+            copy(index, source, source).wait_recv()
+            copy(index, lax.rem(me + k, n), me).wait_send()
+            return carry
+
+        lax.fori_loop(1, n, finish, 0)
+        owns[index].wait()
+
+
+def to_channels(x):
+    n = lax.axis_size("ctx")
+    count, tokens, channels = x.shape
+    return pl.pallas_call(
+        functools.partial(channel_kernel, n),
+        out_shape=jax.ShapeDtypeStruct((count, channels // n, tokens * n), x.dtype),
+        in_specs=[pl.BlockSpec(memory_space=pltpu.VMEM)],
+        out_specs=pl.BlockSpec(memory_space=pltpu.VMEM),
+        scratch_shapes=[
+            pltpu.VMEM((count, channels, tokens), x.dtype),
+            pltpu.SemaphoreType.DMA((count,)),
+            pltpu.SemaphoreType.DMA((count, n)),
+            pltpu.SemaphoreType.DMA((count, n)),
+        ],
+        compiler_params=pltpu.CompilerParams(collective_id=1, has_side_effects=True),
+    )(x)
 
 
 def passed_along(value, axis, steps):
@@ -202,9 +274,7 @@
     resid = inputs + beta * branch * gate_mid
     long_in = (resid * gate_long).astype(jnp.bfloat16)
     grad_z = (beta * adjoint * gate_out).astype(jnp.bfloat16)
-    channel_z, channel_w = lax.all_to_all(
-        jnp.stack([grad_z.T, long_in.T]), "ctx", split_axis=1, concat_axis=2, tiled=True
-    )
+    channel_z, channel_w = to_channels(jnp.stack([grad_z, long_in]))
     factor_b = math.gcd(seq_len, 128)
     factor_a = 2 * seq_len // factor_b
     zspec = to_spectrum(channel_z[:, None], factor_a, factor_b)

time: 317 us -> 316 us (level)
  Pallas kernels: 30.1 us -> 95.1 us
  waiting for transfers between devices: 78.9 us -> 28.8 us
  starting transfers between devices: 32 us -> 19.8 us
  local copies, waits for them, and re-layouts: 22.3 us -> 17.5 us
    pallas_call x0 -> x1, Pallas kernels: none -> 65 us  [to_channels(): pl.pallas_call(functools.partial(channel_kernel, n), out_shape=jax.ShapeD...]
    all_to_all x1 -> x0, waiting for transfers between devices: 43.4 us -> none  [per_device(): lax.all_to_all(jnp.stack([grad_z.T, long_in.T]), 'ctx', split_axis=1, con...]
    all_to_all x1 -> x0, starting transfers between devices: 14.4 us -> none  [per_device(): lax.all_to_all(jnp.stack([grad_z.T, long_in.T]), 'ctx', split_axis=1, con...]
    ppermute x2, waiting for transfers between devices: 8.74 us -> 2.06 us  [shifted(): return lax.ppermute(array, axis, pairs)]
    another operation x2 -> x0, local copies, waits for them, and re-layouts: 6.23 us -> none  [the longest x1 6.16 us: per_device(): jnp.stack([grad_z.T, long_in.T])]
  transfers between devices with their start and end apart: 5 -> 4, of which waited for: 3 -> 2; matrix products, arithmetic and copies ran while one was open for 24% -> 25% of each run, Pallas kernels for 10% -> 10%
where the time goes in v4:
time: 316 us; the launch traced here: 312 us
  matrix products  116 us (37%)
  Pallas kernels  95.1 us (30%)
  other arithmetic  33.6 us (11%)
  waiting for transfers between devices  28.8 us (9%)
  starting transfers between devices  19.8 us (6%)
  local copies, waits for them, and re-layouts  17.5 us (6%)
    pallas_call x1, Pallas kernels, to_channels(): pl.pallas_call(functools.partial(channel_kernel, n), out_shape=jax.ShapeD...  65 us
    conv_general_dilated x2, matrix products, depthwise(): lax.conv_general_dilated(extended[None], kernel[:, None, :], (1,), 'VALID...  60.5 us
    pallas_call x1, Pallas kernels, tap_exchange(): pl.pallas_call(functools.partial(tap_exchange_kernel, nz, nx, nc, scale),...  30.1 us
    conv_general_dilated x1, matrix products, per_device(): lax.conv_general_dilated(extended[None], grad_b[:, None, :], (1,), 'VALID...  29.1 us
    all_to_all x1, waiting for transfers between devices, per_device(): lax.all_to_all(input_part.astype(jnp.bfloat16), 'ctx', split_axis=1, conc...  26.7 us
    dot_general x6, matrix products, contract(): jnp.einsum(form, left, right, precision=lax.Precision.HIGH, preferred_ele...  26.2 us
    all_to_all x1, starting transfers between devices, per_device(): lax.all_to_all(input_part.astype(jnp.bfloat16), 'ctx', split_axis=1, conc...  9.25 us
    ppermute x2, starting transfers between devices, shifted(): return lax.ppermute(array, axis, pairs)  7.75 us
  transfers between devices with their start and end apart: 4, of which 2 were waited for; matrix products, arithmetic and copies ran while one was open for 25% of the time, Pallas kernels for 10%

profile of v4, /device:TPU:1, one launch (start us, length us, event | category | flops | bytes accessed | tf_op | source)
XLA Modules:
  0.0 312.4 jit_solution(15661986064370557571)
XLA Ops:
  3.8 4.5 %collective-permute-start.1 = (bf16[127,4096]{1,0:T(8,128)(2,1)}, bf16[127,4096]{1,0:T(8,128)(2,1)}, u32[]{:S(2)}, u32[]{:S(2)}) collective-permute-start(bf16[127,4096]{1,0:T(8,128)(2,1)} %slice_bitcast_fusion.1), channel_id=1, source_target_pairs={{0,1},{1,2},{2,3},{3,4},{4,5},{5,6},{6,7},{7,8},{8,9},{9,10},{10,1... | collective-permute-start | bytes 3121160 | tf_op jit(solution)/shard_map/ppermute | solution.py:176
  8.3 2.8 collective-permute-start
  18.2 2.1 collective-permute-done.1
  21.9 30.4 %fusion.16 = f32[1,128,4096]{2,0,1:T(1,128)S(1)} fusion(bf16[1,255,4096]{2,1,0:T(8,128)(2,1)S(1)} %maximum_bitcast_fusion.13, bf16[128,1,4096]{2,0,1:T(8,128)(2,1)S(1)} %fusion.11), kind=kOutput, calls=%fused_computation.30 | convolution fusion | flops 134217728 | bytes 5234688 | tf_op jit(solution)/shard_map/conv_general_dilated | solution.py:240
  52.4 2.1 fusion.31
  56.4 65.0 %shard_map.103 = bf16[2,64,8192]{2,1,0:T(8,128)(2,1)} custom-call(bf16[2,128,4096]{2,1,0:T(8,128)(2,1)} %pad_maximum_fusion.x_ref), custom_call_target="tpu_custom_call" | custom-call | tf_op jit(solution)/shard_map/pallas_call | solution.py:152
  123.7 2.4 convolution_bitcast_fusion
  126.2 2.4 convolution_bitcast_fusion.1
  128.5 6.3 %multiply_subtract_fusion.3 = (f32[64,1,128,128]{2,3,1,0:T(8,128)S(1)}, f32[64,1,128,128]{2,3,1,0:T(8,128)}, f32[64,1,128,128]{2,3,1,0:T(8,128)}, f32[64,1,128,128]{2,3,1,0:T(8,128)}) fusion(f32[64,2,128,128]{2,3,1,0:T(8,128)S(1)} %convolution_bitcast_fusion, f32[128,128]{0,1:T(8,128)S(1)} %get-tuple-element.29, f32[128,128]{0,1:T(8,128)S(1)} %get-tuple-element.30, ...), kind=kLoop, calls=%fused_computation.25 | loop fusion | flops 12582912 | bytes 33685504 | tf_op jit(solution)/shard_map/sub | solution.py:209
  134.9 7.1 %fusion.22 = f32[64,2,128,128]{2,3,0,1:T(8,128)S(1)} fusion(f32[64,1,128,128]{2,3,1,0:T(8,128)} %get-tuple-element.8, f32[64,1,128,128]{2,3,1,0:T(8,128)S(1)} %get-tuple-element.7, f32[1,2,128,128]{2,3,0,1:T(8,128)S(1)} %get-tuple-element.16, f32[1,2,128,128]{2,3,0,1:T(8,128)S(1)} %get-tuple-element.21), kind=kOutput, calls=%fused_computation.35 | convolution fusion | flops 3223388160 | bytes 17039360 | tf_op jit(solution)/shard_map/nqcb,qpbd->npcd/dot_general | solution.py:187
  142.0 4.9 %fusion.21 = f32[64,2,128,128]{2,3,0,1:T(8,128)S(1)} fusion(f32[64,1,128,128]{2,3,1,0:T(8,128)S(1)} %copy-done.3, f32[64,1,128,128]{2,3,1,0:T(8,128)S(1)} %copy-done.4, f32[1,2,128,128]{2,3,0,1:T(8,128)S(1)} %get-tuple-element.16, f32[1,2,128,128]{2,3,0,1:T(8,128)S(1)} %get-tuple-element.21), kind=kOutput, calls=%fused_computation.34 | convolution fusion | flops 3223388160 | bytes 17039360 | tf_op jit(solution)/shard_map/nqcb,qpbd->npcd/dot_general | solution.py:187
  146.9 2.7 multiply_add_fusion.1
  149.7 5.0 %fusion.18 = f32[64,2,128,128]{2,3,1,0:T(8,128)S(1)} fusion(f32[64,1,128,128]{2,3,0,1:T(8,128)S(1)} %get-tuple-element.4, f32[64,1,128,128]{2,3,0,1:T(8,128)S(1)} %get-tuple-element.3, f32[1,2,128,128]{2,3,1,0:T(8,128)S(1)} %copy-done.22, f32[1,2,128,128]{2,3,1,0:T(8,128)S(1)} %copy-done.21), kind=kOutput, calls=%fused_computation.32 | convolution fusion | flops 3223388160 | bytes 17039360 | tf_op jit(solution)/shard_map/npcd,pqdb->nqcb/dot_general | solution.py:187
  156.6 4.4 %fusion.38 = bf16[64,2,64,128]{3,2,1,0:T(8,128)(2,1)S(1)} fusion(f32[64,1,128,128]{2,3,1,0:T(8,128)S(1)} %get-tuple-element.6, f32[64,1,128,128]{2,3,1,0:T(8,128)S(1)} %get-tuple-element.5, f32[1,2,64,128]{3,2,1,0:T(8,128)S(1)} %copy-done.19, f32[1,2,64,128]{3,2,1,0:T(8,128)S(1)} %copy-done.18), kind=kOutput, calls=%fused_computation.66 | convolution fusion | flops 1613791232 | bytes 10616832 | tf_op jit(solution)/shard_map/rqac,nqcb->nrab/dot_general | solution.py:187
  162.9 9.2 %all-to-all-start = ((bf16[64,64,128]{2,0,1:T(8,128)(2,1)}), bf16[64,64,128]{2,0,1:T(8,128)(2,1)S(1)}, u32[]{:S(2)}, u32[]{:S(2)}) async-start(bf16[64,64,128]{2,0,1:T(8,128)(2,1)} %copy.65), calls=%async_computation | async-start | bytes 2097152 | tf_op jit(solution)/shard_map/all_to_all | solution.py:292
  173.4 26.7 %all-to-all-done = bf16[64,64,128]{2,0,1:T(8,128)(2,1)S(1)} async-done(((bf16[64,64,128]{2,0,1:T(8,128)(2,1)}), bf16[64,64,128]{2,0,1:T(8,128)(2,1)S(1)}, u32[]{:S(2)}, u32[]{:S(2)}) %all-to-all-start) | async-done | bytes 1048608 | tf_op jit(solution)/shard_map/all_to_all | solution.py:292
  201.8 1.9 copy.66
  203.7 4.2 %fusion.30 = bf16[128,4096]{1,0:T(8,128)(2,1)} fusion(bf16[1,128,4096]{2,1,0:T(8,128)(2,1)} %param.11, bf16[1,128,4096]{2,1,0:T(8,128)(2,1)} %param.12, f32[4096,128]{0,1:T(8,128)S(1)} %copy.66, bf16[128,4096]{1,0:T(8,128)(2,1)} %copy-done.5), kind=kLoop, calls=%fused_computation.53 | loop fusion | flops 4194304 | bytes 6291456 | tf_op jit(solution)/shard_map/convert_element_type | solution.py:296
  207.9 3.3 %collective-permute-start.2 = (bf16[127,4096]{1,0:T(8,128)(2,1)}, bf16[127,4096]{1,0:T(8,128)(2,1)}, u32[]{:S(2)}, u32[]{:S(2)}) collective-permute-start(bf16[127,4096]{1,0:T(8,128)(2,1)} %bitcast.182), channel_id=1, source_target_pairs={{1,0},{2,1},{3,2},{4,3},{5,4},{6,5},{7,6},{8,7},{9,8},{10,9},{11,1... | collective-permute-start | bytes 3121160 | tf_op jit(solution)/shard_map/ppermute | solution.py:176
  211.2 29.1 %fusion.14 = f32[1,4096,128]{1,0,2:T(1,128)} fusion(bf16[1,255,4096]{2,1,0:T(8,128)(2,1)S(1)} %copy-done.14, bf16[128,1,4096]{2,0,1:T(8,128)(2,1)} %bitcast.64), kind=kOutput, calls=%fused_computation.28 | convolution fusion | flops 134217728 | bytes 5234688 | tf_op jit(solution)/shard_map/conv_general_dilated | solution.py:300
  240.2 5.6 %copy.72 = f32[1,4096,128]{2,1,0:T(8,128)} copy(f32[1,4096,128]{1,0,2:T(1,128)} %fusion.14) | data formatting | bytes 4194304 | tf_op jit(solution)/shard_map/conv_general_dilated | solution.py:300
  245.9 30.1 %shard_map.104 = bf16[64,128]{1,0:T(8,128)(2,1)} custom-call(f32[8,4,2,64,128]{4,3,2,1,0:T(8,128)} %bitcast.186), custom_call_target="tpu_custom_call" | custom-call | tf_op jit(solution)/shard_map/pallas_call | solution.py:78
  279.2 30.1 %fusion.12 = f32[1,128,4096]{2,0,1:T(1,128)S(1)} fusion(bf16[1,255,4096]{2,1,0:T(8,128)(2,1)S(1)} %maximum_bitcast_fusion.16, bf16[128,1,4096]{2,0,1:T(8,128)(2,1)S(1)} %bitcast.183), kind=kOutput, calls=%fused_computation.26 | convolution fusion | flops 134217728 | bytes 5234688 | tf_op jit(solution)/shard_map/conv_general_dilated | solution.py:240
  309.4 2.8 fusion.39
  (78 shorter events, 25.8 us)
Async XLA Ops:
  0.6 17.2 %copy-start = (bf16[1,128,4096]{2,1,0:T(8,128)(2,1)S(1)}, bf16[1,128,4096]{2,1,0:T(8,128)(2,1)}, u32[]{:S(2)}) copy-start(bf16[1,128,4096]{2,1,0:T(8,128)(2,1)} %param.15) | copy-start | bytes 3145732
  3.8 16.5 %collective-permute-start.1 = (bf16[127,4096]{1,0:T(8,128)(2,1)}, bf16[127,4096]{1,0:T(8,128)(2,1)}, u32[]{:S(2)}, u32[]{:S(2)}) collective-permute-start(bf16[127,4096]{1,0:T(8,128)(2,1)} %slice_bitcast_fusion.1), channel_id=1, source_target_pairs={{0,1},{1,2},{2,3},{3,4},{4,5},{5,6},{6,7},{7,8},{8,9},{9,10},{10,1... | collective-permute-start | bytes 3121160 | tf_op jit(solution)/shard_map/ppermute | solution.py:176
  8.3 46.2 %collective-permute-start = (bf16[128,4096]{1,0:T(8,128)(2,1)}, bf16[128,4096]{1,0:T(8,128)(2,1)S(1)}, u32[]{:S(2)}, u32[]{:S(2)}) collective-permute-start(bf16[128,4096]{1,0:T(8,128)(2,1)} %bitcast), channel_id=1, source_target_pairs={{0,192},{64,0},{128,64},{192,128},{1,193},{65,1},{129,65},{193,129... | collective-permute-start | bytes 3145736 | tf_op jit(solution)/shard_map/ppermute | solution.py:170
  12.0 5.8 %copy-start.20 = (bf16[128,128]{1,0:T(8,128)(2,1)S(1)}, bf16[128,128]{1,0:T(8,128)(2,1)}, u32[]{:S(2)}) copy-start(bf16[128,128]{1,0:T(8,128)(2,1)} %rev.6) | copy-start | bytes 98308
  21.8 30.5 %copy-start.13 = (bf16[1,255,4096]{2,1,0:T(8,128)(2,1)}, bf16[1,255,4096]{2,1,0:T(8,128)(2,1)S(1)}, u32[]{:S(2)}) copy-start(bf16[1,255,4096]{2,1,0:T(8,128)(2,1)S(1)} %maximum_bitcast_fusion.13) | copy-start | bytes 6266884
  21.9 30.5 %copy-start.7 = (bf16[1,128,4096]{2,1,0:T(8,128)(2,1)S(1)}, bf16[1,128,4096]{2,1,0:T(8,128)(2,1)}, u32[]{:S(2)}) copy-start(bf16[1,128,4096]{2,1,0:T(8,128)(2,1)} %param.12) | copy-start | bytes 3145732
  21.9 30.5 %copy-start.9 = (bf16[1,128,4096]{2,1,0:T(8,128)(2,1)S(1)}, bf16[1,128,4096]{2,1,0:T(8,128)(2,1)}, u32[]{:S(2)}) copy-start(bf16[1,128,4096]{2,1,0:T(8,128)(2,1)} %param.9) | copy-start | bytes 3145732
  21.9 30.5 %copy-start.10 = (bf16[1,128,4096]{2,1,0:T(8,128)(2,1)S(1)}, bf16[1,128,4096]{2,1,0:T(8,128)(2,1)}, u32[]{:S(2)}) copy-start(bf16[1,128,4096]{2,1,0:T(8,128)(2,1)} %param.11) | copy-start | bytes 3145732
  54.5 66.9 %copy-start.5 = (bf16[128,4096]{1,0:T(8,128)(2,1)}, bf16[128,4096]{1,0:T(8,128)(2,1)S(1)}, u32[]{:S(2)}) copy-start(bf16[128,4096]{1,0:T(8,128)(2,1)S(1)} %collective-permute-done) | copy-start | bytes 3145732
  121.4 2.3 copy-start.16
  121.4 2.3 copy-start.17
  123.7 2.4 copy-start.12
  134.9 7.1 %copy-start.3 = (f32[64,1,128,128]{2,3,1,0:T(8,128)S(1)}, f32[64,1,128,128]{2,3,1,0:T(8,128)}, u32[]{:S(2)}) copy-start(f32[64,1,128,128]{2,3,1,0:T(8,128)} %get-tuple-element.19) | copy-start | bytes 12582916
  134.9 7.1 %copy-start.4 = (f32[64,1,128,128]{2,3,1,0:T(8,128)S(1)}, f32[64,1,128,128]{2,3,1,0:T(8,128)}, u32[]{:S(2)}) copy-start(f32[64,1,128,128]{2,3,1,0:T(8,128)} %get-tuple-element.20) | copy-start | bytes 12582916
  146.9 2.8 copy-start.21
  146.9 2.8 copy-start.22
  162.9 37.2 %all-to-all-start = ((bf16[64,64,128]{2,0,1:T(8,128)(2,1)}), bf16[64,64,128]{2,0,1:T(8,128)(2,1)S(1)}, u32[]{:S(2)}, u32[]{:S(2)}) async-start(bf16[64,64,128]{2,0,1:T(8,128)(2,1)} %copy.65), calls=%async_computation | async-start | bytes 2097152 | tf_op jit(solution)/shard_map/all_to_all | solution.py:292
  203.7 36.5 %copy-start.1 = (f32[4096,128]{0,1:T(8,128)}, f32[4096,128]{0,1:T(8,128)S(1)}, u32[]{:S(2)}) copy-start(f32[4096,128]{0,1:T(8,128)S(1)} %copy.66) | copy-start | bytes 6291460
  203.7 7.5 %copy-start.14 = (bf16[1,255,4096]{2,1,0:T(8,128)(2,1)S(1)}, bf16[1,255,4096]{2,1,0:T(8,128)(2,1)}, u32[]{:S(2)}) copy-start(bf16[1,255,4096]{2,1,0:T(8,128)(2,1)} %copy-done.13) | copy-start | bytes 6266884
  207.9 69.5 %collective-permute-start.2 = (bf16[127,4096]{1,0:T(8,128)(2,1)}, bf16[127,4096]{1,0:T(8,128)(2,1)}, u32[]{:S(2)}, u32[]{:S(2)}) collective-permute-start(bf16[127,4096]{1,0:T(8,128)(2,1)} %bitcast.182), channel_id=1, source_target_pairs={{1,0},{2,1},{3,2},{4,3},{5,4},{6,5},{7,6},{8,7},{9,8},{10,9},{11,1... | collective-permute-start | bytes 3121160 | tf_op jit(solution)/shard_map/ppermute | solution.py:176
  279.2 30.2 %copy-start.2 = (f32[4096,128]{0,1:T(8,128)S(1)}, f32[4096,128]{0,1:T(8,128)}, u32[]{:S(2)}) copy-start(f32[4096,128]{0,1:T(8,128)} %copy-done.1) | copy-start | bytes 6291460
  279.2 30.2 %copy-start.6 = (bf16[128,4096]{1,0:T(8,128)(2,1)S(1)}, bf16[128,4096]{1,0:T(8,128)(2,1)}, u32[]{:S(2)}) copy-start(bf16[128,4096]{1,0:T(8,128)(2,1)} %copy-done.5) | copy-start | bytes 3145732
  279.2 30.2 %copy-start.8 = (bf16[1,128,4096]{2,1,0:T(8,128)(2,1)S(1)}, bf16[1,128,4096]{2,1,0:T(8,128)(2,1)}, u32[]{:S(2)}) copy-start(bf16[1,128,4096]{2,1,0:T(8,128)(2,1)} %param.12) | copy-start | bytes 3145732
  279.2 30.2 %copy-start.11 = (bf16[1,128,4096]{2,1,0:T(8,128)(2,1)S(1)}, bf16[1,128,4096]{2,1,0:T(8,128)(2,1)}, u32[]{:S(2)}) copy-start(bf16[1,128,4096]{2,1,0:T(8,128)(2,1)} %param.10) | copy-start | bytes 3145732
  (3 other events, 6.0 us)

commit v5 on v4

--- a/solution.py
+++ b/solution.py
@@ -311,7 +311,10 @@
     chip_cores, chips_x = 2, 4
     chips_z = devices // (chip_cores * chips_x)
     parts = tap_part.reshape(chips_z, chips_x, chip_cores, columns, tap_part.shape[1])
-    mid_grad = tap_exchange(parts, scale).T[::-1][None]
+    summed = tap_exchange(parts, scale)
+    taps_flip = jnp.eye(summed.shape[1], dtype=summed.dtype)[::-1]
+    mid_grad = jnp.dot(summed, taps_flip, preferred_element_type=jnp.float32)
+    mid_grad = mid_grad.astype(summed.dtype).T[None]
     return (input_grad, long_grad, mid_grad)
 
 

time: 316 us -> 317 us (level)
  no operation moved by 1% of the time
where the time goes in v5:
time: 317 us; the launch traced here: 313 us
  matrix products  118 us (37%)
  Pallas kernels  95.2 us (30%)
  other arithmetic  33.6 us (11%)
  waiting for transfers between devices  28.7 us (9%)
  starting transfers between devices  19.8 us (6%)
  local copies, waits for them, and re-layouts  16.2 us (5%)
    pallas_call x1, Pallas kernels, to_channels(): pl.pallas_call(functools.partial(channel_kernel, n), out_shape=jax.ShapeD...  65 us
    conv_general_dilated x2, matrix products, depthwise(): lax.conv_general_dilated(extended[None], kernel[:, None, :], (1,), 'VALID...  60.5 us
    pallas_call x1, Pallas kernels, tap_exchange(): pl.pallas_call(functools.partial(tap_exchange_kernel, nz, nx, nc, scale),...  30.1 us
    conv_general_dilated x1, matrix products, per_device(): lax.conv_general_dilated(extended[None], grad_b[:, None, :], (1,), 'VALID...  29.1 us
    all_to_all x1, waiting for transfers between devices, per_device(): lax.all_to_all(input_part.astype(jnp.bfloat16), 'ctx', split_axis=1, conc...  26.7 us
    dot_general x6, matrix products, contract(): jnp.einsum(form, left, right, precision=lax.Precision.HIGH, preferred_ele...  26.1 us
    all_to_all x1, starting transfers between devices, per_device(): lax.all_to_all(input_part.astype(jnp.bfloat16), 'ctx', split_axis=1, conc...  9.26 us
    ppermute x2, starting transfers between devices, shifted(): return lax.ppermute(array, axis, pairs)  7.75 us
  transfers between devices with their start and end apart: 4, of which 2 were waited for; matrix products, arithmetic and copies ran while one was open for 25% of the time, Pallas kernels for 10%

profile of v5, /device:TPU:1, one launch (start us, length us, event | category | flops | bytes accessed | tf_op | source)
XLA Modules:
  0.0 312.6 jit_solution(17336777361686838679)
XLA Ops:
  3.8 4.5 %collective-permute-start.1 = (bf16[127,4096]{1,0:T(8,128)(2,1)}, bf16[127,4096]{1,0:T(8,128)(2,1)}, u32[]{:S(2)}, u32[]{:S(2)}) collective-permute-start(bf16[127,4096]{1,0:T(8,128)(2,1)} %slice_bitcast_fusion.1), channel_id=1, source_target_pairs={{0,1},{1,2},{2,3},{3,4},{4,5},{5,6},{6,7},{7,8},{8,9},{9,10},{10,1... | collective-permute-start | bytes 3121160 | tf_op jit(solution)/shard_map/ppermute | solution.py:176
  8.3 2.8 collective-permute-start
  18.3 2.0 collective-permute-done.1
  21.9 30.4 %fusion.16 = f32[1,128,4096]{2,0,1:T(1,128)S(1)} fusion(bf16[1,255,4096]{2,1,0:T(8,128)(2,1)S(1)} %maximum_bitcast_fusion.13, bf16[128,1,4096]{2,0,1:T(8,128)(2,1)S(1)} %fusion.11), kind=kOutput, calls=%fused_computation.30 | convolution fusion | flops 134217728 | bytes 5234688 | tf_op jit(solution)/shard_map/conv_general_dilated | solution.py:240
  52.4 2.1 fusion.31
  56.4 65.0 %shard_map.103 = bf16[2,64,8192]{2,1,0:T(8,128)(2,1)} custom-call(bf16[2,128,4096]{2,1,0:T(8,128)(2,1)} %pad_maximum_fusion.x_ref), custom_call_target="tpu_custom_call" | custom-call | tf_op jit(solution)/shard_map/pallas_call | solution.py:152
  123.8 2.4 convolution_bitcast_fusion
  126.1 2.4 convolution_bitcast_fusion.1
  128.5 6.4 %multiply_subtract_fusion.3 = (f32[64,1,128,128]{2,3,1,0:T(8,128)S(1)}, f32[64,1,128,128]{2,3,1,0:T(8,128)}, f32[64,1,128,128]{2,3,1,0:T(8,128)}, f32[64,1,128,128]{2,3,1,0:T(8,128)}) fusion(f32[64,2,128,128]{2,3,1,0:T(8,128)S(1)} %convolution_bitcast_fusion, f32[128,128]{0,1:T(8,128)S(1)} %get-tuple-element.29, f32[128,128]{0,1:T(8,128)S(1)} %get-tuple-element.30, ...), kind=kLoop, calls=%fused_computation.25 | loop fusion | flops 12582912 | bytes 33685504 | tf_op jit(solution)/shard_map/sub | solution.py:209
  134.9 7.1 %fusion.22 = f32[64,2,128,128]{2,3,0,1:T(8,128)S(1)} fusion(f32[64,1,128,128]{2,3,1,0:T(8,128)} %get-tuple-element.8, f32[64,1,128,128]{2,3,1,0:T(8,128)S(1)} %get-tuple-element.7, f32[1,2,128,128]{2,3,0,1:T(8,128)S(1)} %get-tuple-element.16, f32[1,2,128,128]{2,3,0,1:T(8,128)S(1)} %get-tuple-element.21), kind=kOutput, calls=%fused_computation.35 | convolution fusion | flops 3223388160 | bytes 17039360 | tf_op jit(solution)/shard_map/nqcb,qpbd->npcd/dot_general | solution.py:187
  142.0 4.9 %fusion.21 = f32[64,2,128,128]{2,3,0,1:T(8,128)S(1)} fusion(f32[64,1,128,128]{2,3,1,0:T(8,128)S(1)} %copy-done.3, f32[64,1,128,128]{2,3,1,0:T(8,128)S(1)} %copy-done.4, f32[1,2,128,128]{2,3,0,1:T(8,128)S(1)} %get-tuple-element.16, f32[1,2,128,128]{2,3,0,1:T(8,128)S(1)} %get-tuple-element.21), kind=kOutput, calls=%fused_computation.34 | convolution fusion | flops 3223388160 | bytes 17039360 | tf_op jit(solution)/shard_map/nqcb,qpbd->npcd/dot_general | solution.py:187
  147.0 2.7 multiply_add_fusion.1
  149.7 5.0 %fusion.18 = f32[64,2,128,128]{2,3,1,0:T(8,128)S(1)} fusion(f32[64,1,128,128]{2,3,0,1:T(8,128)S(1)} %get-tuple-element.4, f32[64,1,128,128]{2,3,0,1:T(8,128)S(1)} %get-tuple-element.3, f32[1,2,128,128]{2,3,1,0:T(8,128)S(1)} %copy-done.23, f32[1,2,128,128]{2,3,1,0:T(8,128)S(1)} %copy-done.22), kind=kOutput, calls=%fused_computation.32 | convolution fusion | flops 3223388160 | bytes 17039360 | tf_op jit(solution)/shard_map/npcd,pqdb->nqcb/dot_general | solution.py:187
  156.7 4.4 %fusion.38 = bf16[64,2,64,128]{3,2,1,0:T(8,128)(2,1)S(1)} fusion(f32[64,1,128,128]{2,3,1,0:T(8,128)S(1)} %get-tuple-element.6, f32[64,1,128,128]{2,3,1,0:T(8,128)S(1)} %get-tuple-element.5, f32[1,2,64,128]{3,2,1,0:T(8,128)S(1)} %copy-done.21, f32[1,2,64,128]{3,2,1,0:T(8,128)S(1)} %copy-done.20), kind=kOutput, calls=%fused_computation.66 | convolution fusion | flops 1613791232 | bytes 10616832 | tf_op jit(solution)/shard_map/rqac,nqcb->nrab/dot_general | solution.py:187
  162.9 9.3 %all-to-all-start = ((bf16[64,64,128]{2,0,1:T(8,128)(2,1)}), bf16[64,64,128]{2,0,1:T(8,128)(2,1)S(1)}, u32[]{:S(2)}, u32[]{:S(2)}) async-start(bf16[64,64,128]{2,0,1:T(8,128)(2,1)} %copy.65), calls=%async_computation | async-start | bytes 2097152 | tf_op jit(solution)/shard_map/all_to_all | solution.py:292
  173.5 26.7 %all-to-all-done = bf16[64,64,128]{2,0,1:T(8,128)(2,1)S(1)} async-done(((bf16[64,64,128]{2,0,1:T(8,128)(2,1)}), bf16[64,64,128]{2,0,1:T(8,128)(2,1)S(1)}, u32[]{:S(2)}, u32[]{:S(2)}) %all-to-all-start) | async-done | bytes 1048608 | tf_op jit(solution)/shard_map/all_to_all | solution.py:292
  201.8 1.9 copy.66
  203.7 4.2 %fusion.30 = bf16[128,4096]{1,0:T(8,128)(2,1)} fusion(bf16[1,128,4096]{2,1,0:T(8,128)(2,1)} %param.11, bf16[1,128,4096]{2,1,0:T(8,128)(2,1)} %param.12, f32[4096,128]{0,1:T(8,128)S(1)} %copy.66, bf16[128,4096]{1,0:T(8,128)(2,1)} %copy-done.5), kind=kLoop, calls=%fused_computation.53 | loop fusion | flops 4194304 | bytes 6291456 | tf_op jit(solution)/shard_map/convert_element_type | solution.py:296
  207.9 3.3 %collective-permute-start.2 = (bf16[127,4096]{1,0:T(8,128)(2,1)}, bf16[127,4096]{1,0:T(8,128)(2,1)}, u32[]{:S(2)}, u32[]{:S(2)}) collective-permute-start(bf16[127,4096]{1,0:T(8,128)(2,1)} %bitcast.184), channel_id=1, source_target_pairs={{1,0},{2,1},{3,2},{4,3},{5,4},{6,5},{7,6},{8,7},{9,8},{10,9},{11,1... | collective-permute-start | bytes 3121160 | tf_op jit(solution)/shard_map/ppermute | solution.py:176
  211.2 29.1 %fusion.14 = f32[1,4096,128]{1,0,2:T(1,128)} fusion(bf16[1,255,4096]{2,1,0:T(8,128)(2,1)S(1)} %copy-done.14, bf16[128,1,4096]{2,0,1:T(8,128)(2,1)} %bitcast.64), kind=kOutput, calls=%fused_computation.28 | convolution fusion | flops 134217728 | bytes 5234688 | tf_op jit(solution)/shard_map/conv_general_dilated | solution.py:300
  240.3 5.7 %copy.72 = f32[1,4096,128]{2,1,0:T(8,128)} copy(f32[1,4096,128]{1,0,2:T(1,128)} %fusion.14) | data formatting | bytes 4194304 | tf_op jit(solution)/shard_map/conv_general_dilated | solution.py:300
  245.9 30.1 %shard_map.104 = bf16[64,128]{1,0:T(8,128)(2,1)} custom-call(f32[8,4,2,64,128]{4,3,2,1,0:T(8,128)} %bitcast.188), custom_call_target="tpu_custom_call" | custom-call | tf_op jit(solution)/shard_map/pallas_call | solution.py:78
  279.3 30.1 %fusion.12 = f32[1,128,4096]{2,0,1:T(1,128)S(1)} fusion(bf16[1,255,4096]{2,1,0:T(8,128)(2,1)S(1)} %maximum_bitcast_fusion.16, bf16[128,1,4096]{2,0,1:T(8,128)(2,1)S(1)} %bitcast.185), kind=kOutput, calls=%fused_computation.26 | convolution fusion | flops 134217728 | bytes 5234688 | tf_op jit(solution)/shard_map/conv_general_dilated | solution.py:240
  309.5 2.8 fusion.40
  (80 shorter events, 25.9 us)
Async XLA Ops:
  0.6 17.2 %copy-start = (bf16[1,128,4096]{2,1,0:T(8,128)(2,1)S(1)}, bf16[1,128,4096]{2,1,0:T(8,128)(2,1)}, u32[]{:S(2)}) copy-start(bf16[1,128,4096]{2,1,0:T(8,128)(2,1)} %param.15) | copy-start | bytes 3145732
  3.8 16.5 %collective-permute-start.1 = (bf16[127,4096]{1,0:T(8,128)(2,1)}, bf16[127,4096]{1,0:T(8,128)(2,1)}, u32[]{:S(2)}, u32[]{:S(2)}) collective-permute-start(bf16[127,4096]{1,0:T(8,128)(2,1)} %slice_bitcast_fusion.1), channel_id=1, source_target_pairs={{0,1},{1,2},{2,3},{3,4},{4,5},{5,6},{6,7},{7,8},{8,9},{9,10},{10,1... | collective-permute-start | bytes 3121160 | tf_op jit(solution)/shard_map/ppermute | solution.py:176
  8.3 46.2 %collective-permute-start = (bf16[128,4096]{1,0:T(8,128)(2,1)}, bf16[128,4096]{1,0:T(8,128)(2,1)S(1)}, u32[]{:S(2)}, u32[]{:S(2)}) collective-permute-start(bf16[128,4096]{1,0:T(8,128)(2,1)} %bitcast), channel_id=1, source_target_pairs={{0,192},{64,0},{128,64},{192,128},{1,193},{65,1},{129,65},{193,129... | collective-permute-start | bytes 3145736 | tf_op jit(solution)/shard_map/ppermute | solution.py:170
  12.0 5.8 %copy-start.18 = (bf16[128,128]{1,0:T(8,128)(2,1)S(1)}, bf16[128,128]{1,0:T(8,128)(2,1)}, u32[]{:S(2)}) copy-start(bf16[128,128]{1,0:T(8,128)(2,1)} %rev.4) | copy-start | bytes 98308
  21.8 30.5 %copy-start.13 = (bf16[1,255,4096]{2,1,0:T(8,128)(2,1)}, bf16[1,255,4096]{2,1,0:T(8,128)(2,1)S(1)}, u32[]{:S(2)}) copy-start(bf16[1,255,4096]{2,1,0:T(8,128)(2,1)S(1)} %maximum_bitcast_fusion.13) | copy-start | bytes 6266884
  21.9 30.5 %copy-start.7 = (bf16[1,128,4096]{2,1,0:T(8,128)(2,1)S(1)}, bf16[1,128,4096]{2,1,0:T(8,128)(2,1)}, u32[]{:S(2)}) copy-start(bf16[1,128,4096]{2,1,0:T(8,128)(2,1)} %param.12) | copy-start | bytes 3145732
  21.9 30.5 %copy-start.9 = (bf16[1,128,4096]{2,1,0:T(8,128)(2,1)S(1)}, bf16[1,128,4096]{2,1,0:T(8,128)(2,1)}, u32[]{:S(2)}) copy-start(bf16[1,128,4096]{2,1,0:T(8,128)(2,1)} %param.9) | copy-start | bytes 3145732
  21.9 30.5 %copy-start.10 = (bf16[1,128,4096]{2,1,0:T(8,128)(2,1)S(1)}, bf16[1,128,4096]{2,1,0:T(8,128)(2,1)}, u32[]{:S(2)}) copy-start(bf16[1,128,4096]{2,1,0:T(8,128)(2,1)} %param.11) | copy-start | bytes 3145732
  54.5 66.9 %copy-start.5 = (bf16[128,4096]{1,0:T(8,128)(2,1)}, bf16[128,4096]{1,0:T(8,128)(2,1)S(1)}, u32[]{:S(2)}) copy-start(bf16[128,4096]{1,0:T(8,128)(2,1)S(1)} %collective-permute-done) | copy-start | bytes 3145732
  121.4 2.3 copy-start.16
  123.7 2.4 copy-start.12
  134.9 7.1 %copy-start.3 = (f32[64,1,128,128]{2,3,1,0:T(8,128)S(1)}, f32[64,1,128,128]{2,3,1,0:T(8,128)}, u32[]{:S(2)}) copy-start(f32[64,1,128,128]{2,3,1,0:T(8,128)} %get-tuple-element.19) | copy-start | bytes 12582916
  134.9 7.1 %copy-start.4 = (f32[64,1,128,128]{2,3,1,0:T(8,128)S(1)}, f32[64,1,128,128]{2,3,1,0:T(8,128)}, u32[]{:S(2)}) copy-start(f32[64,1,128,128]{2,3,1,0:T(8,128)} %get-tuple-element.20) | copy-start | bytes 12582916
  146.9 2.8 copy-start.22
  147.0 2.8 copy-start.23
  162.9 37.3 %all-to-all-start = ((bf16[64,64,128]{2,0,1:T(8,128)(2,1)}), bf16[64,64,128]{2,0,1:T(8,128)(2,1)S(1)}, u32[]{:S(2)}, u32[]{:S(2)}) async-start(bf16[64,64,128]{2,0,1:T(8,128)(2,1)} %copy.65), calls=%async_computation | async-start | bytes 2097152 | tf_op jit(solution)/shard_map/all_to_all | solution.py:292
  203.7 36.5 %copy-start.1 = (f32[4096,128]{0,1:T(8,128)}, f32[4096,128]{0,1:T(8,128)S(1)}, u32[]{:S(2)}) copy-start(f32[4096,128]{0,1:T(8,128)S(1)} %copy.66) | copy-start | bytes 6291460
  203.7 7.5 %copy-start.14 = (bf16[1,255,4096]{2,1,0:T(8,128)(2,1)S(1)}, bf16[1,255,4096]{2,1,0:T(8,128)(2,1)}, u32[]{:S(2)}) copy-start(bf16[1,255,4096]{2,1,0:T(8,128)(2,1)} %copy-done.13) | copy-start | bytes 6266884
  207.9 69.6 %collective-permute-start.2 = (bf16[127,4096]{1,0:T(8,128)(2,1)}, bf16[127,4096]{1,0:T(8,128)(2,1)}, u32[]{:S(2)}, u32[]{:S(2)}) collective-permute-start(bf16[127,4096]{1,0:T(8,128)(2,1)} %bitcast.184), channel_id=1, source_target_pairs={{1,0},{2,1},{3,2},{4,3},{5,4},{6,5},{7,6},{8,7},{9,8},{10,9},{11,1... | collective-permute-start | bytes 3121160 | tf_op jit(solution)/shard_map/ppermute | solution.py:176
  240.3 35.8 %copy-start.19 = (bf16[128,128]{1,0:T(8,128)(2,1)S(1)}, bf16[128,128]{1,0:T(8,128)(2,1)}, u32[]{:S(2)}) copy-start(bf16[128,128]{1,0:T(8,128)(2,1)} %rev.4) | copy-start | bytes 98308
  279.3 30.2 %copy-start.2 = (f32[4096,128]{0,1:T(8,128)S(1)}, f32[4096,128]{0,1:T(8,128)}, u32[]{:S(2)}) copy-start(f32[4096,128]{0,1:T(8,128)} %copy-done.1) | copy-start | bytes 6291460
  279.3 30.2 %copy-start.6 = (bf16[128,4096]{1,0:T(8,128)(2,1)S(1)}, bf16[128,4096]{1,0:T(8,128)(2,1)}, u32[]{:S(2)}) copy-start(bf16[128,4096]{1,0:T(8,128)(2,1)} %copy-done.5) | copy-start | bytes 3145732
  279.3 30.2 %copy-start.8 = (bf16[1,128,4096]{2,1,0:T(8,128)(2,1)S(1)}, bf16[1,128,4096]{2,1,0:T(8,128)(2,1)}, u32[]{:S(2)}) copy-start(bf16[1,128,4096]{2,1,0:T(8,128)(2,1)} %param.12) | copy-start | bytes 3145732
  279.3 30.2 %copy-start.11 = (bf16[1,128,4096]{2,1,0:T(8,128)(2,1)S(1)}, bf16[1,128,4096]{2,1,0:T(8,128)(2,1)}, u32[]{:S(2)}) copy-start(bf16[1,128,4096]{2,1,0:T(8,128)(2,1)} %param.10) | copy-start | bytes 3145732
  (4 other events, 8.3 us)

commit v6 on v5

--- a/solution.py
+++ b/solution.py
@@ -39,20 +39,28 @@
             device_id_type=MESH_IDS,
         )
 
-    first = send(x_ref.at[:, :, 1 - core], r1, peers[0], 0, 0)
-    first.start()
-    first.wait()
-    s1[...] = x_ref[:, :, core] + r1[...]
-
+    firsts = []
+    for target in range(nx):
+        copy = send(x_ref.at[:, target, 1 - core], r1.at[:, target], peers[0], target, target)
+        copy.start()
+        firsts.append(copy)
     second = []
-    for k in range(1, nx):
+    for k in range(1, nx + 1):
         target = (xi + k) % nx
-        copy = send(s1.at[:, target], r2.at[xi], device(zi, target, core), 1 + target, 1 + xi)
-        copy.start()
-        second.append(copy)
+        for block in range(nx):
+
+            @pl.when(target == block)
+            def _(block=block):
+                firsts[block].wait()
+
+        s1[:, target] = x_ref[:, target, core] + r1[:, target]
+        if k < nx:
+            copy = send(s1.at[:, target], r2.at[xi], device(zi, target, core), nx + target, nx + xi)
+            copy.start()
+            second.append(copy)
     for k in range(1, nx):
         source = (xi + nx - k) % nx
-        send(s1.at[:, source], r2.at[source], device(zi, source, core), 1 + source, 1 + source).wait_recv()
+        send(s1.at[:, source], r2.at[source], device(zi, source, core), nx + source, nx + source).wait_recv()
     for copy in second:
         copy.wait_send()
     r2[xi] = s1[:, xi]
@@ -61,12 +69,12 @@
     third = []
     for k in range(1, nz):
         target = (zi + k) % nz
-        copy = send(s2.at[target], r3.at[zi], device(target, xi, core), 1 + nx + target, 1 + nx + zi)
+        copy = send(s2.at[target], r3.at[zi], device(target, xi, core), 2 * nx + target, 2 * nx + zi)
         copy.start()
         third.append(copy)
     for k in range(1, nz):
         source = (zi + nz - k) % nz
-        send(s2.at[source], r3.at[source], device(source, xi, core), 1 + nx + source, 1 + nx + source).wait_recv()
+        send(s2.at[source], r3.at[source], device(source, xi, core), 2 * nx + source, 2 * nx + source).wait_recv()
     for copy in third:
         copy.wait_send()
     r3[zi] = s2[zi]
@@ -86,7 +94,7 @@
             pltpu.VMEM((nx, nz, taps, width), jnp.float32),
             pltpu.VMEM((nz, taps, width), jnp.float32),
             pltpu.VMEM((nz, taps, width), jnp.float32),
-            pltpu.SemaphoreType.DMA((2, 1 + nx + nz)),
+            pltpu.SemaphoreType.DMA((2, 2 * nx + nz)),
         ],
         compiler_params=pltpu.CompilerParams(collective_id=0, has_side_effects=True),
     )(parts)

time: 317 us -> 317 us (level)
  no operation moved by 1% of the time
where the time goes in v6:
time: 317 us; the launch traced here: 313 us
  matrix products  118 us (37%)
  Pallas kernels  95.1 us (30%)
  other arithmetic  33.6 us (11%)
  waiting for transfers between devices  28.7 us (9%)
  starting transfers between devices  19.8 us (6%)
  local copies, waits for them, and re-layouts  16.2 us (5%)
    pallas_call x1, Pallas kernels, to_channels(): pl.pallas_call(functools.partial(channel_kernel, n), out_shape=jax.ShapeD...  65 us
    conv_general_dilated x2, matrix products, depthwise(): lax.conv_general_dilated(extended[None], kernel[:, None, :], (1,), 'VALID...  60.5 us
    pallas_call x1, Pallas kernels, tap_exchange(): pl.pallas_call(functools.partial(tap_exchange_kernel, nz, nx, nc, scale),...  30.1 us
    conv_general_dilated x1, matrix products, per_device(): lax.conv_general_dilated(extended[None], grad_b[:, None, :], (1,), 'VALID...  29.1 us
    all_to_all x1, waiting for transfers between devices, per_device(): lax.all_to_all(input_part.astype(jnp.bfloat16), 'ctx', split_axis=1, conc...  26.7 us
    dot_general x6, matrix products, contract(): jnp.einsum(form, left, right, precision=lax.Precision.HIGH, preferred_ele...  26.1 us
    all_to_all x1, starting transfers between devices, per_device(): lax.all_to_all(input_part.astype(jnp.bfloat16), 'ctx', split_axis=1, conc...  9.26 us
    ppermute x2, starting transfers between devices, shifted(): return lax.ppermute(array, axis, pairs)  7.75 us
  transfers between devices with their start and end apart: 4, of which 2 were waited for; matrix products, arithmetic and copies ran while one was open for 25% of the time, Pallas kernels for 10%

profile of v6, /device:TPU:1, one launch (start us, length us, event | category | flops | bytes accessed | tf_op | source)
XLA Modules:
  0.0 312.5 jit_solution(15738256810926840996)
XLA Ops:
  3.8 4.5 %collective-permute-start.1 = (bf16[127,4096]{1,0:T(8,128)(2,1)}, bf16[127,4096]{1,0:T(8,128)(2,1)}, u32[]{:S(2)}, u32[]{:S(2)}) collective-permute-start(bf16[127,4096]{1,0:T(8,128)(2,1)} %slice_bitcast_fusion.1), channel_id=1, source_target_pairs={{0,1},{1,2},{2,3},{3,4},{4,5},{5,6},{6,7},{7,8},{8,9},{9,10},{10,1... | collective-permute-start | bytes 3121160 | tf_op jit(solution)/shard_map/ppermute | solution.py:184
  8.3 2.8 collective-permute-start
  18.3 2.0 collective-permute-done.1
  21.9 30.4 %fusion.16 = f32[1,128,4096]{2,0,1:T(1,128)S(1)} fusion(bf16[1,255,4096]{2,1,0:T(8,128)(2,1)S(1)} %maximum_bitcast_fusion.13, bf16[128,1,4096]{2,0,1:T(8,128)(2,1)S(1)} %fusion.11), kind=kOutput, calls=%fused_computation.30 | convolution fusion | flops 134217728 | bytes 5234688 | tf_op jit(solution)/shard_map/conv_general_dilated | solution.py:248
  52.4 2.1 fusion.31
  56.4 65.0 %shard_map.103 = bf16[2,64,8192]{2,1,0:T(8,128)(2,1)} custom-call(bf16[2,128,4096]{2,1,0:T(8,128)(2,1)} %pad_maximum_fusion.x_ref), custom_call_target="tpu_custom_call" | custom-call | tf_op jit(solution)/shard_map/pallas_call | solution.py:160
  123.8 2.4 convolution_bitcast_fusion
  126.1 2.4 convolution_bitcast_fusion.1
  128.5 6.4 %multiply_subtract_fusion.3 = (f32[64,1,128,128]{2,3,1,0:T(8,128)S(1)}, f32[64,1,128,128]{2,3,1,0:T(8,128)}, f32[64,1,128,128]{2,3,1,0:T(8,128)}, f32[64,1,128,128]{2,3,1,0:T(8,128)}) fusion(f32[64,2,128,128]{2,3,1,0:T(8,128)S(1)} %convolution_bitcast_fusion, f32[128,128]{0,1:T(8,128)S(1)} %get-tuple-element.29, f32[128,128]{0,1:T(8,128)S(1)} %get-tuple-element.30, ...), kind=kLoop, calls=%fused_computation.25 | loop fusion | flops 12582912 | bytes 33685504 | tf_op jit(solution)/shard_map/sub | solution.py:217
  134.9 7.1 %fusion.22 = f32[64,2,128,128]{2,3,0,1:T(8,128)S(1)} fusion(f32[64,1,128,128]{2,3,1,0:T(8,128)} %get-tuple-element.8, f32[64,1,128,128]{2,3,1,0:T(8,128)S(1)} %get-tuple-element.7, f32[1,2,128,128]{2,3,0,1:T(8,128)S(1)} %get-tuple-element.16, f32[1,2,128,128]{2,3,0,1:T(8,128)S(1)} %get-tuple-element.21), kind=kOutput, calls=%fused_computation.35 | convolution fusion | flops 3223388160 | bytes 17039360 | tf_op jit(solution)/shard_map/nqcb,qpbd->npcd/dot_general | solution.py:195
  142.0 4.9 %fusion.21 = f32[64,2,128,128]{2,3,0,1:T(8,128)S(1)} fusion(f32[64,1,128,128]{2,3,1,0:T(8,128)S(1)} %copy-done.3, f32[64,1,128,128]{2,3,1,0:T(8,128)S(1)} %copy-done.4, f32[1,2,128,128]{2,3,0,1:T(8,128)S(1)} %get-tuple-element.16, f32[1,2,128,128]{2,3,0,1:T(8,128)S(1)} %get-tuple-element.21), kind=kOutput, calls=%fused_computation.34 | convolution fusion | flops 3223388160 | bytes 17039360 | tf_op jit(solution)/shard_map/nqcb,qpbd->npcd/dot_general | solution.py:195
  147.0 2.7 multiply_add_fusion.1
  149.7 5.0 %fusion.18 = f32[64,2,128,128]{2,3,1,0:T(8,128)S(1)} fusion(f32[64,1,128,128]{2,3,0,1:T(8,128)S(1)} %get-tuple-element.4, f32[64,1,128,128]{2,3,0,1:T(8,128)S(1)} %get-tuple-element.3, f32[1,2,128,128]{2,3,1,0:T(8,128)S(1)} %copy-done.23, f32[1,2,128,128]{2,3,1,0:T(8,128)S(1)} %copy-done.22), kind=kOutput, calls=%fused_computation.32 | convolution fusion | flops 3223388160 | bytes 17039360 | tf_op jit(solution)/shard_map/npcd,pqdb->nqcb/dot_general | solution.py:195
  156.7 4.4 %fusion.38 = bf16[64,2,64,128]{3,2,1,0:T(8,128)(2,1)S(1)} fusion(f32[64,1,128,128]{2,3,1,0:T(8,128)S(1)} %get-tuple-element.6, f32[64,1,128,128]{2,3,1,0:T(8,128)S(1)} %get-tuple-element.5, f32[1,2,64,128]{3,2,1,0:T(8,128)S(1)} %copy-done.21, f32[1,2,64,128]{3,2,1,0:T(8,128)S(1)} %copy-done.20), kind=kOutput, calls=%fused_computation.66 | convolution fusion | flops 1613791232 | bytes 10616832 | tf_op jit(solution)/shard_map/rqac,nqcb->nrab/dot_general | solution.py:195
  162.9 9.3 %all-to-all-start = ((bf16[64,64,128]{2,0,1:T(8,128)(2,1)}), bf16[64,64,128]{2,0,1:T(8,128)(2,1)S(1)}, u32[]{:S(2)}, u32[]{:S(2)}) async-start(bf16[64,64,128]{2,0,1:T(8,128)(2,1)} %copy.65), calls=%async_computation | async-start | bytes 2097152 | tf_op jit(solution)/shard_map/all_to_all | solution.py:300
  173.5 26.7 %all-to-all-done = bf16[64,64,128]{2,0,1:T(8,128)(2,1)S(1)} async-done(((bf16[64,64,128]{2,0,1:T(8,128)(2,1)}), bf16[64,64,128]{2,0,1:T(8,128)(2,1)S(1)}, u32[]{:S(2)}, u32[]{:S(2)}) %all-to-all-start) | async-done | bytes 1048608 | tf_op jit(solution)/shard_map/all_to_all | solution.py:300
  201.8 1.9 copy.66
  203.7 4.2 %fusion.30 = bf16[128,4096]{1,0:T(8,128)(2,1)} fusion(bf16[1,128,4096]{2,1,0:T(8,128)(2,1)} %param.11, bf16[1,128,4096]{2,1,0:T(8,128)(2,1)} %param.12, f32[4096,128]{0,1:T(8,128)S(1)} %copy.66, bf16[128,4096]{1,0:T(8,128)(2,1)} %copy-done.5), kind=kLoop, calls=%fused_computation.53 | loop fusion | flops 4194304 | bytes 6291456 | tf_op jit(solution)/shard_map/convert_element_type | solution.py:304
  207.9 3.3 %collective-permute-start.2 = (bf16[127,4096]{1,0:T(8,128)(2,1)}, bf16[127,4096]{1,0:T(8,128)(2,1)}, u32[]{:S(2)}, u32[]{:S(2)}) collective-permute-start(bf16[127,4096]{1,0:T(8,128)(2,1)} %bitcast.184), channel_id=1, source_target_pairs={{1,0},{2,1},{3,2},{4,3},{5,4},{6,5},{7,6},{8,7},{9,8},{10,9},{11,1... | collective-permute-start | bytes 3121160 | tf_op jit(solution)/shard_map/ppermute | solution.py:184
  211.2 29.1 %fusion.14 = f32[1,4096,128]{1,0,2:T(1,128)} fusion(bf16[1,255,4096]{2,1,0:T(8,128)(2,1)S(1)} %copy-done.14, bf16[128,1,4096]{2,0,1:T(8,128)(2,1)} %bitcast.64), kind=kOutput, calls=%fused_computation.28 | convolution fusion | flops 134217728 | bytes 5234688 | tf_op jit(solution)/shard_map/conv_general_dilated | solution.py:308
  240.3 5.7 %copy.72 = f32[1,4096,128]{2,1,0:T(8,128)} copy(f32[1,4096,128]{1,0,2:T(1,128)} %fusion.14) | data formatting | bytes 4194304 | tf_op jit(solution)/shard_map/conv_general_dilated | solution.py:308
  245.9 30.1 %shard_map.104 = bf16[64,128]{1,0:T(8,128)(2,1)} custom-call(f32[8,4,2,64,128]{4,3,2,1,0:T(8,128)} %bitcast.188), custom_call_target="tpu_custom_call" | custom-call | tf_op jit(solution)/shard_map/pallas_call | solution.py:86
  279.3 30.1 %fusion.12 = f32[1,128,4096]{2,0,1:T(1,128)S(1)} fusion(bf16[1,255,4096]{2,1,0:T(8,128)(2,1)S(1)} %maximum_bitcast_fusion.16, bf16[128,1,4096]{2,0,1:T(8,128)(2,1)S(1)} %bitcast.185), kind=kOutput, calls=%fused_computation.26 | convolution fusion | flops 134217728 | bytes 5234688 | tf_op jit(solution)/shard_map/conv_general_dilated | solution.py:248
  309.5 2.8 fusion.40
  (80 shorter events, 25.9 us)
Async XLA Ops:
  0.6 17.2 %copy-start = (bf16[1,128,4096]{2,1,0:T(8,128)(2,1)S(1)}, bf16[1,128,4096]{2,1,0:T(8,128)(2,1)}, u32[]{:S(2)}) copy-start(bf16[1,128,4096]{2,1,0:T(8,128)(2,1)} %param.15) | copy-start | bytes 3145732
  3.8 16.5 %collective-permute-start.1 = (bf16[127,4096]{1,0:T(8,128)(2,1)}, bf16[127,4096]{1,0:T(8,128)(2,1)}, u32[]{:S(2)}, u32[]{:S(2)}) collective-permute-start(bf16[127,4096]{1,0:T(8,128)(2,1)} %slice_bitcast_fusion.1), channel_id=1, source_target_pairs={{0,1},{1,2},{2,3},{3,4},{4,5},{5,6},{6,7},{7,8},{8,9},{9,10},{10,1... | collective-permute-start | bytes 3121160 | tf_op jit(solution)/shard_map/ppermute | solution.py:184
  8.3 46.2 %collective-permute-start = (bf16[128,4096]{1,0:T(8,128)(2,1)}, bf16[128,4096]{1,0:T(8,128)(2,1)S(1)}, u32[]{:S(2)}, u32[]{:S(2)}) collective-permute-start(bf16[128,4096]{1,0:T(8,128)(2,1)} %bitcast), channel_id=1, source_target_pairs={{0,192},{64,0},{128,64},{192,128},{1,193},{65,1},{129,65},{193,129... | collective-permute-start | bytes 3145736 | tf_op jit(solution)/shard_map/ppermute | solution.py:178
  12.0 5.8 %copy-start.18 = (bf16[128,128]{1,0:T(8,128)(2,1)S(1)}, bf16[128,128]{1,0:T(8,128)(2,1)}, u32[]{:S(2)}) copy-start(bf16[128,128]{1,0:T(8,128)(2,1)} %rev.4) | copy-start | bytes 98308
  21.8 30.5 %copy-start.13 = (bf16[1,255,4096]{2,1,0:T(8,128)(2,1)}, bf16[1,255,4096]{2,1,0:T(8,128)(2,1)S(1)}, u32[]{:S(2)}) copy-start(bf16[1,255,4096]{2,1,0:T(8,128)(2,1)S(1)} %maximum_bitcast_fusion.13) | copy-start | bytes 6266884
  21.9 30.5 %copy-start.7 = (bf16[1,128,4096]{2,1,0:T(8,128)(2,1)S(1)}, bf16[1,128,4096]{2,1,0:T(8,128)(2,1)}, u32[]{:S(2)}) copy-start(bf16[1,128,4096]{2,1,0:T(8,128)(2,1)} %param.12) | copy-start | bytes 3145732
  21.9 30.5 %copy-start.9 = (bf16[1,128,4096]{2,1,0:T(8,128)(2,1)S(1)}, bf16[1,128,4096]{2,1,0:T(8,128)(2,1)}, u32[]{:S(2)}) copy-start(bf16[1,128,4096]{2,1,0:T(8,128)(2,1)} %param.9) | copy-start | bytes 3145732
  21.9 30.5 %copy-start.10 = (bf16[1,128,4096]{2,1,0:T(8,128)(2,1)S(1)}, bf16[1,128,4096]{2,1,0:T(8,128)(2,1)}, u32[]{:S(2)}) copy-start(bf16[1,128,4096]{2,1,0:T(8,128)(2,1)} %param.11) | copy-start | bytes 3145732
  54.5 66.9 %copy-start.5 = (bf16[128,4096]{1,0:T(8,128)(2,1)}, bf16[128,4096]{1,0:T(8,128)(2,1)S(1)}, u32[]{:S(2)}) copy-start(bf16[128,4096]{1,0:T(8,128)(2,1)S(1)} %collective-permute-done) | copy-start | bytes 3145732
  121.4 2.3 copy-start.16
  123.7 2.4 copy-start.12
  134.9 7.1 %copy-start.3 = (f32[64,1,128,128]{2,3,1,0:T(8,128)S(1)}, f32[64,1,128,128]{2,3,1,0:T(8,128)}, u32[]{:S(2)}) copy-start(f32[64,1,128,128]{2,3,1,0:T(8,128)} %get-tuple-element.19) | copy-start | bytes 12582916
  134.9 7.1 %copy-start.4 = (f32[64,1,128,128]{2,3,1,0:T(8,128)S(1)}, f32[64,1,128,128]{2,3,1,0:T(8,128)}, u32[]{:S(2)}) copy-start(f32[64,1,128,128]{2,3,1,0:T(8,128)} %get-tuple-element.20) | copy-start | bytes 12582916
  146.9 2.8 copy-start.22
  147.0 2.8 copy-start.23
  162.9 37.3 %all-to-all-start = ((bf16[64,64,128]{2,0,1:T(8,128)(2,1)}), bf16[64,64,128]{2,0,1:T(8,128)(2,1)S(1)}, u32[]{:S(2)}, u32[]{:S(2)}) async-start(bf16[64,64,128]{2,0,1:T(8,128)(2,1)} %copy.65), calls=%async_computation | async-start | bytes 2097152 | tf_op jit(solution)/shard_map/all_to_all | solution.py:300
  203.7 36.5 %copy-start.1 = (f32[4096,128]{0,1:T(8,128)}, f32[4096,128]{0,1:T(8,128)S(1)}, u32[]{:S(2)}) copy-start(f32[4096,128]{0,1:T(8,128)S(1)} %copy.66) | copy-start | bytes 6291460
  203.7 7.5 %copy-start.14 = (bf16[1,255,4096]{2,1,0:T(8,128)(2,1)S(1)}, bf16[1,255,4096]{2,1,0:T(8,128)(2,1)}, u32[]{:S(2)}) copy-start(bf16[1,255,4096]{2,1,0:T(8,128)(2,1)} %copy-done.13) | copy-start | bytes 6266884
  207.9 69.6 %collective-permute-start.2 = (bf16[127,4096]{1,0:T(8,128)(2,1)}, bf16[127,4096]{1,0:T(8,128)(2,1)}, u32[]{:S(2)}, u32[]{:S(2)}) collective-permute-start(bf16[127,4096]{1,0:T(8,128)(2,1)} %bitcast.184), channel_id=1, source_target_pairs={{1,0},{2,1},{3,2},{4,3},{5,4},{6,5},{7,6},{8,7},{9,8},{10,9},{11,1... | collective-permute-start | bytes 3121160 | tf_op jit(solution)/shard_map/ppermute | solution.py:184
  240.3 35.8 %copy-start.19 = (bf16[128,128]{1,0:T(8,128)(2,1)S(1)}, bf16[128,128]{1,0:T(8,128)(2,1)}, u32[]{:S(2)}) copy-start(bf16[128,128]{1,0:T(8,128)(2,1)} %rev.4) | copy-start | bytes 98308
  279.3 30.2 %copy-start.2 = (f32[4096,128]{0,1:T(8,128)S(1)}, f32[4096,128]{0,1:T(8,128)}, u32[]{:S(2)}) copy-start(f32[4096,128]{0,1:T(8,128)} %copy-done.1) | copy-start | bytes 6291460
  279.3 30.2 %copy-start.6 = (bf16[128,4096]{1,0:T(8,128)(2,1)S(1)}, bf16[128,4096]{1,0:T(8,128)(2,1)}, u32[]{:S(2)}) copy-start(bf16[128,4096]{1,0:T(8,128)(2,1)} %copy-done.5) | copy-start | bytes 3145732
  279.3 30.2 %copy-start.8 = (bf16[1,128,4096]{2,1,0:T(8,128)(2,1)S(1)}, bf16[1,128,4096]{2,1,0:T(8,128)(2,1)}, u32[]{:S(2)}) copy-start(bf16[1,128,4096]{2,1,0:T(8,128)(2,1)} %param.12) | copy-start | bytes 3145732
  279.3 30.2 %copy-start.11 = (bf16[1,128,4096]{2,1,0:T(8,128)(2,1)S(1)}, bf16[1,128,4096]{2,1,0:T(8,128)(2,1)}, u32[]{:S(2)}) copy-start(bf16[1,128,4096]{2,1,0:T(8,128)(2,1)} %param.10) | copy-start | bytes 3145732
  (4 other events, 8.3 us)

commit v7 on v5

--- a/solution.py
+++ b/solution.py
@@ -121,7 +121,9 @@
     for index in range(count):
         stage[index] = x_ref[index].astype(jnp.float32).T.astype(stage.dtype)
 
-        def start(k, carry, index=index):
+        def start(j, carry, index=index):
+            odd = j % 2
+            k = odd * ((j + 1) // 2) + (1 - odd) * (n - j // 2)
             copy(index, lax.rem(me + k, n), me).start()
             return carry
 

time: 317 us -> 317 us (level)
  no operation moved by 1% of the time
where the time goes in v7:
time: 317 us; the launch traced here: 313 us
  matrix products  118 us (37%)
  Pallas kernels  93.5 us (29%)
  other arithmetic  33.6 us (11%)
  waiting for transfers between devices  28.7 us (9%)
  starting transfers between devices  21.6 us (7%)
  local copies, waits for them, and re-layouts  16.2 us (5%)
    pallas_call x1, Pallas kernels, to_channels(): pl.pallas_call(functools.partial(channel_kernel, n), out_shape=jax.ShapeD...  63.4 us
    conv_general_dilated x2, matrix products, depthwise(): lax.conv_general_dilated(extended[None], kernel[:, None, :], (1,), 'VALID...  60.5 us
    pallas_call x1, Pallas kernels, tap_exchange(): pl.pallas_call(functools.partial(tap_exchange_kernel, nz, nx, nc, scale),...  30.1 us
    conv_general_dilated x1, matrix products, per_device(): lax.conv_general_dilated(extended[None], grad_b[:, None, :], (1,), 'VALID...  29.1 us
    all_to_all x1, waiting for transfers between devices, per_device(): lax.all_to_all(input_part.astype(jnp.bfloat16), 'ctx', split_axis=1, conc...  26.7 us
    dot_general x6, matrix products, contract(): jnp.einsum(form, left, right, precision=lax.Precision.HIGH, preferred_ele...  26.2 us
    all_to_all x1, starting transfers between devices, per_device(): lax.all_to_all(input_part.astype(jnp.bfloat16), 'ctx', split_axis=1, conc...  11.1 us
    ppermute x2, starting transfers between devices, shifted(): return lax.ppermute(array, axis, pairs)  7.75 us
  transfers between devices with their start and end apart: 4, of which 2 were waited for; matrix products, arithmetic and copies ran while one was open for 25% of the time, Pallas kernels for 10%

profile of v7, /device:TPU:1, one launch (start us, length us, event | category | flops | bytes accessed | tf_op | source)
XLA Modules:
  0.0 312.7 jit_solution(2005440273408090549)
XLA Ops:
  3.8 4.5 %collective-permute-start.1 = (bf16[127,4096]{1,0:T(8,128)(2,1)}, bf16[127,4096]{1,0:T(8,128)(2,1)}, u32[]{:S(2)}, u32[]{:S(2)}) collective-permute-start(bf16[127,4096]{1,0:T(8,128)(2,1)} %slice_bitcast_fusion.1), channel_id=1, source_target_pairs={{0,1},{1,2},{2,3},{3,4},{4,5},{5,6},{6,7},{7,8},{8,9},{9,10},{10,1... | collective-permute-start | bytes 3121160 | tf_op jit(solution)/shard_map/ppermute | solution.py:178
  8.3 2.8 collective-permute-start
  18.3 2.0 collective-permute-done.1
  21.9 30.4 %fusion.16 = f32[1,128,4096]{2,0,1:T(1,128)S(1)} fusion(bf16[1,255,4096]{2,1,0:T(8,128)(2,1)S(1)} %maximum_bitcast_fusion.13, bf16[128,1,4096]{2,0,1:T(8,128)(2,1)S(1)} %fusion.11), kind=kOutput, calls=%fused_computation.30 | convolution fusion | flops 134217728 | bytes 5234688 | tf_op jit(solution)/shard_map/conv_general_dilated | solution.py:242
  52.4 2.1 fusion.31
  56.4 63.4 %shard_map.103 = bf16[2,64,8192]{2,1,0:T(8,128)(2,1)} custom-call(bf16[2,128,4096]{2,1,0:T(8,128)(2,1)} %pad_maximum_fusion.x_ref), custom_call_target="tpu_custom_call" | custom-call | tf_op jit(solution)/shard_map/pallas_call | solution.py:154
  122.1 2.4 convolution_bitcast_fusion
  124.5 2.4 convolution_bitcast_fusion.1
  126.9 6.4 %multiply_subtract_fusion.3 = (f32[64,1,128,128]{2,3,1,0:T(8,128)S(1)}, f32[64,1,128,128]{2,3,1,0:T(8,128)}, f32[64,1,128,128]{2,3,1,0:T(8,128)}, f32[64,1,128,128]{2,3,1,0:T(8,128)}) fusion(f32[64,2,128,128]{2,3,1,0:T(8,128)S(1)} %convolution_bitcast_fusion, f32[128,128]{0,1:T(8,128)S(1)} %get-tuple-element.29, f32[128,128]{0,1:T(8,128)S(1)} %get-tuple-element.30, ...), kind=kLoop, calls=%fused_computation.25 | loop fusion | flops 12582912 | bytes 33685504 | tf_op jit(solution)/shard_map/sub | solution.py:211
  133.3 7.1 %fusion.22 = f32[64,2,128,128]{2,3,0,1:T(8,128)S(1)} fusion(f32[64,1,128,128]{2,3,1,0:T(8,128)} %get-tuple-element.8, f32[64,1,128,128]{2,3,1,0:T(8,128)S(1)} %get-tuple-element.7, f32[1,2,128,128]{2,3,0,1:T(8,128)S(1)} %get-tuple-element.16, f32[1,2,128,128]{2,3,0,1:T(8,128)S(1)} %get-tuple-element.21), kind=kOutput, calls=%fused_computation.35 | convolution fusion | flops 3223388160 | bytes 17039360 | tf_op jit(solution)/shard_map/nqcb,qpbd->npcd/dot_general | solution.py:189
  140.4 4.9 %fusion.21 = f32[64,2,128,128]{2,3,0,1:T(8,128)S(1)} fusion(f32[64,1,128,128]{2,3,1,0:T(8,128)S(1)} %copy-done.3, f32[64,1,128,128]{2,3,1,0:T(8,128)S(1)} %copy-done.4, f32[1,2,128,128]{2,3,0,1:T(8,128)S(1)} %get-tuple-element.16, f32[1,2,128,128]{2,3,0,1:T(8,128)S(1)} %get-tuple-element.21), kind=kOutput, calls=%fused_computation.34 | convolution fusion | flops 3223388160 | bytes 17039360 | tf_op jit(solution)/shard_map/nqcb,qpbd->npcd/dot_general | solution.py:189
  145.3 2.7 multiply_add_fusion.1
  148.1 5.0 %fusion.18 = f32[64,2,128,128]{2,3,1,0:T(8,128)S(1)} fusion(f32[64,1,128,128]{2,3,0,1:T(8,128)S(1)} %get-tuple-element.4, f32[64,1,128,128]{2,3,0,1:T(8,128)S(1)} %get-tuple-element.3, f32[1,2,128,128]{2,3,1,0:T(8,128)S(1)} %copy-done.23, f32[1,2,128,128]{2,3,1,0:T(8,128)S(1)} %copy-done.22), kind=kOutput, calls=%fused_computation.32 | convolution fusion | flops 3223388160 | bytes 17039360 | tf_op jit(solution)/shard_map/npcd,pqdb->nqcb/dot_general | solution.py:189
  155.0 4.4 %fusion.38 = bf16[64,2,64,128]{3,2,1,0:T(8,128)(2,1)S(1)} fusion(f32[64,1,128,128]{2,3,1,0:T(8,128)S(1)} %get-tuple-element.6, f32[64,1,128,128]{2,3,1,0:T(8,128)S(1)} %get-tuple-element.5, f32[1,2,64,128]{3,2,1,0:T(8,128)S(1)} %copy-done.21, f32[1,2,64,128]{3,2,1,0:T(8,128)S(1)} %copy-done.20), kind=kOutput, calls=%fused_computation.66 | convolution fusion | flops 1613791232 | bytes 10616832 | tf_op jit(solution)/shard_map/rqac,nqcb->nrab/dot_general | solution.py:189
  161.3 11.1 %all-to-all-start = ((bf16[64,64,128]{2,0,1:T(8,128)(2,1)}), bf16[64,64,128]{2,0,1:T(8,128)(2,1)S(1)}, u32[]{:S(2)}, u32[]{:S(2)}) async-start(bf16[64,64,128]{2,0,1:T(8,128)(2,1)} %copy.65), calls=%async_computation | async-start | bytes 2097152 | tf_op jit(solution)/shard_map/all_to_all | solution.py:294
  173.6 26.7 %all-to-all-done = bf16[64,64,128]{2,0,1:T(8,128)(2,1)S(1)} async-done(((bf16[64,64,128]{2,0,1:T(8,128)(2,1)}), bf16[64,64,128]{2,0,1:T(8,128)(2,1)S(1)}, u32[]{:S(2)}, u32[]{:S(2)}) %all-to-all-start) | async-done | bytes 1048608 | tf_op jit(solution)/shard_map/all_to_all | solution.py:294
  201.9 1.9 copy.66
  203.9 4.2 %fusion.30 = bf16[128,4096]{1,0:T(8,128)(2,1)} fusion(bf16[1,128,4096]{2,1,0:T(8,128)(2,1)} %param.11, bf16[1,128,4096]{2,1,0:T(8,128)(2,1)} %param.12, f32[4096,128]{0,1:T(8,128)S(1)} %copy.66, bf16[128,4096]{1,0:T(8,128)(2,1)} %copy-done.5), kind=kLoop, calls=%fused_computation.53 | loop fusion | flops 4194304 | bytes 6291456 | tf_op jit(solution)/shard_map/convert_element_type | solution.py:298
  208.1 3.3 %collective-permute-start.2 = (bf16[127,4096]{1,0:T(8,128)(2,1)}, bf16[127,4096]{1,0:T(8,128)(2,1)}, u32[]{:S(2)}, u32[]{:S(2)}) collective-permute-start(bf16[127,4096]{1,0:T(8,128)(2,1)} %bitcast.184), channel_id=1, source_target_pairs={{1,0},{2,1},{3,2},{4,3},{5,4},{6,5},{7,6},{8,7},{9,8},{10,9},{11,1... | collective-permute-start | bytes 3121160 | tf_op jit(solution)/shard_map/ppermute | solution.py:178
  211.4 29.1 %fusion.14 = f32[1,4096,128]{1,0,2:T(1,128)} fusion(bf16[1,255,4096]{2,1,0:T(8,128)(2,1)S(1)} %copy-done.14, bf16[128,1,4096]{2,0,1:T(8,128)(2,1)} %bitcast.64), kind=kOutput, calls=%fused_computation.28 | convolution fusion | flops 134217728 | bytes 5234688 | tf_op jit(solution)/shard_map/conv_general_dilated | solution.py:302
  240.4 5.7 %copy.72 = f32[1,4096,128]{2,1,0:T(8,128)} copy(f32[1,4096,128]{1,0,2:T(1,128)} %fusion.14) | data formatting | bytes 4194304 | tf_op jit(solution)/shard_map/conv_general_dilated | solution.py:302
  246.1 30.1 %shard_map.104 = bf16[64,128]{1,0:T(8,128)(2,1)} custom-call(f32[8,4,2,64,128]{4,3,2,1,0:T(8,128)} %bitcast.188), custom_call_target="tpu_custom_call" | custom-call | tf_op jit(solution)/shard_map/pallas_call | solution.py:78
  279.5 30.1 %fusion.12 = f32[1,128,4096]{2,0,1:T(1,128)S(1)} fusion(bf16[1,255,4096]{2,1,0:T(8,128)(2,1)S(1)} %maximum_bitcast_fusion.16, bf16[128,1,4096]{2,0,1:T(8,128)(2,1)S(1)} %bitcast.185), kind=kOutput, calls=%fused_computation.26 | convolution fusion | flops 134217728 | bytes 5234688 | tf_op jit(solution)/shard_map/conv_general_dilated | solution.py:242
  309.6 2.8 fusion.40
  (80 shorter events, 25.9 us)
Async XLA Ops:
  0.6 17.2 %copy-start = (bf16[1,128,4096]{2,1,0:T(8,128)(2,1)S(1)}, bf16[1,128,4096]{2,1,0:T(8,128)(2,1)}, u32[]{:S(2)}) copy-start(bf16[1,128,4096]{2,1,0:T(8,128)(2,1)} %param.15) | copy-start | bytes 3145732
  3.8 16.5 %collective-permute-start.1 = (bf16[127,4096]{1,0:T(8,128)(2,1)}, bf16[127,4096]{1,0:T(8,128)(2,1)}, u32[]{:S(2)}, u32[]{:S(2)}) collective-permute-start(bf16[127,4096]{1,0:T(8,128)(2,1)} %slice_bitcast_fusion.1), channel_id=1, source_target_pairs={{0,1},{1,2},{2,3},{3,4},{4,5},{5,6},{6,7},{7,8},{8,9},{9,10},{10,1... | collective-permute-start | bytes 3121160 | tf_op jit(solution)/shard_map/ppermute | solution.py:178
  8.3 46.2 %collective-permute-start = (bf16[128,4096]{1,0:T(8,128)(2,1)}, bf16[128,4096]{1,0:T(8,128)(2,1)S(1)}, u32[]{:S(2)}, u32[]{:S(2)}) collective-permute-start(bf16[128,4096]{1,0:T(8,128)(2,1)} %bitcast), channel_id=1, source_target_pairs={{0,192},{64,0},{128,64},{192,128},{1,193},{65,1},{129,65},{193,129... | collective-permute-start | bytes 3145736 | tf_op jit(solution)/shard_map/ppermute | solution.py:172
  12.0 5.8 %copy-start.18 = (bf16[128,128]{1,0:T(8,128)(2,1)S(1)}, bf16[128,128]{1,0:T(8,128)(2,1)}, u32[]{:S(2)}) copy-start(bf16[128,128]{1,0:T(8,128)(2,1)} %rev.4) | copy-start | bytes 98308
  21.8 30.5 %copy-start.13 = (bf16[1,255,4096]{2,1,0:T(8,128)(2,1)}, bf16[1,255,4096]{2,1,0:T(8,128)(2,1)S(1)}, u32[]{:S(2)}) copy-start(bf16[1,255,4096]{2,1,0:T(8,128)(2,1)S(1)} %maximum_bitcast_fusion.13) | copy-start | bytes 6266884
  21.9 30.5 %copy-start.7 = (bf16[1,128,4096]{2,1,0:T(8,128)(2,1)S(1)}, bf16[1,128,4096]{2,1,0:T(8,128)(2,1)}, u32[]{:S(2)}) copy-start(bf16[1,128,4096]{2,1,0:T(8,128)(2,1)} %param.12) | copy-start | bytes 3145732
  21.9 30.5 %copy-start.9 = (bf16[1,128,4096]{2,1,0:T(8,128)(2,1)S(1)}, bf16[1,128,4096]{2,1,0:T(8,128)(2,1)}, u32[]{:S(2)}) copy-start(bf16[1,128,4096]{2,1,0:T(8,128)(2,1)} %param.9) | copy-start | bytes 3145732
  21.9 30.5 %copy-start.10 = (bf16[1,128,4096]{2,1,0:T(8,128)(2,1)S(1)}, bf16[1,128,4096]{2,1,0:T(8,128)(2,1)}, u32[]{:S(2)}) copy-start(bf16[1,128,4096]{2,1,0:T(8,128)(2,1)} %param.11) | copy-start | bytes 3145732
  54.5 65.2 %copy-start.5 = (bf16[128,4096]{1,0:T(8,128)(2,1)}, bf16[128,4096]{1,0:T(8,128)(2,1)S(1)}, u32[]{:S(2)}) copy-start(bf16[128,4096]{1,0:T(8,128)(2,1)S(1)} %collective-permute-done) | copy-start | bytes 3145732
  119.7 2.3 copy-start.16
  122.1 2.4 copy-start.12
  133.2 7.1 %copy-start.3 = (f32[64,1,128,128]{2,3,1,0:T(8,128)S(1)}, f32[64,1,128,128]{2,3,1,0:T(8,128)}, u32[]{:S(2)}) copy-start(f32[64,1,128,128]{2,3,1,0:T(8,128)} %get-tuple-element.19) | copy-start | bytes 12582916
  133.3 7.1 %copy-start.4 = (f32[64,1,128,128]{2,3,1,0:T(8,128)S(1)}, f32[64,1,128,128]{2,3,1,0:T(8,128)}, u32[]{:S(2)}) copy-start(f32[64,1,128,128]{2,3,1,0:T(8,128)} %get-tuple-element.20) | copy-start | bytes 12582916
  145.3 2.8 copy-start.22
  145.3 2.8 copy-start.23
  161.3 39.1 %all-to-all-start = ((bf16[64,64,128]{2,0,1:T(8,128)(2,1)}), bf16[64,64,128]{2,0,1:T(8,128)(2,1)S(1)}, u32[]{:S(2)}, u32[]{:S(2)}) async-start(bf16[64,64,128]{2,0,1:T(8,128)(2,1)} %copy.65), calls=%async_computation | async-start | bytes 2097152 | tf_op jit(solution)/shard_map/all_to_all | solution.py:294
  203.9 36.5 %copy-start.1 = (f32[4096,128]{0,1:T(8,128)}, f32[4096,128]{0,1:T(8,128)S(1)}, u32[]{:S(2)}) copy-start(f32[4096,128]{0,1:T(8,128)S(1)} %copy.66) | copy-start | bytes 6291460
  203.9 7.5 %copy-start.14 = (bf16[1,255,4096]{2,1,0:T(8,128)(2,1)S(1)}, bf16[1,255,4096]{2,1,0:T(8,128)(2,1)}, u32[]{:S(2)}) copy-start(bf16[1,255,4096]{2,1,0:T(8,128)(2,1)} %copy-done.13) | copy-start | bytes 6266884
  208.1 69.6 %collective-permute-start.2 = (bf16[127,4096]{1,0:T(8,128)(2,1)}, bf16[127,4096]{1,0:T(8,128)(2,1)}, u32[]{:S(2)}, u32[]{:S(2)}) collective-permute-start(bf16[127,4096]{1,0:T(8,128)(2,1)} %bitcast.184), channel_id=1, source_target_pairs={{1,0},{2,1},{3,2},{4,3},{5,4},{6,5},{7,6},{8,7},{9,8},{10,9},{11,1... | collective-permute-start | bytes 3121160 | tf_op jit(solution)/shard_map/ppermute | solution.py:178
  240.4 35.8 %copy-start.19 = (bf16[128,128]{1,0:T(8,128)(2,1)S(1)}, bf16[128,128]{1,0:T(8,128)(2,1)}, u32[]{:S(2)}) copy-start(bf16[128,128]{1,0:T(8,128)(2,1)} %rev.4) | copy-start | bytes 98308
  279.4 30.2 %copy-start.2 = (f32[4096,128]{0,1:T(8,128)S(1)}, f32[4096,128]{0,1:T(8,128)}, u32[]{:S(2)}) copy-start(f32[4096,128]{0,1:T(8,128)} %copy-done.1) | copy-start | bytes 6291460
  279.5 30.2 %copy-start.6 = (bf16[128,4096]{1,0:T(8,128)(2,1)S(1)}, bf16[128,4096]{1,0:T(8,128)(2,1)}, u32[]{:S(2)}) copy-start(bf16[128,4096]{1,0:T(8,128)(2,1)} %copy-done.5) | copy-start | bytes 3145732
  279.5 30.2 %copy-start.8 = (bf16[1,128,4096]{2,1,0:T(8,128)(2,1)S(1)}, bf16[1,128,4096]{2,1,0:T(8,128)(2,1)}, u32[]{:S(2)}) copy-start(bf16[1,128,4096]{2,1,0:T(8,128)(2,1)} %param.12) | copy-start | bytes 3145732
  279.5 30.2 %copy-start.11 = (bf16[1,128,4096]{2,1,0:T(8,128)(2,1)S(1)}, bf16[1,128,4096]{2,1,0:T(8,128)(2,1)}, u32[]{:S(2)}) copy-start(bf16[1,128,4096]{2,1,0:T(8,128)(2,1)} %param.10) | copy-start | bytes 3145732
  (4 other events, 8.3 us)

commit v8 on v5

--- a/solution.py
+++ b/solution.py
@@ -11,7 +11,7 @@
 MESH_IDS = pl.DeviceIdType.MESH
 
 
-def tap_exchange_kernel(nz, nx, nc, scale, x_ref, o_ref, r1, s1, r2, s2, r3, sems):
+def tap_exchange_kernel(nz, nx, nc, scale, x_ref, o_ref, r1, s1, r2, s2, r3, mine, local_sem, sems):
     me = lax.axis_index("ctx")
     sec = lax.axis_index("section")
     core = me % nc
@@ -41,8 +41,11 @@
 
     first = send(x_ref.at[:, :, 1 - core], r1, peers[0], 0, 0)
     first.start()
+    local = pltpu.make_async_copy(x_ref.at[:, :, core], mine, local_sem)
+    local.start()
+    local.wait()
     first.wait()
-    s1[...] = x_ref[:, :, core] + r1[...]
+    s1[...] = mine[...] + r1[...]
 
     second = []
     for k in range(1, nx):
@@ -78,7 +81,7 @@
     return pl.pallas_call(
         functools.partial(tap_exchange_kernel, nz, nx, nc, scale),
         out_shape=jax.ShapeDtypeStruct((taps, width), jnp.bfloat16),
-        in_specs=[pl.BlockSpec(memory_space=pltpu.VMEM)],
+        in_specs=[pl.BlockSpec(memory_space=pl.ANY)],
         out_specs=pl.BlockSpec(memory_space=pltpu.VMEM),
         scratch_shapes=[
             pltpu.VMEM((nz, nx, taps, width), jnp.float32),
@@ -86,6 +89,8 @@
             pltpu.VMEM((nx, nz, taps, width), jnp.float32),
             pltpu.VMEM((nz, taps, width), jnp.float32),
             pltpu.VMEM((nz, taps, width), jnp.float32),
+            pltpu.VMEM((nz, nx, taps, width), jnp.float32),
+            pltpu.SemaphoreType.DMA(()),
             pltpu.SemaphoreType.DMA((2, 1 + nx + nz)),
         ],
         compiler_params=pltpu.CompilerParams(collective_id=0, has_side_effects=True),

time: 317 us -> 315 us (level)
  transfers between devices with their start and end apart: 4 -> 4, of which waited for: 2 -> 2; matrix products, arithmetic and copies ran while one was open for 25% -> 25% of each run, Pallas kernels for 10% -> 9%
where the time goes in v8:
time: 315 us; the launch traced here: 311 us
  matrix products  118 us (37%)
  Pallas kernels  93.8 us (30%)
  other arithmetic  33.6 us (11%)
  waiting for transfers between devices  28.7 us (9%)
  starting transfers between devices  19.8 us (6%)
  local copies, waits for them, and re-layouts  16.2 us (5%)
    pallas_call x1, Pallas kernels, to_channels(): pl.pallas_call(functools.partial(channel_kernel, n), out_shape=jax.ShapeD...  65 us
    conv_general_dilated x2, matrix products, depthwise(): lax.conv_general_dilated(extended[None], kernel[:, None, :], (1,), 'VALID...  60.5 us
    conv_general_dilated x1, matrix products, per_device(): lax.conv_general_dilated(extended[None], grad_b[:, None, :], (1,), 'VALID...  29.1 us
    pallas_call x1, Pallas kernels, tap_exchange(): pl.pallas_call(functools.partial(tap_exchange_kernel, nz, nx, nc, scale),...  28.7 us
    all_to_all x1, waiting for transfers between devices, per_device(): lax.all_to_all(input_part.astype(jnp.bfloat16), 'ctx', split_axis=1, conc...  26.7 us
    dot_general x6, matrix products, contract(): jnp.einsum(form, left, right, precision=lax.Precision.HIGH, preferred_ele...  26.1 us
    all_to_all x1, starting transfers between devices, per_device(): lax.all_to_all(input_part.astype(jnp.bfloat16), 'ctx', split_axis=1, conc...  9.26 us
    ppermute x2, starting transfers between devices, shifted(): return lax.ppermute(array, axis, pairs)  7.75 us
  transfers between devices with their start and end apart: 4, of which 2 were waited for; matrix products, arithmetic and copies ran while one was open for 25% of the time, Pallas kernels for 9%

profile of v8, /device:TPU:1, one launch (start us, length us, event | category | flops | bytes accessed | tf_op | source)
XLA Modules:
  0.0 311.2 jit_solution(10315050100716793023)
XLA Ops:
  3.8 4.5 %collective-permute-start.1 = (bf16[127,4096]{1,0:T(8,128)(2,1)}, bf16[127,4096]{1,0:T(8,128)(2,1)}, u32[]{:S(2)}, u32[]{:S(2)}) collective-permute-start(bf16[127,4096]{1,0:T(8,128)(2,1)} %slice_bitcast_fusion.1), channel_id=1, source_target_pairs={{0,1},{1,2},{2,3},{3,4},{4,5},{5,6},{6,7},{7,8},{8,9},{9,10},{10,1... | collective-permute-start | bytes 3121160 | tf_op jit(solution)/shard_map/ppermute | solution.py:181
  8.3 2.8 collective-permute-start
  18.3 2.0 collective-permute-done.1
  21.9 30.4 %fusion.16 = f32[1,128,4096]{2,0,1:T(1,128)S(1)} fusion(bf16[1,255,4096]{2,1,0:T(8,128)(2,1)S(1)} %maximum_bitcast_fusion.13, bf16[128,1,4096]{2,0,1:T(8,128)(2,1)S(1)} %fusion.11), kind=kOutput, calls=%fused_computation.30 | convolution fusion | flops 134217728 | bytes 5234688 | tf_op jit(solution)/shard_map/conv_general_dilated | solution.py:245
  52.4 2.1 fusion.31
  56.4 65.0 %shard_map.103 = bf16[2,64,8192]{2,1,0:T(8,128)(2,1)} custom-call(bf16[2,128,4096]{2,1,0:T(8,128)(2,1)} %pad_maximum_fusion.x_ref), custom_call_target="tpu_custom_call" | custom-call | tf_op jit(solution)/shard_map/pallas_call | solution.py:157
  123.8 2.4 convolution_bitcast_fusion
  126.1 2.4 convolution_bitcast_fusion.1
  128.5 6.4 %multiply_subtract_fusion.3 = (f32[64,1,128,128]{2,3,1,0:T(8,128)S(1)}, f32[64,1,128,128]{2,3,1,0:T(8,128)}, f32[64,1,128,128]{2,3,1,0:T(8,128)}, f32[64,1,128,128]{2,3,1,0:T(8,128)}) fusion(f32[64,2,128,128]{2,3,1,0:T(8,128)S(1)} %convolution_bitcast_fusion, f32[128,128]{0,1:T(8,128)S(1)} %get-tuple-element.29, f32[128,128]{0,1:T(8,128)S(1)} %get-tuple-element.30, ...), kind=kLoop, calls=%fused_computation.25 | loop fusion | flops 12582912 | bytes 33685504 | tf_op jit(solution)/shard_map/sub | solution.py:214
  134.9 7.1 %fusion.22 = f32[64,2,128,128]{2,3,0,1:T(8,128)S(1)} fusion(f32[64,1,128,128]{2,3,1,0:T(8,128)} %get-tuple-element.8, f32[64,1,128,128]{2,3,1,0:T(8,128)S(1)} %get-tuple-element.7, f32[1,2,128,128]{2,3,0,1:T(8,128)S(1)} %get-tuple-element.16, f32[1,2,128,128]{2,3,0,1:T(8,128)S(1)} %get-tuple-element.21), kind=kOutput, calls=%fused_computation.35 | convolution fusion | flops 3223388160 | bytes 17039360 | tf_op jit(solution)/shard_map/nqcb,qpbd->npcd/dot_general | solution.py:192
  142.0 4.9 %fusion.21 = f32[64,2,128,128]{2,3,0,1:T(8,128)S(1)} fusion(f32[64,1,128,128]{2,3,1,0:T(8,128)S(1)} %copy-done.3, f32[64,1,128,128]{2,3,1,0:T(8,128)S(1)} %copy-done.4, f32[1,2,128,128]{2,3,0,1:T(8,128)S(1)} %get-tuple-element.16, f32[1,2,128,128]{2,3,0,1:T(8,128)S(1)} %get-tuple-element.21), kind=kOutput, calls=%fused_computation.34 | convolution fusion | flops 3223388160 | bytes 17039360 | tf_op jit(solution)/shard_map/nqcb,qpbd->npcd/dot_general | solution.py:192
  147.0 2.7 multiply_add_fusion.1
  149.7 5.0 %fusion.18 = f32[64,2,128,128]{2,3,1,0:T(8,128)S(1)} fusion(f32[64,1,128,128]{2,3,0,1:T(8,128)S(1)} %get-tuple-element.4, f32[64,1,128,128]{2,3,0,1:T(8,128)S(1)} %get-tuple-element.3, f32[1,2,128,128]{2,3,1,0:T(8,128)S(1)} %copy-done.23, f32[1,2,128,128]{2,3,1,0:T(8,128)S(1)} %copy-done.22), kind=kOutput, calls=%fused_computation.32 | convolution fusion | flops 3223388160 | bytes 17039360 | tf_op jit(solution)/shard_map/npcd,pqdb->nqcb/dot_general | solution.py:192
  156.7 4.4 %fusion.38 = bf16[64,2,64,128]{3,2,1,0:T(8,128)(2,1)S(1)} fusion(f32[64,1,128,128]{2,3,1,0:T(8,128)S(1)} %get-tuple-element.6, f32[64,1,128,128]{2,3,1,0:T(8,128)S(1)} %get-tuple-element.5, f32[1,2,64,128]{3,2,1,0:T(8,128)S(1)} %copy-done.21, f32[1,2,64,128]{3,2,1,0:T(8,128)S(1)} %copy-done.20), kind=kOutput, calls=%fused_computation.66 | convolution fusion | flops 1613791232 | bytes 10616832 | tf_op jit(solution)/shard_map/rqac,nqcb->nrab/dot_general | solution.py:192
  162.9 9.3 %all-to-all-start = ((bf16[64,64,128]{2,0,1:T(8,128)(2,1)}), bf16[64,64,128]{2,0,1:T(8,128)(2,1)S(1)}, u32[]{:S(2)}, u32[]{:S(2)}) async-start(bf16[64,64,128]{2,0,1:T(8,128)(2,1)} %copy.65), calls=%async_computation | async-start | bytes 2097152 | tf_op jit(solution)/shard_map/all_to_all | solution.py:297
  173.5 26.7 %all-to-all-done = bf16[64,64,128]{2,0,1:T(8,128)(2,1)S(1)} async-done(((bf16[64,64,128]{2,0,1:T(8,128)(2,1)}), bf16[64,64,128]{2,0,1:T(8,128)(2,1)S(1)}, u32[]{:S(2)}, u32[]{:S(2)}) %all-to-all-start) | async-done | bytes 1048608 | tf_op jit(solution)/shard_map/all_to_all | solution.py:297
  201.8 1.9 copy.66
  203.7 4.2 %fusion.30 = bf16[128,4096]{1,0:T(8,128)(2,1)} fusion(bf16[1,128,4096]{2,1,0:T(8,128)(2,1)} %param.11, bf16[1,128,4096]{2,1,0:T(8,128)(2,1)} %param.12, f32[4096,128]{0,1:T(8,128)S(1)} %copy.66, bf16[128,4096]{1,0:T(8,128)(2,1)} %copy-done.5), kind=kLoop, calls=%fused_computation.53 | loop fusion | flops 4194304 | bytes 6291456 | tf_op jit(solution)/shard_map/convert_element_type | solution.py:301
  207.9 3.3 %collective-permute-start.2 = (bf16[127,4096]{1,0:T(8,128)(2,1)}, bf16[127,4096]{1,0:T(8,128)(2,1)}, u32[]{:S(2)}, u32[]{:S(2)}) collective-permute-start(bf16[127,4096]{1,0:T(8,128)(2,1)} %bitcast.184), channel_id=1, source_target_pairs={{1,0},{2,1},{3,2},{4,3},{5,4},{6,5},{7,6},{8,7},{9,8},{10,9},{11,1... | collective-permute-start | bytes 3121160 | tf_op jit(solution)/shard_map/ppermute | solution.py:181
  211.2 29.1 %fusion.14 = f32[1,4096,128]{1,0,2:T(1,128)} fusion(bf16[1,255,4096]{2,1,0:T(8,128)(2,1)S(1)} %copy-done.14, bf16[128,1,4096]{2,0,1:T(8,128)(2,1)} %bitcast.64), kind=kOutput, calls=%fused_computation.28 | convolution fusion | flops 134217728 | bytes 5234688 | tf_op jit(solution)/shard_map/conv_general_dilated | solution.py:305
  240.3 5.7 %copy.72 = f32[1,4096,128]{2,1,0:T(8,128)} copy(f32[1,4096,128]{1,0,2:T(1,128)} %fusion.14) | data formatting | bytes 4194304 | tf_op jit(solution)/shard_map/conv_general_dilated | solution.py:305
  245.9 28.7 %shard_map.104 = bf16[64,128]{1,0:T(8,128)(2,1)} custom-call(f32[8,4,2,64,128]{4,3,2,1,0:T(8,128)} %bitcast.188), custom_call_target="tpu_custom_call" | custom-call | tf_op jit(solution)/shard_map/pallas_call | solution.py:81
  278.0 30.1 %fusion.12 = f32[1,128,4096]{2,0,1:T(1,128)S(1)} fusion(bf16[1,255,4096]{2,1,0:T(8,128)(2,1)S(1)} %maximum_bitcast_fusion.16, bf16[128,1,4096]{2,0,1:T(8,128)(2,1)S(1)} %bitcast.185), kind=kOutput, calls=%fused_computation.26 | convolution fusion | flops 134217728 | bytes 5234688 | tf_op jit(solution)/shard_map/conv_general_dilated | solution.py:245
  308.1 2.8 fusion.40
  (80 shorter events, 25.9 us)
Async XLA Ops:
  0.6 17.2 %copy-start = (bf16[1,128,4096]{2,1,0:T(8,128)(2,1)S(1)}, bf16[1,128,4096]{2,1,0:T(8,128)(2,1)}, u32[]{:S(2)}) copy-start(bf16[1,128,4096]{2,1,0:T(8,128)(2,1)} %param.15) | copy-start | bytes 3145732
  3.8 16.5 %collective-permute-start.1 = (bf16[127,4096]{1,0:T(8,128)(2,1)}, bf16[127,4096]{1,0:T(8,128)(2,1)}, u32[]{:S(2)}, u32[]{:S(2)}) collective-permute-start(bf16[127,4096]{1,0:T(8,128)(2,1)} %slice_bitcast_fusion.1), channel_id=1, source_target_pairs={{0,1},{1,2},{2,3},{3,4},{4,5},{5,6},{6,7},{7,8},{8,9},{9,10},{10,1... | collective-permute-start | bytes 3121160 | tf_op jit(solution)/shard_map/ppermute | solution.py:181
  8.3 46.2 %collective-permute-start = (bf16[128,4096]{1,0:T(8,128)(2,1)}, bf16[128,4096]{1,0:T(8,128)(2,1)S(1)}, u32[]{:S(2)}, u32[]{:S(2)}) collective-permute-start(bf16[128,4096]{1,0:T(8,128)(2,1)} %bitcast), channel_id=1, source_target_pairs={{0,192},{64,0},{128,64},{192,128},{1,193},{65,1},{129,65},{193,129... | collective-permute-start | bytes 3145736 | tf_op jit(solution)/shard_map/ppermute | solution.py:175
  12.0 5.8 %copy-start.18 = (bf16[128,128]{1,0:T(8,128)(2,1)S(1)}, bf16[128,128]{1,0:T(8,128)(2,1)}, u32[]{:S(2)}) copy-start(bf16[128,128]{1,0:T(8,128)(2,1)} %rev.4) | copy-start | bytes 98308
  21.8 30.5 %copy-start.13 = (bf16[1,255,4096]{2,1,0:T(8,128)(2,1)}, bf16[1,255,4096]{2,1,0:T(8,128)(2,1)S(1)}, u32[]{:S(2)}) copy-start(bf16[1,255,4096]{2,1,0:T(8,128)(2,1)S(1)} %maximum_bitcast_fusion.13) | copy-start | bytes 6266884
  21.9 30.5 %copy-start.7 = (bf16[1,128,4096]{2,1,0:T(8,128)(2,1)S(1)}, bf16[1,128,4096]{2,1,0:T(8,128)(2,1)}, u32[]{:S(2)}) copy-start(bf16[1,128,4096]{2,1,0:T(8,128)(2,1)} %param.12) | copy-start | bytes 3145732
  21.9 30.5 %copy-start.9 = (bf16[1,128,4096]{2,1,0:T(8,128)(2,1)S(1)}, bf16[1,128,4096]{2,1,0:T(8,128)(2,1)}, u32[]{:S(2)}) copy-start(bf16[1,128,4096]{2,1,0:T(8,128)(2,1)} %param.9) | copy-start | bytes 3145732
  21.9 30.5 %copy-start.10 = (bf16[1,128,4096]{2,1,0:T(8,128)(2,1)S(1)}, bf16[1,128,4096]{2,1,0:T(8,128)(2,1)}, u32[]{:S(2)}) copy-start(bf16[1,128,4096]{2,1,0:T(8,128)(2,1)} %param.11) | copy-start | bytes 3145732
  54.5 66.9 %copy-start.5 = (bf16[128,4096]{1,0:T(8,128)(2,1)}, bf16[128,4096]{1,0:T(8,128)(2,1)S(1)}, u32[]{:S(2)}) copy-start(bf16[128,4096]{1,0:T(8,128)(2,1)S(1)} %collective-permute-done) | copy-start | bytes 3145732
  121.4 2.3 copy-start.16
  123.7 2.4 copy-start.12
  134.9 7.1 %copy-start.3 = (f32[64,1,128,128]{2,3,1,0:T(8,128)S(1)}, f32[64,1,128,128]{2,3,1,0:T(8,128)}, u32[]{:S(2)}) copy-start(f32[64,1,128,128]{2,3,1,0:T(8,128)} %get-tuple-element.19) | copy-start | bytes 12582916
  134.9 7.1 %copy-start.4 = (f32[64,1,128,128]{2,3,1,0:T(8,128)S(1)}, f32[64,1,128,128]{2,3,1,0:T(8,128)}, u32[]{:S(2)}) copy-start(f32[64,1,128,128]{2,3,1,0:T(8,128)} %get-tuple-element.20) | copy-start | bytes 12582916
  146.9 2.8 copy-start.22
  147.0 2.8 copy-start.23
  162.9 37.3 %all-to-all-start = ((bf16[64,64,128]{2,0,1:T(8,128)(2,1)}), bf16[64,64,128]{2,0,1:T(8,128)(2,1)S(1)}, u32[]{:S(2)}, u32[]{:S(2)}) async-start(bf16[64,64,128]{2,0,1:T(8,128)(2,1)} %copy.65), calls=%async_computation | async-start | bytes 2097152 | tf_op jit(solution)/shard_map/all_to_all | solution.py:297
  203.7 36.5 %copy-start.1 = (f32[4096,128]{0,1:T(8,128)}, f32[4096,128]{0,1:T(8,128)S(1)}, u32[]{:S(2)}) copy-start(f32[4096,128]{0,1:T(8,128)S(1)} %copy.66) | copy-start | bytes 6291460
  203.7 7.5 %copy-start.14 = (bf16[1,255,4096]{2,1,0:T(8,128)(2,1)S(1)}, bf16[1,255,4096]{2,1,0:T(8,128)(2,1)}, u32[]{:S(2)}) copy-start(bf16[1,255,4096]{2,1,0:T(8,128)(2,1)} %copy-done.13) | copy-start | bytes 6266884
  207.9 68.2 %collective-permute-start.2 = (bf16[127,4096]{1,0:T(8,128)(2,1)}, bf16[127,4096]{1,0:T(8,128)(2,1)}, u32[]{:S(2)}, u32[]{:S(2)}) collective-permute-start(bf16[127,4096]{1,0:T(8,128)(2,1)} %bitcast.184), channel_id=1, source_target_pairs={{1,0},{2,1},{3,2},{4,3},{5,4},{6,5},{7,6},{8,7},{9,8},{10,9},{11,1... | collective-permute-start | bytes 3121160 | tf_op jit(solution)/shard_map/ppermute | solution.py:181
  240.3 34.4 %copy-start.19 = (bf16[128,128]{1,0:T(8,128)(2,1)S(1)}, bf16[128,128]{1,0:T(8,128)(2,1)}, u32[]{:S(2)}) copy-start(bf16[128,128]{1,0:T(8,128)(2,1)} %rev.4) | copy-start | bytes 98308
  277.9 30.2 %copy-start.2 = (f32[4096,128]{0,1:T(8,128)S(1)}, f32[4096,128]{0,1:T(8,128)}, u32[]{:S(2)}) copy-start(f32[4096,128]{0,1:T(8,128)} %copy-done.1) | copy-start | bytes 6291460
  277.9 30.2 %copy-start.6 = (bf16[128,4096]{1,0:T(8,128)(2,1)S(1)}, bf16[128,4096]{1,0:T(8,128)(2,1)}, u32[]{:S(2)}) copy-start(bf16[128,4096]{1,0:T(8,128)(2,1)} %copy-done.5) | copy-start | bytes 3145732
  278.0 30.2 %copy-start.8 = (bf16[1,128,4096]{2,1,0:T(8,128)(2,1)S(1)}, bf16[1,128,4096]{2,1,0:T(8,128)(2,1)}, u32[]{:S(2)}) copy-start(bf16[1,128,4096]{2,1,0:T(8,128)(2,1)} %param.12) | copy-start | bytes 3145732
  278.0 30.2 %copy-start.11 = (bf16[1,128,4096]{2,1,0:T(8,128)(2,1)S(1)}, bf16[1,128,4096]{2,1,0:T(8,128)(2,1)}, u32[]{:S(2)}) copy-start(bf16[1,128,4096]{2,1,0:T(8,128)(2,1)} %param.10) | copy-start | bytes 3145732
  (4 other events, 8.3 us)

commit v9 on v8

--- a/solution.py
+++ b/solution.py
@@ -158,7 +158,7 @@
         functools.partial(channel_kernel, n),
         out_shape=jax.ShapeDtypeStruct((count, channels // n, tokens * n), x.dtype),
         in_specs=[pl.BlockSpec(memory_space=pltpu.VMEM)],
-        out_specs=pl.BlockSpec(memory_space=pltpu.VMEM),
+        out_specs=pl.BlockSpec(memory_space=pl.ANY),
         scratch_shapes=[
             pltpu.VMEM((count, channels, tokens), x.dtype),
             pltpu.SemaphoreType.DMA((count,)),

time: 315 us -> 314 us (level)
  no operation moved by 1% of the time
where the time goes in v9:
time: 314 us; the launch traced here: 310 us
  matrix products  118 us (38%)
  Pallas kernels  92.5 us (29%)
  other arithmetic  33.3 us (11%)
  waiting for transfers between devices  28.7 us (9%)
  starting transfers between devices  19.8 us (6%)
  local copies, waits for them, and re-layouts  16.2 us (5%)
    pallas_call x1, Pallas kernels, to_channels(): pl.pallas_call(functools.partial(channel_kernel, n), out_shape=jax.ShapeD...  63.8 us
    conv_general_dilated x2, matrix products, depthwise(): lax.conv_general_dilated(extended[None], kernel[:, None, :], (1,), 'VALID...  60.8 us
    conv_general_dilated x1, matrix products, per_device(): lax.conv_general_dilated(extended[None], grad_b[:, None, :], (1,), 'VALID...  29.1 us
    pallas_call x1, Pallas kernels, tap_exchange(): pl.pallas_call(functools.partial(tap_exchange_kernel, nz, nx, nc, scale),...  28.7 us
    all_to_all x1, waiting for transfers between devices, per_device(): lax.all_to_all(input_part.astype(jnp.bfloat16), 'ctx', split_axis=1, conc...  26.7 us
    dot_general x6, matrix products, contract(): jnp.einsum(form, left, right, precision=lax.Precision.HIGH, preferred_ele...  26.2 us
    all_to_all x1, starting transfers between devices, per_device(): lax.all_to_all(input_part.astype(jnp.bfloat16), 'ctx', split_axis=1, conc...  9.25 us
    ppermute x2, starting transfers between devices, shifted(): return lax.ppermute(array, axis, pairs)  7.75 us
  transfers between devices with their start and end apart: 4, of which 2 were waited for; matrix products, arithmetic and copies ran while one was open for 25% of the time, Pallas kernels for 9%

profile of v9, /device:TPU:1, one launch (start us, length us, event | category | flops | bytes accessed | tf_op | source)
XLA Modules:
  0.0 309.9 jit_solution(12024422843028178866)
XLA Ops:
  3.8 4.5 %collective-permute-start.1 = (bf16[127,4096]{1,0:T(8,128)(2,1)}, bf16[127,4096]{1,0:T(8,128)(2,1)}, u32[]{:S(2)}, u32[]{:S(2)}) collective-permute-start(bf16[127,4096]{1,0:T(8,128)(2,1)} %slice_bitcast_fusion.1), channel_id=1, source_target_pairs={{0,1},{1,2},{2,3},{3,4},{4,5},{5,6},{6,7},{7,8},{8,9},{9,10},{10,1... | collective-permute-start | bytes 3121160 | tf_op jit(solution)/shard_map/ppermute | solution.py:181
  8.3 2.8 collective-permute-start
  18.3 2.0 collective-permute-done.1
  21.9 30.6 %fusion.16 = f32[1,128,4096]{2,0,1:T(1,128)S(1)} fusion(bf16[1,255,4096]{2,1,0:T(8,128)(2,1)S(1)} %maximum_bitcast_fusion.13, bf16[128,1,4096]{2,0,1:T(8,128)(2,1)S(1)} %fusion.11), kind=kOutput, calls=%fused_computation.30 | convolution fusion | flops 134217728 | bytes 5234688 | tf_op jit(solution)/shard_map/conv_general_dilated | solution.py:245
  52.6 2.1 fusion.31
  56.6 63.8 %shard_map.103 = bf16[2,64,8192]{2,1,0:T(8,128)(2,1)} custom-call(bf16[2,128,4096]{2,1,0:T(8,128)(2,1)} %pad_maximum_fusion.x_ref), custom_call_target="tpu_custom_call" | custom-call | tf_op jit(solution)/shard_map/pallas_call | solution.py:157
  122.8 2.4 convolution_bitcast_fusion
  125.2 2.4 convolution_bitcast_fusion.1
  127.5 6.0 %multiply_subtract_fusion.3 = (f32[64,1,128,128]{2,3,1,0:T(8,128)S(1)}, f32[64,1,128,128]{2,3,1,0:T(8,128)}, f32[64,1,128,128]{2,3,1,0:T(8,128)}, f32[64,1,128,128]{2,3,1,0:T(8,128)}) fusion(f32[64,2,128,128]{2,3,1,0:T(8,128)S(1)} %convolution_bitcast_fusion, f32[128,128]{0,1:T(8,128)S(1)} %get-tuple-element.29, f32[128,128]{0,1:T(8,128)S(1)} %get-tuple-element.30, ...), kind=kLoop, calls=%fused_computation.25 | loop fusion | flops 12582912 | bytes 33685504 | tf_op jit(solution)/shard_map/sub | solution.py:214
  133.6 7.1 %fusion.22 = f32[64,2,128,128]{2,3,0,1:T(8,128)S(1)} fusion(f32[64,1,128,128]{2,3,1,0:T(8,128)} %get-tuple-element.8, f32[64,1,128,128]{2,3,1,0:T(8,128)S(1)} %get-tuple-element.7, f32[1,2,128,128]{2,3,0,1:T(8,128)S(1)} %get-tuple-element.16, f32[1,2,128,128]{2,3,0,1:T(8,128)S(1)} %get-tuple-element.21), kind=kOutput, calls=%fused_computation.35 | convolution fusion | flops 3223388160 | bytes 17039360 | tf_op jit(solution)/shard_map/nqcb,qpbd->npcd/dot_general | solution.py:192
  140.7 4.9 %fusion.21 = f32[64,2,128,128]{2,3,0,1:T(8,128)S(1)} fusion(f32[64,1,128,128]{2,3,1,0:T(8,128)S(1)} %copy-done.3, f32[64,1,128,128]{2,3,1,0:T(8,128)S(1)} %copy-done.4, f32[1,2,128,128]{2,3,0,1:T(8,128)S(1)} %get-tuple-element.16, f32[1,2,128,128]{2,3,0,1:T(8,128)S(1)} %get-tuple-element.21), kind=kOutput, calls=%fused_computation.34 | convolution fusion | flops 3223388160 | bytes 17039360 | tf_op jit(solution)/shard_map/nqcb,qpbd->npcd/dot_general | solution.py:192
  145.6 2.8 multiply_add_fusion.1
  148.4 5.0 %fusion.18 = f32[64,2,128,128]{2,3,1,0:T(8,128)S(1)} fusion(f32[64,1,128,128]{2,3,0,1:T(8,128)S(1)} %get-tuple-element.4, f32[64,1,128,128]{2,3,0,1:T(8,128)S(1)} %get-tuple-element.3, f32[1,2,128,128]{2,3,1,0:T(8,128)S(1)} %copy-done.23, f32[1,2,128,128]{2,3,1,0:T(8,128)S(1)} %copy-done.22), kind=kOutput, calls=%fused_computation.32 | convolution fusion | flops 3223388160 | bytes 17039360 | tf_op jit(solution)/shard_map/npcd,pqdb->nqcb/dot_general | solution.py:192
  155.4 4.4 %fusion.38 = bf16[64,2,64,128]{3,2,1,0:T(8,128)(2,1)S(1)} fusion(f32[64,1,128,128]{2,3,1,0:T(8,128)S(1)} %get-tuple-element.6, f32[64,1,128,128]{2,3,1,0:T(8,128)S(1)} %get-tuple-element.5, f32[1,2,64,128]{3,2,1,0:T(8,128)S(1)} %copy-done.21, f32[1,2,64,128]{3,2,1,0:T(8,128)S(1)} %copy-done.20), kind=kOutput, calls=%fused_computation.66 | convolution fusion | flops 1613791232 | bytes 10616832 | tf_op jit(solution)/shard_map/rqac,nqcb->nrab/dot_general | solution.py:192
  161.6 9.2 %all-to-all-start = ((bf16[64,64,128]{2,0,1:T(8,128)(2,1)}), bf16[64,64,128]{2,0,1:T(8,128)(2,1)S(1)}, u32[]{:S(2)}, u32[]{:S(2)}) async-start(bf16[64,64,128]{2,0,1:T(8,128)(2,1)} %copy.65), calls=%async_computation | async-start | bytes 2097152 | tf_op jit(solution)/shard_map/all_to_all | solution.py:297
  172.2 26.7 %all-to-all-done = bf16[64,64,128]{2,0,1:T(8,128)(2,1)S(1)} async-done(((bf16[64,64,128]{2,0,1:T(8,128)(2,1)}), bf16[64,64,128]{2,0,1:T(8,128)(2,1)S(1)}, u32[]{:S(2)}, u32[]{:S(2)}) %all-to-all-start) | async-done | bytes 1048608 | tf_op jit(solution)/shard_map/all_to_all | solution.py:297
  200.5 1.9 copy.66
  202.4 4.2 %fusion.30 = bf16[128,4096]{1,0:T(8,128)(2,1)} fusion(bf16[1,128,4096]{2,1,0:T(8,128)(2,1)} %param.11, bf16[1,128,4096]{2,1,0:T(8,128)(2,1)} %param.12, f32[4096,128]{0,1:T(8,128)S(1)} %copy.66, bf16[128,4096]{1,0:T(8,128)(2,1)} %copy-done.5), kind=kLoop, calls=%fused_computation.53 | loop fusion | flops 4194304 | bytes 6291456 | tf_op jit(solution)/shard_map/convert_element_type | solution.py:301
  206.6 3.3 %collective-permute-start.2 = (bf16[127,4096]{1,0:T(8,128)(2,1)}, bf16[127,4096]{1,0:T(8,128)(2,1)}, u32[]{:S(2)}, u32[]{:S(2)}) collective-permute-start(bf16[127,4096]{1,0:T(8,128)(2,1)} %bitcast.184), channel_id=1, source_target_pairs={{1,0},{2,1},{3,2},{4,3},{5,4},{6,5},{7,6},{8,7},{9,8},{10,9},{11,1... | collective-permute-start | bytes 3121160 | tf_op jit(solution)/shard_map/ppermute | solution.py:181
  209.9 29.1 %fusion.14 = f32[1,4096,128]{1,0,2:T(1,128)} fusion(bf16[1,255,4096]{2,1,0:T(8,128)(2,1)S(1)} %copy-done.14, bf16[128,1,4096]{2,0,1:T(8,128)(2,1)} %bitcast.64), kind=kOutput, calls=%fused_computation.28 | convolution fusion | flops 134217728 | bytes 5234688 | tf_op jit(solution)/shard_map/conv_general_dilated | solution.py:305
  239.0 5.7 %copy.72 = f32[1,4096,128]{2,1,0:T(8,128)} copy(f32[1,4096,128]{1,0,2:T(1,128)} %fusion.14) | data formatting | bytes 4194304 | tf_op jit(solution)/shard_map/conv_general_dilated | solution.py:305
  244.7 28.7 %shard_map.104 = bf16[64,128]{1,0:T(8,128)(2,1)} custom-call(f32[8,4,2,64,128]{4,3,2,1,0:T(8,128)} %bitcast.188), custom_call_target="tpu_custom_call" | custom-call | tf_op jit(solution)/shard_map/pallas_call | solution.py:81
  276.7 30.1 %fusion.12 = f32[1,128,4096]{2,0,1:T(1,128)S(1)} fusion(bf16[1,255,4096]{2,1,0:T(8,128)(2,1)S(1)} %maximum_bitcast_fusion.16, bf16[128,1,4096]{2,0,1:T(8,128)(2,1)S(1)} %bitcast.185), kind=kOutput, calls=%fused_computation.26 | convolution fusion | flops 134217728 | bytes 5234688 | tf_op jit(solution)/shard_map/conv_general_dilated | solution.py:245
  306.9 2.8 fusion.40
  (80 shorter events, 25.9 us)
Async XLA Ops:
  0.6 17.2 %copy-start = (bf16[1,128,4096]{2,1,0:T(8,128)(2,1)S(1)}, bf16[1,128,4096]{2,1,0:T(8,128)(2,1)}, u32[]{:S(2)}) copy-start(bf16[1,128,4096]{2,1,0:T(8,128)(2,1)} %param.15) | copy-start | bytes 3145732
  3.8 16.5 %collective-permute-start.1 = (bf16[127,4096]{1,0:T(8,128)(2,1)}, bf16[127,4096]{1,0:T(8,128)(2,1)}, u32[]{:S(2)}, u32[]{:S(2)}) collective-permute-start(bf16[127,4096]{1,0:T(8,128)(2,1)} %slice_bitcast_fusion.1), channel_id=1, source_target_pairs={{0,1},{1,2},{2,3},{3,4},{4,5},{5,6},{6,7},{7,8},{8,9},{9,10},{10,1... | collective-permute-start | bytes 3121160 | tf_op jit(solution)/shard_map/ppermute | solution.py:181
  8.3 46.4 %collective-permute-start = (bf16[128,4096]{1,0:T(8,128)(2,1)}, bf16[128,4096]{1,0:T(8,128)(2,1)S(1)}, u32[]{:S(2)}, u32[]{:S(2)}) collective-permute-start(bf16[128,4096]{1,0:T(8,128)(2,1)} %bitcast), channel_id=1, source_target_pairs={{0,192},{64,0},{128,64},{192,128},{1,193},{65,1},{129,65},{193,129... | collective-permute-start | bytes 3145736 | tf_op jit(solution)/shard_map/ppermute | solution.py:175
  12.0 5.8 %copy-start.18 = (bf16[128,128]{1,0:T(8,128)(2,1)S(1)}, bf16[128,128]{1,0:T(8,128)(2,1)}, u32[]{:S(2)}) copy-start(bf16[128,128]{1,0:T(8,128)(2,1)} %rev.4) | copy-start | bytes 98308
  21.8 30.7 %copy-start.13 = (bf16[1,255,4096]{2,1,0:T(8,128)(2,1)}, bf16[1,255,4096]{2,1,0:T(8,128)(2,1)S(1)}, u32[]{:S(2)}) copy-start(bf16[1,255,4096]{2,1,0:T(8,128)(2,1)S(1)} %maximum_bitcast_fusion.13) | copy-start | bytes 6266884
  21.9 30.7 %copy-start.7 = (bf16[1,128,4096]{2,1,0:T(8,128)(2,1)S(1)}, bf16[1,128,4096]{2,1,0:T(8,128)(2,1)}, u32[]{:S(2)}) copy-start(bf16[1,128,4096]{2,1,0:T(8,128)(2,1)} %param.12) | copy-start | bytes 3145732
  21.9 30.7 %copy-start.9 = (bf16[1,128,4096]{2,1,0:T(8,128)(2,1)S(1)}, bf16[1,128,4096]{2,1,0:T(8,128)(2,1)}, u32[]{:S(2)}) copy-start(bf16[1,128,4096]{2,1,0:T(8,128)(2,1)} %param.9) | copy-start | bytes 3145732
  21.9 30.7 %copy-start.10 = (bf16[1,128,4096]{2,1,0:T(8,128)(2,1)S(1)}, bf16[1,128,4096]{2,1,0:T(8,128)(2,1)}, u32[]{:S(2)}) copy-start(bf16[1,128,4096]{2,1,0:T(8,128)(2,1)} %param.11) | copy-start | bytes 3145732
  54.7 65.7 %copy-start.5 = (bf16[128,4096]{1,0:T(8,128)(2,1)}, bf16[128,4096]{1,0:T(8,128)(2,1)S(1)}, u32[]{:S(2)}) copy-start(bf16[128,4096]{1,0:T(8,128)(2,1)S(1)} %collective-permute-done) | copy-start | bytes 3145732
  120.4 2.3 copy-start.16
  122.7 2.4 copy-start.12
  133.6 7.1 %copy-start.3 = (f32[64,1,128,128]{2,3,1,0:T(8,128)S(1)}, f32[64,1,128,128]{2,3,1,0:T(8,128)}, u32[]{:S(2)}) copy-start(f32[64,1,128,128]{2,3,1,0:T(8,128)} %get-tuple-element.19) | copy-start | bytes 12582916
  133.6 7.1 %copy-start.4 = (f32[64,1,128,128]{2,3,1,0:T(8,128)S(1)}, f32[64,1,128,128]{2,3,1,0:T(8,128)}, u32[]{:S(2)}) copy-start(f32[64,1,128,128]{2,3,1,0:T(8,128)} %get-tuple-element.20) | copy-start | bytes 12582916
  145.6 2.8 copy-start.22
  145.6 2.8 copy-start.23
  161.6 37.2 %all-to-all-start = ((bf16[64,64,128]{2,0,1:T(8,128)(2,1)}), bf16[64,64,128]{2,0,1:T(8,128)(2,1)S(1)}, u32[]{:S(2)}, u32[]{:S(2)}) async-start(bf16[64,64,128]{2,0,1:T(8,128)(2,1)} %copy.65), calls=%async_computation | async-start | bytes 2097152 | tf_op jit(solution)/shard_map/all_to_all | solution.py:297
  202.4 36.6 %copy-start.1 = (f32[4096,128]{0,1:T(8,128)}, f32[4096,128]{0,1:T(8,128)S(1)}, u32[]{:S(2)}) copy-start(f32[4096,128]{0,1:T(8,128)S(1)} %copy.66) | copy-start | bytes 6291460
  202.4 7.5 %copy-start.14 = (bf16[1,255,4096]{2,1,0:T(8,128)(2,1)S(1)}, bf16[1,255,4096]{2,1,0:T(8,128)(2,1)}, u32[]{:S(2)}) copy-start(bf16[1,255,4096]{2,1,0:T(8,128)(2,1)} %copy-done.13) | copy-start | bytes 6266884
  206.6 68.3 %collective-permute-start.2 = (bf16[127,4096]{1,0:T(8,128)(2,1)}, bf16[127,4096]{1,0:T(8,128)(2,1)}, u32[]{:S(2)}, u32[]{:S(2)}) collective-permute-start(bf16[127,4096]{1,0:T(8,128)(2,1)} %bitcast.184), channel_id=1, source_target_pairs={{1,0},{2,1},{3,2},{4,3},{5,4},{6,5},{7,6},{8,7},{9,8},{10,9},{11,1... | collective-permute-start | bytes 3121160 | tf_op jit(solution)/shard_map/ppermute | solution.py:181
  239.0 34.4 %copy-start.19 = (bf16[128,128]{1,0:T(8,128)(2,1)S(1)}, bf16[128,128]{1,0:T(8,128)(2,1)}, u32[]{:S(2)}) copy-start(bf16[128,128]{1,0:T(8,128)(2,1)} %rev.4) | copy-start | bytes 98308
  276.7 30.2 %copy-start.2 = (f32[4096,128]{0,1:T(8,128)S(1)}, f32[4096,128]{0,1:T(8,128)}, u32[]{:S(2)}) copy-start(f32[4096,128]{0,1:T(8,128)} %copy-done.1) | copy-start | bytes 6291460
  276.7 30.2 %copy-start.6 = (bf16[128,4096]{1,0:T(8,128)(2,1)S(1)}, bf16[128,4096]{1,0:T(8,128)(2,1)}, u32[]{:S(2)}) copy-start(bf16[128,4096]{1,0:T(8,128)(2,1)} %copy-done.5) | copy-start | bytes 3145732
  276.7 30.2 %copy-start.8 = (bf16[1,128,4096]{2,1,0:T(8,128)(2,1)S(1)}, bf16[1,128,4096]{2,1,0:T(8,128)(2,1)}, u32[]{:S(2)}) copy-start(bf16[1,128,4096]{2,1,0:T(8,128)(2,1)} %param.12) | copy-start | bytes 3145732
  276.7 30.2 %copy-start.11 = (bf16[1,128,4096]{2,1,0:T(8,128)(2,1)S(1)}, bf16[1,128,4096]{2,1,0:T(8,128)(2,1)}, u32[]{:S(2)}) copy-start(bf16[1,128,4096]{2,1,0:T(8,128)(2,1)} %param.10) | copy-start | bytes 3145732
  (4 other events, 8.3 us)
